TPU v7x, 128 devices: a whole 4x4x4 slice. The times are simulated.
128 devices in a mesh: comp: 8 (over z, core), sub: 16 (over y, x).
Axes of the slice: x: 4, y: 4, z: 4, core: 2. Of those that a mesh axis runs over, the one named last changes fastest.
Arguments:
- atmos_profiles: bfloat16 [4, 72, 1048576], P(None, None, ('comp', 'sub')), may hold values from -6 to 6
- atmos_mixing: bfloat16 [72, 72], replicated
- drag_factor: float32 [1048576], P(('comp', 'sub')), may hold values from 0.5 to 1.5
- surface_before: float32 [4, 1048576], P(None, ('comp', 'sub')), may hold values from -6 to 6
- downward_fluxes: float32 [4, 1048576], P(None, ('comp', 'sub')), may hold values from -6 to 6
- land_weight: float32 [1048576], P(('comp', 'sub')), may hold values from 0.05 to 1
- land_surface: float32 [4, 1048576], P(None, ('comp', 'sub')), may hold values from -6 to 6
- ocean_state: float32 [4, 60, 1048576], P(None, None, ('comp', 'sub')), may hold values from -6 to 6
- ocean_mixing: float32 [60, 60], replicated
- sea_mask: int32 [1048576], P(('comp', 'sub')), may hold values 0 or 1
- exchange_slot: int32 [4, 1048576], P(None, ('comp', 'sub')), may hold values from 0 to 65535, as said below
- parent_column: int32 [4, 1048576], P(None, ('comp', 'sub')), may hold values from 0 to 8191, as said below
- ocean_weight: float32 [4, 1048576], P(None, ('comp', 'sub')), may hold values from 0.1 to 1
- atmos_weight: float32 [4, 1048576], P(None, ('comp', 'sub')), may hold values from 0.05 to 0.5
Outputs:
- atmos_updated: bfloat16 [4, 72, 1048576], P(None, None, ('comp', 'sub'))
- ocean_updated: float32 [4, 60, 1048576], P(None, None, ('comp', 'sub'))
- surface_state: float32 [4, 1048576], P(None, ('comp', 'sub'))
Inputs may be any that keep to these rules, and one draw needn't show every extreme that they name: Within the 8192 cells of one device block along the second dimension, all 32768 values are distinct, at most 512 of them share one value of exchange_slot // 512, and in every block some value of exchange_slot // 512 is shared by exactly 512 of them. In every aligned group of 128 cells along the second dimension (one k), the values are t * 128 + 0, 1, ..., 127 in order, for one t. In every aligned group of 128 cells along the second dimension (one k), all values share one value of parent_column // 128.
All inputs are finite; a program needn't handle non-finite values. No bound on the sum of `sea_mask` on one device may be relied on, other than what follows from the above.
Results may differ from a plain program's by a relative error of at most 0.001.
Values sent between devices are 32-bit elements; how exact they have to be, the bound alone decides.
A program may use at most 128 MiB of HBM per device.

v0:
```python
import jax
import jax.numpy as jnp
from jax import lax
from jax.sharding import PartitionSpec as P

couple_rate = 0.5
highest = lax.Precision.HIGHEST


def surface_fluxes(atmos_profiles, drag_factor, surface_before, downward_fluxes):
    bottom = atmos_profiles[:, -1, :].astype(jnp.float32)
    east_gap = bottom[2] - surface_before[2]
    north_gap = bottom[3] - surface_before[3]
    wind_speed = jnp.sqrt(1.0 + east_gap * east_gap + north_gap * north_gap)
    transfer = drag_factor * wind_speed
    sensible = transfer * (surface_before[0] - bottom[0])
    latent = transfer * (surface_before[1] - bottom[1])
    return jnp.stack(
        [
            sensible,
            latent,
            transfer * east_gap,
            transfer * north_gap,
            downward_fluxes[0],
            downward_fluxes[1],
            downward_fluxes[2],
            downward_fluxes[3],
        ]
    )


def diffuse_atmos(atmos_profiles, atmos_mixing, fluxes):
    lowest = atmos_mixing[:, -1].astype(jnp.float32)
    tendency = couple_rate * jnp.stack([fluxes[0], fluxes[1], -fluxes[2], -fluxes[3]])
    result = []
    for member in range(4):
        mixed_rows = jnp.dot(
            atmos_mixing, atmos_profiles[member], preferred_element_type=jnp.float32
        )
        result.append(mixed_rows + lowest[:, None] * tendency[member][None, :])
    return jnp.stack(result).astype(jnp.bfloat16)


def forcing_rows(fluxes):
    return couple_rate * jnp.stack(
        [
            fluxes[4] + fluxes[5] - fluxes[0] - fluxes[1],
            fluxes[1] - fluxes[6] - fluxes[7],
            fluxes[2],
            fluxes[3],
        ]
    )


def per_device(
    atmos_profiles,
    atmos_mixing,
    drag_factor,
    surface_before,
    downward_fluxes,
    land_weight,
    land_surface,
    ocean_state,
    ocean_mixing,
    sea_mask,
    exchange_slot,
    parent_column,
    ocean_weight,
    atmos_weight,
):
    comp_count = lax.axis_size("comp")
    sub_count = lax.axis_size("sub")
    devices = comp_count * sub_count
    columns = atmos_profiles.shape[2]
    intersections = exchange_slot.shape[0]
    ocean_cells = exchange_slot.shape[1]
    capacity = 2 * intersections * ocean_cells // devices
    width = min(128, capacity)
    tile_count = intersections * ocean_cells // width
    slot_tiles = devices * capacity // width
    windows = columns // width
    tile_place = exchange_slot.reshape(tile_count, width)[:, 0] // width
    placement = (tile_place[None, :] == jnp.arange(slot_tiles, dtype=jnp.int32)[:, None]).astype(
        jnp.float32
    )

    def to_slots(values):
        return jnp.einsum("qt,ftl->fql", placement, values, precision=highest)

    wanted = parent_column.reshape(1, tile_count, width).astype(jnp.float32)
    request = (to_slots(wanted)[0] + 0.5).astype(jnp.int32).reshape(devices, capacity)
    asked_ids = lax.all_to_all(request, ("comp", "sub"), split_axis=0, concat_axis=0, tiled=True)
    asked_tiles = asked_ids.reshape(slot_tiles, width)
    window_hot = (
        (asked_tiles[:, 0] // width)[:, None] == jnp.arange(windows, dtype=jnp.int32)[None, :]
    ).astype(jnp.float32)
    lane_hot = (
        (asked_tiles % width)[:, :, None] == jnp.arange(width, dtype=jnp.int32)[None, None, :]
    ).astype(jnp.float32)
    fluxes = surface_fluxes(atmos_profiles, drag_factor, surface_before, downward_fluxes)
    column_forcing = forcing_rows(fluxes)
    window_rows = jnp.einsum(
        "qw,fwl->fql", window_hot, column_forcing.reshape(4, windows, width), precision=highest
    )
    served = jnp.einsum("fql,qml->fqm", window_rows, lane_hot, precision=highest)
    base_mix = jnp.stack(
        [jnp.dot(ocean_mixing, ocean_state[member], precision=highest) for member in range(4)]
    )
    arrived = lax.all_to_all(
        served.reshape(4, devices, capacity),
        ("comp", "sub"),
        split_axis=1,
        concat_axis=1,
        tiled=True,
    )
    atmos_updated = diffuse_atmos(atmos_profiles, atmos_mixing, fluxes)
    at_cells = jnp.einsum(
        "qt,fql->ftl", placement, arrived.reshape(4, slot_tiles, width), precision=highest
    ).reshape(4, intersections, ocean_cells)
    forcing = jnp.sum(ocean_weight[None] * at_cells, axis=1) / jnp.sum(ocean_weight, axis=0)[None]
    mixed_state = base_mix + ocean_mixing[:, 0][None, :, None] * forcing[:, None, :]
    ocean_updated = jnp.where(sea_mask[None, None, :] == 1, mixed_state, ocean_state)
    sea_share = atmos_weight * sea_mask.astype(jnp.float32)[None, :]
    outgoing = jnp.concatenate(
        [sea_share[None] * ocean_updated[:, 0, :][:, None, :], sea_share[None]], axis=0
    )
    send_buffer = to_slots(outgoing.reshape(5, tile_count, width))
    returned = lax.all_to_all(
        send_buffer.reshape(5, devices, capacity),
        ("comp", "sub"),
        split_axis=1,
        concat_axis=1,
        tiled=True,
    )
    lanes_back = jnp.einsum(
        "fqm,qml->fql", returned.reshape(5, slot_tiles, width), lane_hot, precision=highest
    )
    summed = jnp.einsum("qw,fql->fwl", window_hot, lanes_back, precision=highest).reshape(
        5, columns
    )
    surface_state = (summed[:4] + land_weight[None] * land_surface) / (summed[4] + land_weight)[
        None
    ]
    return (atmos_updated, ocean_updated, surface_state)


def solution(mesh):
    return jax.shard_map(
        per_device,
        mesh=mesh,
        in_specs=(
            P(None, None, ("comp", "sub")),
            P(),
            P(("comp", "sub")),
            P(None, ("comp", "sub")),
            P(None, ("comp", "sub")),
            P(("comp", "sub")),
            P(None, ("comp", "sub")),
            P(None, None, ("comp", "sub")),
            P(),
            P(("comp", "sub")),
            P(None, ("comp", "sub")),
            P(None, ("comp", "sub")),
            P(None, ("comp", "sub")),
            P(None, ("comp", "sub")),
        ),
        out_specs=(
            P(None, None, ("comp", "sub")),
            P(None, None, ("comp", "sub")),
            P(None, ("comp", "sub")),
        ),
        check_vma=False,
    )
```

profile of v0, /device:TPU:1, one launch (start us, length us, event | category | flops | bytes accessed | tf_op | source)
XLA Modules:
  0.0 178.1 jit_solution(6388314276726355119)
XLA Ops:
  3.9 11.5 %all-to-all-start = ((s32[128,1,512]{2,1,0:T(1,128)}), s32[128,1,512]{2,1,0:T(1,128)S(1)}, u32[]{:S(2)}, u32[]{:S(2)}) async-start(s32[128,1,512]{2,1,0:T(1,128)} %bitcast.36), calls=%async_computation | async-start | bytes 524288 | tf_op jit(solution)/shard_map/all_to_all | solution.py:92
  15.4 7.8 %copy.68 = f32[4,60,8192]{2,1,0:T(8,128)S(1)} copy(f32[4,60,8192]{2,0,1:T(4,128)} %param.21) | data formatting | bytes 15728640 | tf_op args[7]
  23.2 1.9 %convolution_bitcast_fusion = f32[1,60,8192]{2,1,0:T(8,128)S(1)} fusion(f32[60,60]{1,0:T(8,128)S(1)} %copy-done.4, f32[4,60,8192]{2,1,0:T(8,128)S(1)} %copy.68), kind=kOutput, calls=%fused_computation.9 | convolution fusion | flops 353894400 | bytes 4096000 | tf_op jit(solution)/shard_map/dot_general | solution.py:107
  25.2 3.2 %convolution_bitcast_fusion.1 = f32[1,60,8192]{2,1,0:T(8,128)} fusion(f32[60,60]{1,0:T(8,128)S(1)} %copy-done.4, f32[4,60,8192]{2,1,0:T(8,128)S(1)} %copy.68), kind=kOutput, calls=%fused_computation.10 | convolution fusion | flops 353894400 | bytes 4096000 | tf_op jit(solution)/shard_map/dot_general | solution.py:107
  32.6 1.3 copy.74
  33.9 30.5 %fusion.1 = f32[512,128,4]{1,2,0:T(4,128)} fusion(f32[4,512,128]{2,0,1:T(4,128)} %copy.74, s32[512,128]{1,0:T(8,128)} %add_select_fusion.1), kind=kOutput, calls=%fused_computation.2 | convolution fusion | flops 411041792 | bytes 2359296 | tf_op jit(solution)/shard_map/fql,qml->fqm/dot_general | solution.py:105
  64.4 10.2 %all-to-all-start.1 = ((f32[4,128,512]{2,0,1:T(4,128)}), f32[4,128,512]{2,0,1:T(4,128)}, u32[]{:S(2)}, u32[]{:S(2)}) async-start(f32[4,128,512]{2,0,1:T(4,128)} %bitcast.48), calls=%async_computation.1 | async-start | bytes 2097152 | tf_op jit(solution)/shard_map/all_to_all | solution.py:109
  75.9 4.9 %convolution_bitcast_fusion.2 = f32[1,60,8192]{2,1,0:T(8,128)} fusion(f32[60,60]{1,0:T(8,128)S(1)} %copy-done.4, f32[4,60,8192]{2,1,0:T(8,128)} %copy-done.1), kind=kOutput, calls=%fused_computation.11 | convolution fusion | flops 353894400 | bytes 4077632 | tf_op jit(solution)/shard_map/dot_general | solution.py:107
  80.9 4.9 %convolution_bitcast_fusion.3 = f32[1,60,8192]{2,1,0:T(8,128)} fusion(f32[60,60]{1,0:T(8,128)S(1)} %copy-done.4, f32[4,60,8192]{2,1,0:T(8,128)} %copy-done.1), kind=kOutput, calls=%fused_computation.12 | convolution fusion | flops 353894400 | bytes 4077632 | tf_op jit(solution)/shard_map/dot_general | solution.py:107
  85.8 1.6 fusion.10
  87.4 1.5 fusion.11
  88.9 4.2 %all-to-all-done.1 = f32[4,128,512]{2,0,1:T(4,128)} async-done(((f32[4,128,512]{2,0,1:T(4,128)}), f32[4,128,512]{2,0,1:T(4,128)}, u32[]{:S(2)}, u32[]{:S(2)}) %all-to-all-start.1) | async-done | bytes 1048608 | tf_op jit(solution)/shard_map/all_to_all | solution.py:109
  93.1 1.6 copy.77
  95.7 2.2 %convolution_bitcast_fusion.6 = f32[4,256,128]{1,2,0:T(8,128)S(1)} fusion(f32[4,512,128]{2,1,0:T(8,128)} %reshape.164, s32[256]{0:T(256)S(1)} %and_select_fusion), kind=kOutput, calls=%fused_computation.33 | convolution fusion | flops 805437440 | bytes 1573888 | tf_op jit(solution)/shard_map/qt,fql->ftl/dot_general | solution.py:117
  99.7 9.6 %fusion.12 = f32[4,60,8192]{2,1,0:T(8,128)S(1)} fusion(f32[1,60,8192]{2,1,0:T(8,128)S(1)} %convolution_bitcast_fusion, f32[1,60,8192]{2,1,0:T(8,128)} %convolution_bitcast_fusion.1, f32[1,60,8192]{2,1,0:T(8,128)} %convolution_bitcast_fusion.2, f32[1,60,8192]{2,1,0:T(8,128)} %convolution_bitcast_fusion.3, f32[4,8192]{1,0:T(4,128)S(1)} %broadcast_divide_fusion, ...), kind=kLoop, calls=%fused_computation.22 | loop fusion | flops 11796480 | bytes 23732464 | tf_op jit(solution)/shard_map/jit(_where)/select_n | solution.py:122
  109.3 3.2 %copy-done = f32[4,60,8192]{2,1,0:T(8,128)} copy-done((f32[4,60,8192]{2,1,0:T(8,128)}, f32[4,60,8192]{2,1,0:T(8,128)S(1)}, u32[]{:S(2)}) %copy-start) | copy-done | bytes 7864344
  114.8 2.2 %copy.85 = f32[5,128,512]{2,0,1:T(8,128)} copy(f32[5,128,512]{2,1,0:T(8,128)S(1)} %reshape.166) | data formatting | bytes 2621440 | tf_op jit(solution)/shard_map/reshape | solution.py:129
  116.9 6.0 %all-to-all-start.2 = ((f32[5,128,512]{2,0,1:T(8,128)}), f32[5,128,512]{2,0,1:T(8,128)}, u32[]{:S(2)}, u32[]{:S(2)}) async-start(f32[5,128,512]{2,0,1:T(8,128)} %copy.85), calls=%async_computation.2 | async-start | bytes 4194304 | tf_op jit(solution)/shard_map/all_to_all | solution.py:128
  122.9 1.9 %fusion.8 = bf16[1,72,8192]{2,1,0:T(8,128)(2,1)S(1)} fusion(bf16[72,72]{1,0:T(8,128)(2,1)S(1)} %copy-done.6, f32[8192]{0:T(1024)S(1)} %bitcast.151, bf16[4,72,8192]{2,1,0:T(8,128)(2,1)} %param.14, f32[72]{0:T(128)S(1)} %convert_reduce_fusion), kind=kOutput, calls=%fused_computation.17 | convolution fusion | flops 86704128 | bytes 2402720 | tf_op jit(solution)/shard_map/dot_general | solution.py:37
  124.8 1.7 fusion.9
  126.6 2.5 %pad_maximum_fusion = bf16[4,72,8192]{2,1,0:T(8,128)(2,1)} fusion(bf16[1,72,8192]{2,1,0:T(8,128)(2,1)S(1)} %fusion.8, bf16[1,72,8192]{2,1,0:T(8,128)(2,1)S(1)} %fusion.9, bf16[1,72,8192]{2,1,0:T(8,128)(2,1)S(1)} %copy-done.2, bf16[1,72,8192]{2,1,0:T(8,128)(2,1)S(1)} %copy-done.3), kind=kLoop, calls=%fused_computation.23 | loop fusion | flops 7077888 | bytes 9437184 | tf_op jit(solution)/shard_map/stack | solution.py:41
  129.1 11.7 %copy.89 = f32[4,60,8192]{2,0,1:T(4,128)} copy(f32[4,60,8192]{2,1,0:T(8,128)} %copy-done) | data formatting | bytes 15728640
  140.8 11.5 %all-to-all-done.2 = f32[5,128,512]{2,0,1:T(8,128)} async-done(((f32[5,128,512]{2,0,1:T(8,128)}), f32[5,128,512]{2,0,1:T(8,128)}, u32[]{:S(2)}, u32[]{:S(2)}) %all-to-all-start.2) | async-done | bytes 1310752 | tf_op jit(solution)/shard_map/all_to_all | solution.py:128
  152.3 24.3 %fusion.13 = f32[5,512,128]{2,0,1:T(8,128)S(1)} fusion(f32[5,512,128]{2,0,1:T(8,128)} %bitcast.52, s32[512,128]{1,0:T(8,128)S(1)} %copy-done.7), kind=kOutput, calls=%fused_computation.28 | convolution fusion | flops 511705088 | bytes 2883584 | tf_op jit(solution)/shard_map/fqm,qml->fql/dot_general | solution.py:135
  (88 shorter events, 15.0 us)
Async XLA Ops:
  3.9 27.1 %all-to-all-start = ((s32[128,1,512]{2,1,0:T(1,128)}), s32[128,1,512]{2,1,0:T(1,128)S(1)}, u32[]{:S(2)}, u32[]{:S(2)}) async-start(s32[128,1,512]{2,1,0:T(1,128)} %bitcast.36), calls=%async_computation | async-start | bytes 524288 | tf_op jit(solution)/shard_map/all_to_all | solution.py:92
  15.4 7.8 %copy-start.4 = (f32[60,60]{1,0:T(8,128)S(1)}, f32[60,60]{1,0:T(8,128)}, u32[]{:S(2)}) copy-start(f32[60,60]{1,0:T(8,128)} %param.22) | copy-start | bytes 43204
  23.2 5.2 %copy-start.1 = (f32[4,60,8192]{2,1,0:T(8,128)}, f32[4,60,8192]{2,1,0:T(8,128)S(1)}, u32[]{:S(2)}) copy-start(f32[4,60,8192]{2,1,0:T(8,128)S(1)} %copy.68) | copy-start | bytes 23592964
  25.1 4.5 %copy-start.14 = (f32[4,8192]{1,0:T(4,128)S(1)}, f32[4,8192]{1,0:T(4,128)}, u32[]{:S(2)}) copy-start(f32[4,8192]{1,0:T(4,128)} %param.18) | copy-start | bytes 393220
  25.1 4.5 %copy-start.11 = (f32[4,8192]{1,0:T(4,128)S(1)}, f32[4,8192]{1,0:T(4,128)}, u32[]{:S(2)}) copy-start(f32[4,8192]{1,0:T(4,128)} %param.17) | copy-start | bytes 393220
  25.1 4.7 %copy-start.18 = (f32[8192]{0:T(1024)S(1)}, f32[8192]{0:T(1024)}, u32[]{:S(2)}) copy-start(f32[8192]{0:T(1024)} %param.16) | copy-start | bytes 98308
  25.1 4.8 %copy-start.15 = (s32[8192]{0:T(1024)S(1)}, s32[8192]{0:T(1024)}, u32[]{:S(2)}) copy-start(s32[8192]{0:T(1024)} %param.23) | copy-start | bytes 98308
  25.2 5.6 %copy-start.17 = (f32[4,8192]{1,0:T(4,128)S(1)}, f32[4,8192]{1,0:T(4,128)}, u32[]{:S(2)}) copy-start(f32[4,8192]{1,0:T(4,128)} %param.27) | copy-start | bytes 393220
  33.9 40.7 %copy-start.6 = (bf16[72,72]{1,0:T(8,128)(2,1)S(1)}, bf16[72,72]{1,0:T(8,128)(2,1)}, u32[]{:S(2)}) copy-start(bf16[72,72]{1,0:T(8,128)(2,1)} %param.15) | copy-start | bytes 31108
  64.4 10.8 %copy-start.5 = (f32[4,8192]{1,0:T(4,128)S(1)}, f32[4,8192]{1,0:T(4,128)}, u32[]{:S(2)}) copy-start(f32[4,8192]{1,0:T(4,128)} %param.26) | copy-start | bytes 393220
  64.4 28.7 %all-to-all-start.1 = ((f32[4,128,512]{2,0,1:T(4,128)}), f32[4,128,512]{2,0,1:T(4,128)}, u32[]{:S(2)}, u32[]{:S(2)}) async-start(f32[4,128,512]{2,0,1:T(4,128)} %bitcast.48), calls=%async_computation.1 | async-start | bytes 2097152 | tf_op jit(solution)/shard_map/all_to_all | solution.py:109
  75.0 10.7 %slice-start = ((s8[4718592]{0:T(1024)(128)(4,1)}), s8[524288]{0:T(1024)(128)(4,1)S(1)}, s32[]{:S(2)}) async-start(s8[4718592]{0:T(1024)(128)(4,1)} %bitcast.139), calls=%async_computation.3 | async-start | bytes 1048576
  75.9 9.8 %slice-start.1 = ((s8[4718592]{0:T(1024)(128)(4,1)}), s8[4194304]{0:T(1024)(128)(4,1)S(1)}, s32[]{:S(2)}) async-start(s8[4718592]{0:T(1024)(128)(4,1)} %bitcast.139), calls=%async_computation.4 | async-start | bytes 8388608
  80.9 4.9 %copy-start.9 = (f32[1,8192]{1,0:T(1,128)S(1)}, f32[1,8192]{1,0:T(1,128)}, u32[]{:S(2)}) copy-start(f32[1,8192]{1,0:T(1,128)} %get-tuple-element.32) | copy-start | bytes 98308
  80.9 6.5 %copy-start.8 = (f32[1,8192]{1,0:T(1,128)S(1)}, f32[1,8192]{1,0:T(1,128)}, u32[]{:S(2)}) copy-start(f32[1,8192]{1,0:T(1,128)} %get-tuple-element.29) | copy-start | bytes 98308
  85.8 3.1 %copy-start.16 = (s32[8192]{0:T(1024)S(1)}, s32[8192]{0:T(1024)}, u32[]{:S(2)}) copy-start(s32[8192]{0:T(1024)} %param.23) | copy-start | bytes 98308
  95.7 3.9 %copy-start.13 = (f32[8192]{0:T(1024)S(1)}, f32[8192]{0:T(1024)}, u32[]{:S(2)}) copy-start(f32[8192]{0:T(1024)} %reduce_sum.19) | copy-start | bytes 98308
  109.3 3.2 %copy-start = (f32[4,60,8192]{2,1,0:T(8,128)}, f32[4,60,8192]{2,1,0:T(8,128)S(1)}, u32[]{:S(2)}) copy-start(f32[4,60,8192]{2,1,0:T(8,128)S(1)} %fusion.12) | copy-start | bytes 23592964
  116.9 35.4 %all-to-all-start.2 = ((f32[5,128,512]{2,0,1:T(8,128)}), f32[5,128,512]{2,0,1:T(8,128)}, u32[]{:S(2)}, u32[]{:S(2)}) async-start(f32[5,128,512]{2,0,1:T(8,128)} %copy.85), calls=%async_computation.2 | async-start | bytes 4194304 | tf_op jit(solution)/shard_map/all_to_all | solution.py:128
  122.9 3.7 %copy-start.2 = (bf16[1,72,8192]{2,1,0:T(8,128)(2,1)S(1)}, bf16[1,72,8192]{2,1,0:T(8,128)(2,1)}, u32[]{:S(2)}) copy-start(bf16[1,72,8192]{2,1,0:T(8,128)(2,1)} %fusion.10) | copy-start | bytes 3538948
  122.9 3.7 %copy-start.3 = (bf16[1,72,8192]{2,1,0:T(8,128)(2,1)S(1)}, bf16[1,72,8192]{2,1,0:T(8,128)(2,1)}, u32[]{:S(2)}) copy-start(bf16[1,72,8192]{2,1,0:T(8,128)(2,1)} %fusion.11) | copy-start | bytes 3538948
  129.1 23.2 %copy-start.7 = (s32[512,128]{1,0:T(8,128)S(1)}, s32[512,128]{1,0:T(8,128)}, u32[]{:S(2)}) copy-start(s32[512,128]{1,0:T(8,128)} %add_select_fusion.1) | copy-start | bytes 786436
  152.3 25.0 %copy-start.10 = (f32[8192]{0:T(1024)S(1)}, f32[8192]{0:T(1024)}, u32[]{:S(2)}) copy-start(f32[8192]{0:T(1024)} %param.19) | copy-start | bytes 98308
  152.3 25.0 %copy-start.12 = (f32[4,8192]{1,0:T(4,128)S(1)}, f32[4,8192]{1,0:T(4,128)}, u32[]{:S(2)}) copy-start(f32[4,8192]{1,0:T(4,128)} %param.20) | copy-start | bytes 393220
where the time goes:
time: 179 us; the launch traced here: 178 us
  matrix products  81.8 us (46%)
  local copies, waits for them, and re-layouts  33 us (18%)
  starting transfers between devices  27.7 us (15%)
  other arithmetic  18.7 us (10%)
  waiting for transfers between devices  15.7 us (9%)
    dot_general x1, matrix products, per_device(): jnp.einsum('fql,qml->fqm', window_rows, lane_hot, precision=highest)  30.5 us
    dot_general x1, matrix products, per_device(): jnp.einsum('fqm,qml->fql', returned.reshape(5, slot_tiles, width), lane_h...  24.3 us
    unnamed x47, local copies, waits for them, and re-layouts  23 us
    dot_general x4, matrix products, per_device(): jnp.dot(ocean_mixing, ocean_state[member], precision=highest)  15 us
    all_to_all x1, starting transfers between devices, per_device(): lax.all_to_all(request, ('comp', 'sub'), split_axis=0, concat_axis=0, til...  11.5 us
    all_to_all x1, waiting for transfers between devices, per_device(): lax.all_to_all(send_buffer.reshape(5, devices, capacity), ('comp', 'sub')...  11.5 us
    all_to_all x1, starting transfers between devices, per_device(): lax.all_to_all(served.reshape(4, devices, capacity), ('comp', 'sub'), spl...  10.2 us
    select_n x1, other arithmetic, per_device(): jnp.where(sea_mask[None, None, :] == 1, mixed_state, ocean_state)  9.59 us
  transfers between devices with their start and end apart: 3, of which 2 were waited for; matrix products, arithmetic and copies ran while one was open for 27% of the time, Pallas kernels for 0%

commit v1 on v0

--- a/solution.py
+++ b/solution.py
@@ -1,10 +1,13 @@
 import jax
 import jax.numpy as jnp
 from jax import lax
+from jax.experimental import pallas as pl
+from jax.experimental.pallas import tpu as pltpu
 from jax.sharding import PartitionSpec as P
 
 couple_rate = 0.5
 highest = lax.Precision.HIGHEST
+high = lax.Precision.HIGH
 
 
 def surface_fluxes(atmos_profiles, drag_factor, surface_before, downward_fluxes):
@@ -50,6 +53,59 @@
             fluxes[3],
         ]
     )
+
+
+def lane_gather_kernel(win_ref, lanes_ref, out_ref):
+    lanes = lanes_ref[...]
+    for field in range(win_ref.shape[0]):
+        out_ref[field] = jnp.take_along_axis(
+            win_ref[field], lanes, axis=1, mode="promise_in_bounds"
+        )
+
+
+def lane_gather(win, lanes):
+    return pl.pallas_call(
+        lane_gather_kernel,
+        out_shape=jax.ShapeDtypeStruct(win.shape, win.dtype),
+        in_specs=[pl.BlockSpec(memory_space=pltpu.VMEM)] * 2,
+        out_specs=pl.BlockSpec(memory_space=pltpu.VMEM),
+    )(win, lanes)
+
+
+def ocean_kernel(m_ref, m0_ref, x_ref, forcing_ref, sea_ref, out_ref, top_ref):
+    m = m_ref[...]
+    m0 = m0_ref[...]
+    sea = sea_ref[...] == 1
+    for field in range(x_ref.shape[1]):
+        x = x_ref[:, field, :]
+        mixed = jnp.dot(m, x, precision=highest, preferred_element_type=jnp.float32)
+        mixed = mixed + m0 * forcing_ref[field : field + 1, :]
+        updated = jnp.where(sea, mixed, x)
+        out_ref[:, field, :] = updated
+        top_ref[field : field + 1, :] = updated[0:1, :]
+
+
+def ocean_update(ocean_mixing, state_by_level, forcing, sea_mask, block=1024):
+    levels, fields, cells = state_by_level.shape
+    return pl.pallas_call(
+        ocean_kernel,
+        grid=(cells // block,),
+        out_shape=(
+            jax.ShapeDtypeStruct(state_by_level.shape, jnp.float32),
+            jax.ShapeDtypeStruct((fields, cells), jnp.float32),
+        ),
+        in_specs=[
+            pl.BlockSpec((levels, levels), lambda i: (0, 0)),
+            pl.BlockSpec((levels, 1), lambda i: (0, 0)),
+            pl.BlockSpec((levels, fields, block), lambda i: (0, 0, i)),
+            pl.BlockSpec((fields, block), lambda i: (0, i)),
+            pl.BlockSpec((1, block), lambda i: (0, i)),
+        ],
+        out_specs=(
+            pl.BlockSpec((levels, fields, block), lambda i: (0, 0, i)),
+            pl.BlockSpec((fields, block), lambda i: (0, i)),
+        ),
+    )(ocean_mixing, ocean_mixing[:, 0:1], state_by_level, forcing, sea_mask.reshape(1, cells))
 
 
 def per_device(
@@ -83,28 +139,22 @@
     placement = (tile_place[None, :] == jnp.arange(slot_tiles, dtype=jnp.int32)[:, None]).astype(
         jnp.float32
     )
-
-    def to_slots(values):
-        return jnp.einsum("qt,ftl->fql", placement, values, precision=highest)
-
-    wanted = parent_column.reshape(1, tile_count, width).astype(jnp.float32)
-    request = (to_slots(wanted)[0] + 0.5).astype(jnp.int32).reshape(devices, capacity)
-    asked_ids = lax.all_to_all(request, ("comp", "sub"), split_axis=0, concat_axis=0, tiled=True)
-    asked_tiles = asked_ids.reshape(slot_tiles, width)
-    window_hot = (
-        (asked_tiles[:, 0] // width)[:, None] == jnp.arange(windows, dtype=jnp.int32)[None, :]
-    ).astype(jnp.float32)
-    lane_hot = (
-        (asked_tiles % width)[:, :, None] == jnp.arange(width, dtype=jnp.int32)[None, None, :]
-    ).astype(jnp.float32)
+    tiles_pc = parent_column.reshape(tile_count, width)
+    window_of_tile = tiles_pc[:, 0] // width
+    lanes = tiles_pc % width
+
+    request = jnp.dot(placement, window_of_tile.astype(jnp.float32), precision=highest)
+    request = (request + 0.5).astype(jnp.int32).reshape(devices, slot_tiles // devices)
+    asked = lax.all_to_all(request, ("comp", "sub"), split_axis=0, concat_axis=0, tiled=True)
+    asked = asked.reshape(slot_tiles)
+    window_hot = (asked[:, None] == jnp.arange(windows, dtype=jnp.int32)[None, :]).astype(
+        jnp.float32
+    )
+
     fluxes = surface_fluxes(atmos_profiles, drag_factor, surface_before, downward_fluxes)
     column_forcing = forcing_rows(fluxes)
-    window_rows = jnp.einsum(
+    served = jnp.einsum(
         "qw,fwl->fql", window_hot, column_forcing.reshape(4, windows, width), precision=highest
-    )
-    served = jnp.einsum("fql,qml->fqm", window_rows, lane_hot, precision=highest)
-    base_mix = jnp.stack(
-        [jnp.dot(ocean_mixing, ocean_state[member], precision=highest) for member in range(4)]
     )
     arrived = lax.all_to_all(
         served.reshape(4, devices, capacity),
@@ -114,17 +164,25 @@
         tiled=True,
     )
     atmos_updated = diffuse_atmos(atmos_profiles, atmos_mixing, fluxes)
-    at_cells = jnp.einsum(
+    win_local = jnp.einsum(
         "qt,fql->ftl", placement, arrived.reshape(4, slot_tiles, width), precision=highest
-    ).reshape(4, intersections, ocean_cells)
+    )
+    at_cells = lane_gather(win_local, lanes).reshape(4, intersections, ocean_cells)
     forcing = jnp.sum(ocean_weight[None] * at_cells, axis=1) / jnp.sum(ocean_weight, axis=0)[None]
-    mixed_state = base_mix + ocean_mixing[:, 0][None, :, None] * forcing[:, None, :]
-    ocean_updated = jnp.where(sea_mask[None, None, :] == 1, mixed_state, ocean_state)
+
+    state_by_level = jnp.transpose(ocean_state, (1, 0, 2))
+    updated_by_level, top = ocean_update(ocean_mixing, state_by_level, forcing, sea_mask)
+    ocean_updated = jnp.transpose(updated_by_level, (1, 0, 2))
+
     sea_share = atmos_weight * sea_mask.astype(jnp.float32)[None, :]
-    outgoing = jnp.concatenate(
-        [sea_share[None] * ocean_updated[:, 0, :][:, None, :], sea_share[None]], axis=0
-    )
-    send_buffer = to_slots(outgoing.reshape(5, tile_count, width))
+    outgoing = jnp.concatenate([sea_share[None] * top[:, None, :], sea_share[None]], axis=0)
+    lane_hot = (lanes[:, :, None] == jnp.arange(width, dtype=jnp.int32)[None, None, :]).astype(
+        jnp.float32
+    )
+    partial = jnp.einsum(
+        "ftl,tlc->ftc", outgoing.reshape(5, tile_count, width), lane_hot, precision=high
+    )
+    send_buffer = jnp.einsum("qt,ftc->fqc", placement, partial, precision=highest)
     returned = lax.all_to_all(
         send_buffer.reshape(5, devices, capacity),
         ("comp", "sub"),
@@ -132,12 +190,9 @@
         concat_axis=1,
         tiled=True,
     )
-    lanes_back = jnp.einsum(
-        "fqm,qml->fql", returned.reshape(5, slot_tiles, width), lane_hot, precision=highest
-    )
-    summed = jnp.einsum("qw,fql->fwl", window_hot, lanes_back, precision=highest).reshape(
-        5, columns
-    )
+    summed = jnp.einsum(
+        "qw,fqc->fwc", window_hot, returned.reshape(5, slot_tiles, width), precision=highest
+    ).reshape(5, columns)
     surface_state = (summed[:4] + land_weight[None] * land_surface) / (summed[4] + land_weight)[
         None
     ]

time: 179 us -> 130 us (0.73)
  matrix products: 81.8 us -> 26 us
  waiting for transfers between devices: 15.7 us -> 39.5 us
  local copies, waits for them, and re-layouts: 33 us -> 12.9 us
  Pallas kernels: 0 us -> 15.4 us
  other arithmetic: 18.7 us -> 12.1 us
  starting transfers between devices: 27.7 us -> 22.1 us
    dot_general x9 -> x4, matrix products: 72.2 us -> 14.7 us  [the longest x1 12.6 us: per_device(): jnp.einsum('ftl,tlc->ftc', outgoing.reshape(5, tile_count, width), lane_h...]
    unnamed x47 -> x18, local copies, waits for them, and re-layouts: 23 us -> 0.29 us
    pallas_call x0 -> x2, Pallas kernels: none -> 15.4 us  [the longest x1 13.1 us: ocean_update(): pl.pallas_call(ocean_kernel, grid=(cells // block,), out_shape=(jax.Shape...]
    all_to_all x1, waiting for transfers between devices: 11.5 us -> 23.7 us  [per_device(): lax.all_to_all(send_buffer.reshape(5, devices, capacity), ('comp', 'sub')...]
    select_n x3 -> x1, other arithmetic: 10.6 us -> 0.7 us  [per_device(): lanes = tiles_pc % width]
    all_to_all x1, waiting for transfers between devices: 4.23 us -> 11.9 us  [per_device(): lax.all_to_all(served.reshape(4, devices, capacity), ('comp', 'sub'), spl...]
    all_to_all x1, starting transfers between devices: 10.2 us -> 5.88 us  [per_device(): lax.all_to_all(served.reshape(4, devices, capacity), ('comp', 'sub'), spl...]
    reshape x1 -> x5, local copies, waits for them, and re-layouts: 0.21 us -> 4.17 us  [the longest x2 1.81 us: per_device(): served.reshape(4, devices, capacity)]
  transfers between devices with their start and end apart: 3 -> 3, of which waited for: 2 -> 3; matrix products, arithmetic and copies ran while one was open for 27% -> 14% of each run, Pallas kernels for 0% -> 0%
where the time goes in v1:
time: 130 us; the launch traced here: 129 us
  waiting for transfers between devices  39.5 us (30%)
  matrix products  26 us (20%)
  starting transfers between devices  22.1 us (17%)
  Pallas kernels  15.4 us (12%)
  local copies, waits for them, and re-layouts  12.9 us (10%)
  other arithmetic  12.1 us (9%)
    all_to_all x1, waiting for transfers between devices, per_device(): lax.all_to_all(send_buffer.reshape(5, devices, capacity), ('comp', 'sub')...  23.7 us
    pallas_call x1, Pallas kernels, ocean_update(): pl.pallas_call(ocean_kernel, grid=(cells // block,), out_shape=(jax.Shape...  13.1 us
    dot_general x1, matrix products, per_device(): jnp.einsum('ftl,tlc->ftc', outgoing.reshape(5, tile_count, width), lane_h...  12.6 us
    all_to_all x1, waiting for transfers between devices, per_device(): lax.all_to_all(served.reshape(4, devices, capacity), ('comp', 'sub'), spl...  11.9 us
    all_to_all x1, starting transfers between devices, per_device(): lax.all_to_all(request, ('comp', 'sub'), split_axis=0, concat_axis=0, til...  11.5 us
    dot_general x4, matrix products, diffuse_atmos(): jnp.dot(atmos_mixing, atmos_profiles[member], preferred_element_type=jnp....  9.16 us
    all_to_all x1, starting transfers between devices, per_device(): lax.all_to_all(served.reshape(4, devices, capacity), ('comp', 'sub'), spl...  5.88 us
    all_to_all x1, starting transfers between devices, per_device(): lax.all_to_all(send_buffer.reshape(5, devices, capacity), ('comp', 'sub')...  4.76 us
  transfers between devices with their start and end apart: 3, of which 3 were waited for; matrix products, arithmetic and copies ran while one was open for 14% of the time, Pallas kernels for 0%

profile of v1, /device:TPU:1, one launch (start us, length us, event | category | flops | bytes accessed | tf_op | source)
XLA Modules:
  0.0 129.1 jit_solution(11523161186490515299)
XLA Ops:
  0.6 1.0 reshape.123
  4.0 11.5 %all-to-all-start = ((s32[128,1,4]{2,1,0:T(1,128)}), s32[128,1,4]{2,1,0:T(1,128)S(1)}, u32[]{:S(2)}, u32[]{:S(2)}) async-start(s32[128,1,4]{2,1,0:T(1,128)} %bitcast.35), calls=%async_computation | async-start | bytes 131072 | tf_op jit(solution)/shard_map/all_to_all | solution.py:148
  16.3 1.2 fusion.53
  17.5 1.1 slice_convert_fusion
  18.7 1.4 %fusion.48 = (f32[1,8192]{1,0:T(1,128)S(1)}, f32[1,8192]{1,0:T(1,128)S(1)}, f32[1,8192]{1,0:T(1,128)S(1)}, f32[1,8192]{1,0:T(1,128)S(1)}) fusion(f32[4,1,8192]{2,1,0:T(1,128)S(1)} %slice_convert_fusion, f32[4,8192]{1,0:T(4,128)} %param.17), kind=kLoop, calls=%fused_computation.75 | loop fusion | flops 32768 | bytes 393216 | tf_op jit(solution)/shard_map/sub | solution.py:15
  21.1 3.9 %all-to-all-done = s32[128,1,4]{2,1,0:T(1,128)S(1)} async-done(((s32[128,1,4]{2,1,0:T(1,128)}), s32[128,1,4]{2,1,0:T(1,128)S(1)}, u32[]{:S(2)}, u32[]{:S(2)}) %all-to-all-start) | async-done | bytes 2080 | tf_op jit(solution)/shard_map/all_to_all | solution.py:148
  27.6 1.6 %copy.37 = f32[4,128,512]{2,0,1:T(4,128)} copy(f32[4,128,512]{2,1,0:T(8,128)S(1)} %reshape.124) | data formatting | bytes 2097152 | tf_op jit(solution)/shard_map/reshape | solution.py:160
  29.3 5.9 %all-to-all-start.1 = ((f32[4,128,512]{2,0,1:T(4,128)}), f32[4,128,512]{2,0,1:T(4,128)S(1)}, u32[]{:S(2)}, u32[]{:S(2)}) async-start(f32[4,128,512]{2,0,1:T(4,128)} %copy.37), calls=%async_computation.1 | async-start | bytes 2097152 | tf_op jit(solution)/shard_map/all_to_all | solution.py:159
  35.8 2.8 %fusion.5 = bf16[1,72,8192]{2,1,0:T(8,128)(2,1)} fusion(bf16[72,72]{1,0:T(8,128)(2,1)S(1)} %copy-done.4, f32[8192]{0:T(1024)S(1)} %bitcast.115, bf16[4,72,8192]{2,1,0:T(8,128)(2,1)} %param.14, f32[72]{0:T(128)S(1)} %convert_reduce_fusion), kind=kOutput, calls=%fused_computation.10 | convolution fusion | flops 86704128 | bytes 2402720 | tf_op jit(solution)/shard_map/dot_general | solution.py:40
  38.6 2.8 %fusion.8 = bf16[1,72,8192]{2,1,0:T(8,128)(2,1)} fusion(bf16[72,72]{1,0:T(8,128)(2,1)S(1)} %copy-done.4, f32[8192]{0:T(1024)S(1)} %bitcast.114, f32[72]{0:T(128)S(1)} %convert_reduce_fusion, bf16[4,72,8192]{2,1,0:T(8,128)(2,1)} %param.14), kind=kOutput, calls=%fused_computation.13 | convolution fusion | flops 86704128 | bytes 2402720 | tf_op jit(solution)/shard_map/dot_general | solution.py:40
  42.0 11.9 %all-to-all-done.1 = f32[4,128,512]{2,0,1:T(4,128)S(1)} async-done(((f32[4,128,512]{2,0,1:T(4,128)}), f32[4,128,512]{2,0,1:T(4,128)S(1)}, u32[]{:S(2)}, u32[]{:S(2)}) %all-to-all-start.1) | async-done | bytes 1048608 | tf_op jit(solution)/shard_map/all_to_all | solution.py:159
  54.3 1.5 %convolution_bitcast_fusion.2.win_ref = f32[4,256,128]{2,1,0:T(8,128)} fusion(f32[4,512,128]{2,1,0:T(8,128)S(1)} %reshape.125, s32[256]{0:T(256)S(1)} %and_select_fusion.1), kind=kOutput, calls=%fused_computation.19 | convolution fusion | flops 805437440 | bytes 1573888 | tf_op jit(solution)/shard_map/qt,fql->ftl/dot_general | solution.py:167
  55.9 2.3 %shard_map.157 = f32[4,256,128]{2,1,0:T(8,128)} custom-call(f32[4,256,128]{2,1,0:T(8,128)} %convolution_bitcast_fusion.2.win_ref, s32[256,128]{1,0:T(8,128)} %add_select_fusion.lanes_ref), custom_call_target="tpu_custom_call" | custom-call | tf_op jit(solution)/shard_map/pallas_call | solution.py:67
  58.1 1.2 reshape.126
  60.5 13.1 %shard_map.158 = (f32[60,4,8192]{2,1,0:T(4,128)}, f32[4,8192]{1,0:T(4,128)}) custom-call(f32[60,60]{1,0:T(8,128)} %m_ref.1, f32[60,1]{1,0:T(8,128)} %bitcast.110, f32[60,4,8192]{2,1,0:T(4,128)} %bitcast.103, f32[4,8192]{1,0:T(4,128)} %broadcast_divide_fusion.forcing_ref, s32[1,8192]{1,0:T(1,128)} %bitcast.111), custom_call_target="tpu_custom_call" | custom-call | tf_op jit(solution)/shard_map/pallas_call | solution.py:90
  73.6 1.0 mul.159
  75.4 12.6 %fusion.10 = f32[5,256,128]{2,0,1:T(8,128)S(1)} fusion(s32[256,128]{1,0:T(8,128)S(1)} %copy-done.2, f32[1,256,128]{2,0,1:T(1,128)S(1)} %concatenate.7, f32[4,256,128]{2,0,1:T(4,128)S(1)} %copy_multiply_fusion), kind=kOutput, calls=%fused_computation.17 | convolution fusion | flops 130187264 | bytes 1441792 | tf_op jit(solution)/shard_map/ftl,tlc->ftc/dot_general | solution.py:182
  88.0 1.2 convolution_bitcast_fusion
  89.8 2.2 %copy.44 = f32[5,128,512]{2,0,1:T(8,128)} copy(f32[5,128,512]{2,1,0:T(8,128)S(1)} %reshape.128) | data formatting | bytes 2621440 | tf_op jit(solution)/shard_map/reshape | solution.py:187
  92.0 4.8 %all-to-all-start.2 = ((f32[5,128,512]{2,0,1:T(8,128)}), f32[5,128,512]{2,0,1:T(8,128)S(1)}, u32[]{:S(2)}, u32[]{:S(2)}) async-start(f32[5,128,512]{2,0,1:T(8,128)} %copy.44), calls=%async_computation.2 | async-start | bytes 4194304 | tf_op jit(solution)/shard_map/all_to_all | solution.py:186
  96.8 1.9 %fusion.6 = bf16[1,72,8192]{2,1,0:T(8,128)(2,1)S(1)} fusion(bf16[72,72]{1,0:T(8,128)(2,1)S(1)} %copy-done.4, f32[8192]{0:T(1024)S(1)} %bitcast.113, bf16[4,72,8192]{2,1,0:T(8,128)(2,1)} %param.14, f32[72]{0:T(128)S(1)} %convert_reduce_fusion), kind=kOutput, calls=%fused_computation.11 | convolution fusion | flops 86704128 | bytes 2402720 | tf_op jit(solution)/shard_map/dot_general | solution.py:40
  98.7 1.7 %fusion.7 = bf16[1,72,8192]{2,1,0:T(8,128)(2,1)S(1)} fusion(bf16[72,72]{1,0:T(8,128)(2,1)S(1)} %copy-done.4, f32[8192]{0:T(1024)S(1)} %bitcast.112, bf16[4,72,8192]{2,1,0:T(8,128)(2,1)} %param.14, f32[72]{0:T(128)S(1)} %convert_reduce_fusion), kind=kOutput, calls=%fused_computation.12 | convolution fusion | flops 86704128 | bytes 2402720 | tf_op jit(solution)/shard_map/dot_general | solution.py:40
  100.4 2.5 %pad_maximum_fusion = bf16[4,72,8192]{2,1,0:T(8,128)(2,1)} fusion(bf16[1,72,8192]{2,1,0:T(8,128)(2,1)S(1)} %copy-done, bf16[1,72,8192]{2,1,0:T(8,128)(2,1)S(1)} %fusion.6, bf16[1,72,8192]{2,1,0:T(8,128)(2,1)S(1)} %fusion.7, bf16[1,72,8192]{2,1,0:T(8,128)(2,1)S(1)} %copy-done.1), kind=kLoop, calls=%fused_computation.15 | loop fusion | flops 7077888 | bytes 9437184 | tf_op jit(solution)/shard_map/stack | solution.py:44
  102.9 23.7 %all-to-all-done.2 = f32[5,128,512]{2,0,1:T(8,128)S(1)} async-done(((f32[5,128,512]{2,0,1:T(8,128)}), f32[5,128,512]{2,0,1:T(8,128)S(1)}, u32[]{:S(2)}, u32[]{:S(2)}) %all-to-all-start.2) | async-done | bytes 1310752 | tf_op jit(solution)/shard_map/all_to_all | solution.py:186
  (56 shorter events, 13.2 us)
Async XLA Ops:
  0.6 20.3 %copy-start.7 = (f32[4,8192]{1,0:T(4,128)S(1)}, f32[4,8192]{1,0:T(4,128)}, u32[]{:S(2)}) copy-start(f32[4,8192]{1,0:T(4,128)} %param.27) | copy-start | bytes 393220
  4.0 21.0 %all-to-all-start = ((s32[128,1,4]{2,1,0:T(1,128)}), s32[128,1,4]{2,1,0:T(1,128)S(1)}, u32[]{:S(2)}, u32[]{:S(2)}) async-start(s32[128,1,4]{2,1,0:T(1,128)} %bitcast.35), calls=%async_computation | async-start | bytes 131072 | tf_op jit(solution)/shard_map/all_to_all | solution.py:148
  27.6 7.9 %copy-start.3 = (f32[4,8192]{1,0:T(4,128)S(1)}, f32[4,8192]{1,0:T(4,128)}, u32[]{:S(2)}) copy-start(f32[4,8192]{1,0:T(4,128)} %param.26) | copy-start | bytes 393220
  27.6 8.0 %copy-start.4 = (bf16[72,72]{1,0:T(8,128)(2,1)S(1)}, bf16[72,72]{1,0:T(8,128)(2,1)}, u32[]{:S(2)}) copy-start(bf16[72,72]{1,0:T(8,128)(2,1)} %param.15) | copy-start | bytes 31108
  29.3 24.7 %all-to-all-start.1 = ((f32[4,128,512]{2,0,1:T(4,128)}), f32[4,128,512]{2,0,1:T(4,128)S(1)}, u32[]{:S(2)}, u32[]{:S(2)}) async-start(f32[4,128,512]{2,0,1:T(4,128)} %copy.37), calls=%async_computation.1 | async-start | bytes 2097152 | tf_op jit(solution)/shard_map/all_to_all | solution.py:159
  73.6 1.8 %copy-start.2 = (s32[256,128]{1,0:T(8,128)S(1)}, s32[256,128]{1,0:T(8,128)}, u32[]{:S(2)}) copy-start(s32[256,128]{1,0:T(8,128)} %add_select_fusion.lanes_ref) | copy-start | bytes 393220
  92.0 34.6 %all-to-all-start.2 = ((f32[5,128,512]{2,0,1:T(8,128)}), f32[5,128,512]{2,0,1:T(8,128)S(1)}, u32[]{:S(2)}, u32[]{:S(2)}) async-start(f32[5,128,512]{2,0,1:T(8,128)} %copy.44), calls=%async_computation.2 | async-start | bytes 4194304 | tf_op jit(solution)/shard_map/all_to_all | solution.py:186
  96.7 3.7 %copy-start = (bf16[1,72,8192]{2,1,0:T(8,128)(2,1)S(1)}, bf16[1,72,8192]{2,1,0:T(8,128)(2,1)}, u32[]{:S(2)}) copy-start(bf16[1,72,8192]{2,1,0:T(8,128)(2,1)} %fusion.5) | copy-start | bytes 3538948
  96.7 3.7 %copy-start.1 = (bf16[1,72,8192]{2,1,0:T(8,128)(2,1)S(1)}, bf16[1,72,8192]{2,1,0:T(8,128)(2,1)}, u32[]{:S(2)}) copy-start(bf16[1,72,8192]{2,1,0:T(8,128)(2,1)} %fusion.8) | copy-start | bytes 3538948
  127.4 0.8 copy-start.5
  127.4 0.9 copy-start.6

commit v2 on v1

--- a/solution.py
+++ b/solution.py
@@ -1,3 +1,5 @@
+import functools
+
 import jax
 import jax.numpy as jnp
 from jax import lax
@@ -5,6 +7,7 @@
 from jax.experimental.pallas import tpu as pltpu
 from jax.sharding import PartitionSpec as P
 
+MESH = pl.DeviceIdType.MESH
 couple_rate = 0.5
 highest = lax.Precision.HIGHEST
 high = lax.Precision.HIGH
@@ -106,6 +109,62 @@
             pl.BlockSpec((fields, block), lambda i: (0, i)),
         ),
     )(ocean_mixing, ocean_mixing[:, 0:1], state_by_level, forcing, sea_mask.reshape(1, cells))
+
+
+def exchange_kernel(n_sub, x_ref, out_ref, send_sem, recv_sem):
+    n = x_ref.shape[0]
+    me = lax.axis_index("comp") * n_sub + lax.axis_index("sub")
+
+    def device_of(peer):
+        return (peer // n_sub, peer % n_sub)
+
+    barrier = pltpu.get_barrier_semaphore()
+
+    def greet(step, carry):
+        peer = lax.rem(me + step, n)
+        pl.semaphore_signal(barrier, 1, device_id=device_of(peer), device_id_type=MESH)
+        return carry
+
+    lax.fori_loop(1, n, greet, 0)
+    pl.semaphore_wait(barrier, n - 1)
+
+    def send(step, carry):
+        peer = lax.rem(me + step, n)
+        pltpu.make_async_remote_copy(
+            src_ref=x_ref.at[peer],
+            dst_ref=out_ref.at[me],
+            send_sem=send_sem,
+            recv_sem=recv_sem,
+            device_id=device_of(peer),
+            device_id_type=MESH,
+        ).start()
+        return carry
+
+    lax.fori_loop(1, n, send, 0)
+    out_ref[me] = x_ref[me]
+    everyone = pltpu.make_async_remote_copy(
+        src_ref=x_ref.at[pl.ds(0, n - 1)],
+        dst_ref=out_ref.at[pl.ds(0, n - 1)],
+        send_sem=send_sem,
+        recv_sem=recv_sem,
+        device_id=device_of(lax.rem(me + 1, n)),
+        device_id_type=MESH,
+    )
+    everyone.wait_send()
+    everyone.wait_recv()
+
+
+def exchange(x, n_sub, collective_id):
+    return pl.pallas_call(
+        functools.partial(exchange_kernel, n_sub),
+        out_shape=jax.ShapeDtypeStruct(x.shape, x.dtype),
+        in_specs=[pl.BlockSpec(memory_space=pltpu.VMEM)],
+        out_specs=pl.BlockSpec(memory_space=pltpu.VMEM),
+        scratch_shapes=[pltpu.SemaphoreType.DMA, pltpu.SemaphoreType.DMA],
+        compiler_params=pltpu.CompilerParams(
+            collective_id=collective_id, has_side_effects=True
+        ),
+    )(x)
 
 
 def per_device(
@@ -144,8 +203,9 @@
     lanes = tiles_pc % width
 
     request = jnp.dot(placement, window_of_tile.astype(jnp.float32), precision=highest)
-    request = (request + 0.5).astype(jnp.int32).reshape(devices, slot_tiles // devices)
-    asked = lax.all_to_all(request, ("comp", "sub"), split_axis=0, concat_axis=0, tiled=True)
+    request = (request + 0.5).astype(jnp.int32).reshape(devices, 1, slot_tiles // devices)
+    request = jnp.pad(request, ((0, 0), (0, 0), (0, width - slot_tiles // devices)))
+    asked = exchange(request, sub_count, 0)[:, 0, : slot_tiles // devices]
     asked = asked.reshape(slot_tiles)
     window_hot = (asked[:, None] == jnp.arange(windows, dtype=jnp.int32)[None, :]).astype(
         jnp.float32
@@ -154,18 +214,12 @@
     fluxes = surface_fluxes(atmos_profiles, drag_factor, surface_before, downward_fluxes)
     column_forcing = forcing_rows(fluxes)
     served = jnp.einsum(
-        "qw,fwl->fql", window_hot, column_forcing.reshape(4, windows, width), precision=highest
-    )
-    arrived = lax.all_to_all(
-        served.reshape(4, devices, capacity),
-        ("comp", "sub"),
-        split_axis=1,
-        concat_axis=1,
-        tiled=True,
-    )
+        "qw,fwl->qfl", window_hot, column_forcing.reshape(4, windows, width), precision=highest
+    )
+    arrived = exchange(served.reshape(devices, -1, width), sub_count, 1)
     atmos_updated = diffuse_atmos(atmos_profiles, atmos_mixing, fluxes)
     win_local = jnp.einsum(
-        "qt,fql->ftl", placement, arrived.reshape(4, slot_tiles, width), precision=highest
+        "qt,qfl->ftl", placement, arrived.reshape(slot_tiles, 4, width), precision=highest
     )
     at_cells = lane_gather(win_local, lanes).reshape(4, intersections, ocean_cells)
     forcing = jnp.sum(ocean_weight[None] * at_cells, axis=1) / jnp.sum(ocean_weight, axis=0)[None]
@@ -182,16 +236,10 @@
     partial = jnp.einsum(
         "ftl,tlc->ftc", outgoing.reshape(5, tile_count, width), lane_hot, precision=high
     )
-    send_buffer = jnp.einsum("qt,ftc->fqc", placement, partial, precision=highest)
-    returned = lax.all_to_all(
-        send_buffer.reshape(5, devices, capacity),
-        ("comp", "sub"),
-        split_axis=1,
-        concat_axis=1,
-        tiled=True,
-    )
+    send_buffer = jnp.einsum("qt,ftc->qfc", placement, partial, precision=highest)
+    returned = exchange(send_buffer.reshape(devices, -1, width), sub_count, 2)
     summed = jnp.einsum(
-        "qw,fqc->fwc", window_hot, returned.reshape(5, slot_tiles, width), precision=highest
+        "qw,qfc->fwc", window_hot, returned.reshape(slot_tiles, 5, width), precision=highest
     ).reshape(5, columns)
     surface_state = (summed[:4] + land_weight[None] * land_surface) / (summed[4] + land_weight)[
         None

time: 130 us -> 136 us (1.046)
  Pallas kernels: 15.4 us -> 85.5 us
  waiting for transfers between devices: 39.5 us -> 0 us
  starting transfers between devices: 22.1 us -> 0 us
    pallas_call x0 -> x3, Pallas kernels: none -> 70.1 us  [exchange(): pl.pallas_call(functools.partial(exchange_kernel, n_sub), out_shape=jax.S...]
    all_to_all x3 -> x0, waiting for transfers between devices: 39.5 us -> none  [the longest x1 23.7 us: per_device(): lax.all_to_all(send_buffer.reshape(5, devices, capacity), ('comp', 'sub')...]
    all_to_all x3 -> x0, starting transfers between devices: 22.1 us -> none  [the longest x1 11.5 us: per_device(): lax.all_to_all(request, ('comp', 'sub'), split_axis=0, concat_axis=0, til...]
    dot_general x0 -> x2, local copies, waits for them, and re-layouts: none -> 2.46 us  [the longest x1 1.65 us: per_device(): jnp.einsum('qw,fwl->qfl', window_hot, column_forcing.reshape(4, windows,...]
    all_to_all x4 -> x0, local copies, waits for them, and re-layouts: 2.37 us -> none  [the longest x2 1.27 us: per_device(): lax.all_to_all(request, ('comp', 'sub'), split_axis=0, concat_axis=0, til...]
    dot_general x4, matrix products: 9.16 us -> 6.97 us  [diffuse_atmos(): jnp.dot(atmos_mixing, atmos_profiles[member], preferred_element_type=jnp....]
    reshape x6 -> x3, local copies, waits for them, and re-layouts: 4.31 us -> 2.97 us  [the longest x1 1.51 us: per_device(): returned.reshape(slot_tiles, 5, width)]
  transfers between devices with their start and end apart: 3 -> 0, of which waited for: 3 -> 0; matrix products, arithmetic and copies ran while one was open for 14% -> 0% of each run, Pallas kernels for 0% -> 0%
where the time goes in v2:
time: 136 us; the launch traced here: 135 us
  Pallas kernels  85.5 us (63%)
  matrix products  24.9 us (18%)
  local copies, waits for them, and re-layouts  12.4 us (9%)
  other arithmetic  11.6 us (9%)
    pallas_call x3, Pallas kernels, exchange(): pl.pallas_call(functools.partial(exchange_kernel, n_sub), out_shape=jax.S...  70.1 us
    pallas_call x1, Pallas kernels, ocean_update(): pl.pallas_call(ocean_kernel, grid=(cells // block,), out_shape=(jax.Shape...  13.1 us
    dot_general x1, matrix products, per_device(): jnp.einsum('ftl,tlc->ftc', outgoing.reshape(5, tile_count, width), lane_h...  12.6 us
    dot_general x4, matrix products, diffuse_atmos(): jnp.dot(atmos_mixing, atmos_profiles[member], preferred_element_type=jnp....  6.97 us
    dot_general x1, matrix products, per_device(): jnp.einsum('qt,qfl->ftl', placement, arrived.reshape(slot_tiles, 4, width...  2.79 us

profile of v2, /device:TPU:1, one launch (start us, length us, event | category | flops | bytes accessed | tf_op | source)
XLA Modules:
  0.0 135.3 jit_solution(15918177329981687623)
XLA Ops:
  2.4 1.0 reduce_sum.19
  3.3 0.9 broadcast_multiply_fusion.1
  4.3 1.3 fusion.58
  5.5 1.0 reshape.121
  7.6 1.0 reshape.120
  9.8 18.4 %shard_map.157 = s32[128,1,128]{2,1,0:T(1,128)} custom-call(s32[128,1,128]{2,1,0:T(1,128)} %pad.4.x_ref), custom_call_target="tpu_custom_call" | custom-call | tf_op jit(solution)/shard_map/pallas_call | solution.py:158
  28.2 1.0 slice_reduce_fusion.1
  29.3 1.1 slice_convert_fusion
  31.6 1.6 %copy.24 = f32[512,4,128]{2,1,0:T(4,128)} copy(f32[512,4,128]{2,0,1:T(8,128)S(1)} %fusion.37) | data formatting | bytes 2097152 | tf_op jit(solution)/shard_map/qw,fwl->qfl/dot_general | solution.py:216
  33.2 24.4 %shard_map.158 = f32[128,16,128]{2,1,0:T(8,128)} custom-call(f32[128,16,128]{2,1,0:T(8,128)} %bitcast.101), custom_call_target="tpu_custom_call" | custom-call | tf_op jit(solution)/shard_map/pallas_call | solution.py:158
  57.6 2.8 %convolution_bitcast_fusion.win_ref = f32[4,256,128]{2,1,0:T(8,128)} fusion(f32[512,4,128]{2,1,0:T(4,128)} %bitcast.102, s32[256]{0:T(256)S(1)} %and_select_fusion.1), kind=kOutput, calls=%fused_computation.18 | convolution fusion | flops 805437440 | bytes 1573888 | tf_op jit(solution)/shard_map/qt,qfl->ftl/dot_general | solution.py:221
  60.4 2.3 %shard_map.159 = f32[4,256,128]{2,1,0:T(8,128)} custom-call(f32[4,256,128]{2,1,0:T(8,128)} %convolution_bitcast_fusion.win_ref, s32[256,128]{1,0:T(8,128)} %add_select_fusion.lanes_ref), custom_call_target="tpu_custom_call" | custom-call | tf_op jit(solution)/shard_map/pallas_call | solution.py:70
  62.7 1.2 reshape.125
  65.0 1.7 %fusion.5 = bf16[1,72,8192]{2,1,0:T(8,128)(2,1)S(1)} fusion(bf16[72,72]{1,0:T(8,128)(2,1)S(1)} %copy-done.2, f32[8192]{0:T(1024)S(1)} %bitcast.115, bf16[4,72,8192]{2,1,0:T(8,128)(2,1)} %param.14, f32[72]{0:T(128)S(1)} %convert_reduce_fusion), kind=kOutput, calls=%fused_computation.10 | convolution fusion | flops 86704128 | bytes 2402720 | tf_op jit(solution)/shard_map/dot_general | solution.py:43
  66.8 1.7 %fusion.8 = bf16[1,72,8192]{2,1,0:T(8,128)(2,1)S(1)} fusion(bf16[72,72]{1,0:T(8,128)(2,1)S(1)} %copy-done.2, f32[8192]{0:T(1024)S(1)} %bitcast.114, f32[72]{0:T(128)S(1)} %convert_reduce_fusion, bf16[4,72,8192]{2,1,0:T(8,128)(2,1)} %param.14), kind=kOutput, calls=%fused_computation.13 | convolution fusion | flops 86704128 | bytes 2402720 | tf_op jit(solution)/shard_map/dot_general | solution.py:43
  68.5 1.7 %fusion.6 = bf16[1,72,8192]{2,1,0:T(8,128)(2,1)S(1)} fusion(bf16[72,72]{1,0:T(8,128)(2,1)S(1)} %copy-done.2, f32[8192]{0:T(1024)S(1)} %bitcast.113, bf16[4,72,8192]{2,1,0:T(8,128)(2,1)} %param.14, f32[72]{0:T(128)S(1)} %convert_reduce_fusion), kind=kOutput, calls=%fused_computation.11 | convolution fusion | flops 86704128 | bytes 2402720 | tf_op jit(solution)/shard_map/dot_general | solution.py:43
  70.3 1.7 %fusion.7 = bf16[1,72,8192]{2,1,0:T(8,128)(2,1)S(1)} fusion(bf16[72,72]{1,0:T(8,128)(2,1)S(1)} %copy-done.2, f32[8192]{0:T(1024)S(1)} %bitcast.112, bf16[4,72,8192]{2,1,0:T(8,128)(2,1)} %param.14, f32[72]{0:T(128)S(1)} %convert_reduce_fusion), kind=kOutput, calls=%fused_computation.12 | convolution fusion | flops 86704128 | bytes 2402720 | tf_op jit(solution)/shard_map/dot_general | solution.py:43
  72.0 2.5 %pad_maximum_fusion = bf16[4,72,8192]{2,1,0:T(8,128)(2,1)} fusion(bf16[1,72,8192]{2,1,0:T(8,128)(2,1)S(1)} %fusion.5, bf16[1,72,8192]{2,1,0:T(8,128)(2,1)S(1)} %fusion.6, bf16[1,72,8192]{2,1,0:T(8,128)(2,1)S(1)} %fusion.7, bf16[1,72,8192]{2,1,0:T(8,128)(2,1)S(1)} %fusion.8), kind=kLoop, calls=%fused_computation.15 | loop fusion | flops 7077888 | bytes 9437184 | tf_op jit(solution)/shard_map/stack | solution.py:47
  74.5 13.1 %shard_map.160 = (f32[60,4,8192]{2,1,0:T(4,128)}, f32[4,8192]{1,0:T(4,128)}) custom-call(f32[60,60]{1,0:T(8,128)} %m_ref.1, f32[60,1]{1,0:T(8,128)} %bitcast.110, f32[60,4,8192]{2,1,0:T(4,128)} %bitcast.100, f32[4,8192]{1,0:T(4,128)} %broadcast_divide_fusion.forcing_ref, s32[1,8192]{1,0:T(1,128)} %bitcast.111), custom_call_target="tpu_custom_call" | custom-call | tf_op jit(solution)/shard_map/pallas_call | solution.py:93
  87.6 1.0 mul.159
  89.2 12.6 %fusion = f32[256,128,5]{1,2,0:T(8,128)S(1)} fusion(s32[256,128]{1,0:T(8,128)S(1)} %copy-done, f32[5,256,128]{2,1,0:T(8,128)S(1)} %pad_maximum_fusion.1), kind=kOutput, calls=%fused_computation.1 | convolution fusion | flops 130023424 | bytes 1441792 | tf_op jit(solution)/shard_map/ftl,tlc->ftc/dot_general | solution.py:236
  103.5 1.3 reshape.127.x_ref
  104.8 27.4 %shard_map.161 = f32[128,20,128]{2,1,0:T(8,128)} custom-call(f32[128,20,128]{2,1,0:T(8,128)} %reshape.127.x_ref), custom_call_target="tpu_custom_call" | custom-call | tf_op jit(solution)/shard_map/pallas_call | solution.py:158
  132.2 1.5 %reshape.128 = f32[512,5,128]{2,1,0:T(8,128)S(1)} reshape(f32[128,20,128]{2,1,0:T(8,128)} %shard_map.161) | data formatting | bytes 2621440 | tf_op jit(solution)/shard_map/reshape | solution.py:242
  (46 shorter events, 9.9 us)
Async XLA Ops:
  0.6 29.8 %copy-start.4 = (f32[4,8192]{1,0:T(4,128)S(1)}, f32[4,8192]{1,0:T(4,128)}, u32[]{:S(2)}) copy-start(f32[4,8192]{1,0:T(4,128)} %param.17) | copy-start | bytes 393220
  0.6 30.0 %copy-start.6 = (f32[8192]{0:T(1024)S(1)}, f32[8192]{0:T(1024)}, u32[]{:S(2)}) copy-start(f32[8192]{0:T(1024)} %param.16) | copy-start | bytes 98308
  57.6 6.4 %copy-start.1 = (f32[4,8192]{1,0:T(4,128)S(1)}, f32[4,8192]{1,0:T(4,128)}, u32[]{:S(2)}) copy-start(f32[4,8192]{1,0:T(4,128)} %param.26) | copy-start | bytes 393220
  57.6 7.4 %copy-start.2 = (bf16[72,72]{1,0:T(8,128)(2,1)S(1)}, bf16[72,72]{1,0:T(8,128)(2,1)}, u32[]{:S(2)}) copy-start(bf16[72,72]{1,0:T(8,128)(2,1)} %param.15) | copy-start | bytes 31108
  87.6 1.5 %copy-start = (s32[256,128]{1,0:T(8,128)S(1)}, s32[256,128]{1,0:T(8,128)}, u32[]{:S(2)}) copy-start(s32[256,128]{1,0:T(8,128)} %add_select_fusion.lanes_ref) | copy-start | bytes 393220
  132.2 2.2 %copy-start.3 = (f32[8192]{0:T(1024)S(1)}, f32[8192]{0:T(1024)}, u32[]{:S(2)}) copy-start(f32[8192]{0:T(1024)} %param.19) | copy-start | bytes 98308
  132.2 2.3 %copy-start.5 = (f32[4,8192]{1,0:T(4,128)S(1)}, f32[4,8192]{1,0:T(4,128)}, u32[]{:S(2)}) copy-start(f32[4,8192]{1,0:T(4,128)} %param.20) | copy-start | bytes 393220

commit v3 on v1

--- a/solution.py
+++ b/solution.py
@@ -72,13 +72,27 @@
     )(win, lanes)
 
 
-def ocean_kernel(m_ref, m0_ref, x_ref, forcing_ref, sea_ref, out_ref, top_ref):
-    m = m_ref[...]
+def split_bf16(values):
+    upper = values.astype(jnp.bfloat16)
+    return upper, (values - upper.astype(jnp.float32)).astype(jnp.bfloat16)
+
+
+def split_kept(values):
+    upper = lax.reduce_precision(values, exponent_bits=8, mantissa_bits=7)
+    return upper.astype(jnp.bfloat16), (values - upper).astype(jnp.bfloat16)
+
+
+def ocean_kernel(m_hi_ref, m_lo_ref, m0_ref, x_ref, forcing_ref, sea_ref, out_ref, top_ref):
+    m_hi = m_hi_ref[...]
+    m_lo = m_lo_ref[...]
     m0 = m0_ref[...]
     sea = sea_ref[...] == 1
     for field in range(x_ref.shape[1]):
         x = x_ref[:, field, :]
-        mixed = jnp.dot(m, x, precision=highest, preferred_element_type=jnp.float32)
+        x_hi, x_lo = split_bf16(x)
+        mixed = jnp.dot(m_hi, x_hi, preferred_element_type=jnp.float32)
+        mixed = mixed + jnp.dot(m_hi, x_lo, preferred_element_type=jnp.float32)
+        mixed = mixed + jnp.dot(m_lo, x_hi, preferred_element_type=jnp.float32)
         mixed = mixed + m0 * forcing_ref[field : field + 1, :]
         updated = jnp.where(sea, mixed, x)
         out_ref[:, field, :] = updated
@@ -95,6 +109,7 @@
             jax.ShapeDtypeStruct((fields, cells), jnp.float32),
         ),
         in_specs=[
+            pl.BlockSpec((levels, levels), lambda i: (0, 0)),
             pl.BlockSpec((levels, levels), lambda i: (0, 0)),
             pl.BlockSpec((levels, 1), lambda i: (0, 0)),
             pl.BlockSpec((levels, fields, block), lambda i: (0, 0, i)),
@@ -105,7 +120,7 @@
             pl.BlockSpec((levels, fields, block), lambda i: (0, 0, i)),
             pl.BlockSpec((fields, block), lambda i: (0, i)),
         ),
-    )(ocean_mixing, ocean_mixing[:, 0:1], state_by_level, forcing, sea_mask.reshape(1, cells))
+    )(*split_kept(ocean_mixing), ocean_mixing[:, 0:1], state_by_level, forcing, sea_mask.reshape(1, cells))
 
 
 def per_device(
@@ -177,11 +192,11 @@
     sea_share = atmos_weight * sea_mask.astype(jnp.float32)[None, :]
     outgoing = jnp.concatenate([sea_share[None] * top[:, None, :], sea_share[None]], axis=0)
     lane_hot = (lanes[:, :, None] == jnp.arange(width, dtype=jnp.int32)[None, None, :]).astype(
-        jnp.float32
-    )
-    partial = jnp.einsum(
-        "ftl,tlc->ftc", outgoing.reshape(5, tile_count, width), lane_hot, precision=high
-    )
+        jnp.bfloat16
+    )
+    pieces = jnp.concatenate(split_kept(outgoing.reshape(5, tile_count, width)), axis=0)
+    partial = jnp.einsum("ftl,tlc->ftc", pieces, lane_hot, preferred_element_type=jnp.float32)
+    partial = partial[:5] + partial[5:]
     send_buffer = jnp.einsum("qt,ftc->fqc", placement, partial, precision=highest)
     returned = lax.all_to_all(
         send_buffer.reshape(5, devices, capacity),

time: 130 us -> 149 us (1.15)
  Pallas kernels: 15.4 us -> 36.4 us
  matrix products: 26 us -> 23.8 us
    pallas_call x1, Pallas kernels: 13.1 us -> 34.1 us  [ocean_update(): pl.pallas_call(ocean_kernel, grid=(cells // block,), out_shape=(jax.Shape...]
    dot_general x1, matrix products: 12.6 us -> 10.4 us  [per_device(): jnp.einsum('ftl,tlc->ftc', pieces, lane_hot, preferred_element_type=jnp.f...]
  transfers between devices with their start and end apart: 3 -> 3, of which waited for: 3 -> 3; matrix products, arithmetic and copies ran while one was open for 14% -> 13% of each run, Pallas kernels for 0% -> 0%
where the time goes in v3:
time: 149 us
  waiting for transfers between devices  38.8 us (26%)
  Pallas kernels  36.4 us (24%)
  matrix products  23.8 us (16%)
  starting transfers between devices  22.4 us (15%)
  other arithmetic  13.1 us (9%)
  local copies, waits for them, and re-layouts  12.9 us (9%)
    pallas_call x1, Pallas kernels, ocean_update(): pl.pallas_call(ocean_kernel, grid=(cells // block,), out_shape=(jax.Shape...  34.1 us
    all_to_all x1, waiting for transfers between devices, per_device(): lax.all_to_all(send_buffer.reshape(5, devices, capacity), ('comp', 'sub')...  23.7 us
    all_to_all x1, starting transfers between devices, per_device(): lax.all_to_all(request, ('comp', 'sub'), split_axis=0, concat_axis=0, til...  11.5 us
    all_to_all x1, waiting for transfers between devices, per_device(): lax.all_to_all(served.reshape(4, devices, capacity), ('comp', 'sub'), spl...  11.3 us
    dot_general x1, matrix products, per_device(): jnp.einsum('ftl,tlc->ftc', pieces, lane_hot, preferred_element_type=jnp.f...  10.4 us
    dot_general x4, matrix products, diffuse_atmos(): jnp.dot(atmos_mixing, atmos_profiles[member], preferred_element_type=jnp....  9.16 us
    all_to_all x1, starting transfers between devices, per_device(): lax.all_to_all(served.reshape(4, devices, capacity), ('comp', 'sub'), spl...  5.88 us
    all_to_all x1, starting transfers between devices, per_device(): lax.all_to_all(send_buffer.reshape(5, devices, capacity), ('comp', 'sub')...  4.98 us
  transfers between devices with their start and end apart: 3, of which 3 were waited for; matrix products, arithmetic and copies ran while one was open for 13% of the time, Pallas kernels for 0%

profile of v3, /device:TPU:1, one launch (start us, length us, event | category | flops | bytes accessed | tf_op | source)
XLA Modules:
  0.0 148.5 jit_solution(5837190986790298272)
XLA Ops:
  0.6 1.0 reshape.123
  4.0 11.5 %all-to-all-start = ((s32[128,1,4]{2,1,0:T(1,128)}), s32[128,1,4]{2,1,0:T(1,128)S(1)}, u32[]{:S(2)}, u32[]{:S(2)}) async-start(s32[128,1,4]{2,1,0:T(1,128)} %bitcast.35), calls=%async_computation | async-start | bytes 131072 | tf_op jit(solution)/shard_map/all_to_all | solution.py:163
  16.3 1.2 fusion.55
  17.5 1.1 slice_convert_fusion
  18.7 1.4 fusion.50
  21.1 3.9 %all-to-all-done = s32[128,1,4]{2,1,0:T(1,128)S(1)} async-done(((s32[128,1,4]{2,1,0:T(1,128)}), s32[128,1,4]{2,1,0:T(1,128)S(1)}, u32[]{:S(2)}, u32[]{:S(2)}) %all-to-all-start) | async-done | bytes 2080 | tf_op jit(solution)/shard_map/all_to_all | solution.py:163
  27.6 1.6 %copy.29 = f32[4,128,512]{2,0,1:T(4,128)} copy(f32[4,128,512]{2,1,0:T(8,128)S(1)} %reshape.124) | data formatting | bytes 2097152 | tf_op jit(solution)/shard_map/reshape | solution.py:175
  29.3 5.9 %all-to-all-start.1 = ((f32[4,128,512]{2,0,1:T(4,128)}), f32[4,128,512]{2,0,1:T(4,128)S(1)}, u32[]{:S(2)}, u32[]{:S(2)}) async-start(f32[4,128,512]{2,0,1:T(4,128)} %copy.29), calls=%async_computation.1 | async-start | bytes 2097152 | tf_op jit(solution)/shard_map/all_to_all | solution.py:174
  35.8 2.8 %fusion.5 = bf16[1,72,8192]{2,1,0:T(8,128)(2,1)} fusion(bf16[72,72]{1,0:T(8,128)(2,1)S(1)} %copy-done.4, f32[8192]{0:T(1024)S(1)} %bitcast.115, bf16[4,72,8192]{2,1,0:T(8,128)(2,1)} %param.14, f32[72]{0:T(128)S(1)} %convert_reduce_fusion), kind=kOutput, calls=%fused_computation.10 | convolution fusion | flops 86704128 | bytes 2402720 | tf_op jit(solution)/shard_map/dot_general | solution.py:40
  38.6 2.8 %fusion.8 = bf16[1,72,8192]{2,1,0:T(8,128)(2,1)} fusion(bf16[72,72]{1,0:T(8,128)(2,1)S(1)} %copy-done.4, f32[8192]{0:T(1024)S(1)} %bitcast.114, f32[72]{0:T(128)S(1)} %convert_reduce_fusion, bf16[4,72,8192]{2,1,0:T(8,128)(2,1)} %param.14), kind=kOutput, calls=%fused_computation.13 | convolution fusion | flops 86704128 | bytes 2402720 | tf_op jit(solution)/shard_map/dot_general | solution.py:40
  42.7 11.3 %all-to-all-done.1 = f32[4,128,512]{2,0,1:T(4,128)S(1)} async-done(((f32[4,128,512]{2,0,1:T(4,128)}), f32[4,128,512]{2,0,1:T(4,128)S(1)}, u32[]{:S(2)}, u32[]{:S(2)}) %all-to-all-start.1) | async-done | bytes 1048608 | tf_op jit(solution)/shard_map/all_to_all | solution.py:174
  54.3 1.5 %convolution_bitcast_fusion.2.win_ref = f32[4,256,128]{2,1,0:T(8,128)} fusion(f32[4,512,128]{2,1,0:T(8,128)S(1)} %reshape.125, s32[256]{0:T(256)S(1)} %and_select_fusion.1), kind=kOutput, calls=%fused_computation.21 | convolution fusion | flops 805437440 | bytes 1573888 | tf_op jit(solution)/shard_map/qt,fql->ftl/dot_general | solution.py:182
  55.9 2.3 %shard_map.157 = f32[4,256,128]{2,1,0:T(8,128)} custom-call(f32[4,256,128]{2,1,0:T(8,128)} %convolution_bitcast_fusion.2.win_ref, s32[256,128]{1,0:T(8,128)} %add_select_fusion.lanes_ref), custom_call_target="tpu_custom_call" | custom-call | tf_op jit(solution)/shard_map/pallas_call | solution.py:67
  58.2 1.2 reshape.126
  60.5 34.1 %shard_map.158 = (f32[60,4,8192]{2,1,0:T(4,128)}, f32[4,8192]{1,0:T(4,128)}) custom-call(bf16[60,60]{1,0:T(8,128)(2,1)} %get-tuple-element.31.m_hi_ref, bf16[60,60]{1,0:T(8,128)(2,1)} %get-tuple-element.30.m_lo_ref, f32[60,1]{1,0:T(8,128)} %bitcast.110, f32[60,4,8192]{2,1,0:T(4,128)} %bitcast.103, f32[4,8192]{1,0:T(4,128)} %broadcast_divide_fusion.forcing_ref, ...), custom_call_target="tpu_custom_call" | custom-call | tf_op jit(solution)/shard_map/pallas_call | solution.py:104
  94.5 1.0 mul.159
  96.7 10.4 %fusion.10 = f32[10,256,128]{2,0,1:T(8,128)S(1)} fusion(s32[256,128]{1,0:T(8,128)S(1)} %copy-done.2, bf16[5,256,128]{2,0,1:T(8,128)(2,1)S(1)} %get-tuple-element.12, bf16[5,256,128]{2,0,1:T(8,128)(2,1)S(1)} %get-tuple-element.11), kind=kOutput, calls=%fused_computation.16 | convolution fusion | flops 89391104 | bytes 2097152 | tf_op jit(solution)/shard_map/ftl,tlc->ftc/dot_general | solution.py:198
  107.2 1.2 convolution_bitcast_fusion
  109.0 2.2 %copy.36 = f32[5,128,512]{2,0,1:T(8,128)} copy(f32[5,128,512]{2,1,0:T(8,128)S(1)} %reshape.128) | data formatting | bytes 2621440 | tf_op jit(solution)/shard_map/reshape | solution.py:202
  111.2 5.0 %all-to-all-start.2 = ((f32[5,128,512]{2,0,1:T(8,128)}), f32[5,128,512]{2,0,1:T(8,128)S(1)}, u32[]{:S(2)}, u32[]{:S(2)}) async-start(f32[5,128,512]{2,0,1:T(8,128)} %copy.36), calls=%async_computation.2 | async-start | bytes 4194304 | tf_op jit(solution)/shard_map/all_to_all | solution.py:201
  116.2 1.9 %fusion.6 = bf16[1,72,8192]{2,1,0:T(8,128)(2,1)S(1)} fusion(bf16[72,72]{1,0:T(8,128)(2,1)S(1)} %copy-done.4, f32[8192]{0:T(1024)S(1)} %bitcast.113, bf16[4,72,8192]{2,1,0:T(8,128)(2,1)} %param.14, f32[72]{0:T(128)S(1)} %convert_reduce_fusion), kind=kOutput, calls=%fused_computation.11 | convolution fusion | flops 86704128 | bytes 2402720 | tf_op jit(solution)/shard_map/dot_general | solution.py:40
  118.1 1.7 %fusion.7 = bf16[1,72,8192]{2,1,0:T(8,128)(2,1)S(1)} fusion(bf16[72,72]{1,0:T(8,128)(2,1)S(1)} %copy-done.4, f32[8192]{0:T(1024)S(1)} %bitcast.112, bf16[4,72,8192]{2,1,0:T(8,128)(2,1)} %param.14, f32[72]{0:T(128)S(1)} %convert_reduce_fusion), kind=kOutput, calls=%fused_computation.12 | convolution fusion | flops 86704128 | bytes 2402720 | tf_op jit(solution)/shard_map/dot_general | solution.py:40
  119.9 2.5 %pad_maximum_fusion = bf16[4,72,8192]{2,1,0:T(8,128)(2,1)} fusion(bf16[1,72,8192]{2,1,0:T(8,128)(2,1)S(1)} %copy-done, bf16[1,72,8192]{2,1,0:T(8,128)(2,1)S(1)} %fusion.6, bf16[1,72,8192]{2,1,0:T(8,128)(2,1)S(1)} %fusion.7, bf16[1,72,8192]{2,1,0:T(8,128)(2,1)S(1)} %copy-done.1), kind=kLoop, calls=%fused_computation.15 | loop fusion | flops 7077888 | bytes 9437184 | tf_op jit(solution)/shard_map/stack | solution.py:44
  122.4 23.7 %all-to-all-done.2 = f32[5,128,512]{2,0,1:T(8,128)S(1)} async-done(((f32[5,128,512]{2,0,1:T(8,128)}), f32[5,128,512]{2,0,1:T(8,128)S(1)}, u32[]{:S(2)}, u32[]{:S(2)}) %all-to-all-start.2) | async-done | bytes 1310752 | tf_op jit(solution)/shard_map/all_to_all | solution.py:201
  (61 shorter events, 14.2 us)
Async XLA Ops:
  0.6 20.3 %copy-start.8 = (f32[4,8192]{1,0:T(4,128)S(1)}, f32[4,8192]{1,0:T(4,128)}, u32[]{:S(2)}) copy-start(f32[4,8192]{1,0:T(4,128)} %param.27) | copy-start | bytes 393220
  4.0 21.0 %all-to-all-start = ((s32[128,1,4]{2,1,0:T(1,128)}), s32[128,1,4]{2,1,0:T(1,128)S(1)}, u32[]{:S(2)}, u32[]{:S(2)}) async-start(s32[128,1,4]{2,1,0:T(1,128)} %bitcast.35), calls=%async_computation | async-start | bytes 131072 | tf_op jit(solution)/shard_map/all_to_all | solution.py:163
  27.6 7.9 %copy-start.3 = (f32[4,8192]{1,0:T(4,128)S(1)}, f32[4,8192]{1,0:T(4,128)}, u32[]{:S(2)}) copy-start(f32[4,8192]{1,0:T(4,128)} %param.26) | copy-start | bytes 393220
  27.6 8.0 %copy-start.4 = (bf16[72,72]{1,0:T(8,128)(2,1)S(1)}, bf16[72,72]{1,0:T(8,128)(2,1)}, u32[]{:S(2)}) copy-start(bf16[72,72]{1,0:T(8,128)(2,1)} %param.15) | copy-start | bytes 31108
  29.3 24.7 %all-to-all-start.1 = ((f32[4,128,512]{2,0,1:T(4,128)}), f32[4,128,512]{2,0,1:T(4,128)S(1)}, u32[]{:S(2)}, u32[]{:S(2)}) async-start(f32[4,128,512]{2,0,1:T(4,128)} %copy.29), calls=%async_computation.1 | async-start | bytes 2097152 | tf_op jit(solution)/shard_map/all_to_all | solution.py:174
  35.8 5.5 %copy-start.5 = (f32[60,60]{1,0:T(8,128)S(1)}, f32[60,60]{1,0:T(8,128)}, u32[]{:S(2)}) copy-start(f32[60,60]{1,0:T(8,128)} %param.22) | copy-start | bytes 43204
  94.5 2.1 %copy-start.2 = (s32[256,128]{1,0:T(8,128)S(1)}, s32[256,128]{1,0:T(8,128)}, u32[]{:S(2)}) copy-start(s32[256,128]{1,0:T(8,128)} %add_select_fusion.lanes_ref) | copy-start | bytes 393220
  111.2 34.8 %all-to-all-start.2 = ((f32[5,128,512]{2,0,1:T(8,128)}), f32[5,128,512]{2,0,1:T(8,128)S(1)}, u32[]{:S(2)}, u32[]{:S(2)}) async-start(f32[5,128,512]{2,0,1:T(8,128)} %copy.36), calls=%async_computation.2 | async-start | bytes 4194304 | tf_op jit(solution)/shard_map/all_to_all | solution.py:201
  116.2 3.7 %copy-start = (bf16[1,72,8192]{2,1,0:T(8,128)(2,1)S(1)}, bf16[1,72,8192]{2,1,0:T(8,128)(2,1)}, u32[]{:S(2)}) copy-start(bf16[1,72,8192]{2,1,0:T(8,128)(2,1)} %fusion.5) | copy-start | bytes 3538948
  116.2 3.7 %copy-start.1 = (bf16[1,72,8192]{2,1,0:T(8,128)(2,1)S(1)}, bf16[1,72,8192]{2,1,0:T(8,128)(2,1)}, u32[]{:S(2)}) copy-start(bf16[1,72,8192]{2,1,0:T(8,128)(2,1)} %fusion.8) | copy-start | bytes 3538948
  146.8 0.8 copy-start.6
  146.8 0.9 copy-start.7

commit v4 on v1

--- a/solution.py
+++ b/solution.py
@@ -72,7 +72,12 @@
     )(win, lanes)
 
 
-def ocean_kernel(m_ref, m0_ref, x_ref, forcing_ref, sea_ref, out_ref, top_ref):
+def split_kept(values):
+    upper = lax.reduce_precision(values, exponent_bits=8, mantissa_bits=7)
+    return upper.astype(jnp.bfloat16), (values - upper).astype(jnp.bfloat16)
+
+
+def ocean_kernel(m_ref, m0_ref, x_ref, forcing_ref, sea_ref, out_ref):
     m = m_ref[...]
     m0 = m0_ref[...]
     sea = sea_ref[...] == 1
@@ -80,9 +85,7 @@
         x = x_ref[:, field, :]
         mixed = jnp.dot(m, x, precision=highest, preferred_element_type=jnp.float32)
         mixed = mixed + m0 * forcing_ref[field : field + 1, :]
-        updated = jnp.where(sea, mixed, x)
-        out_ref[:, field, :] = updated
-        top_ref[field : field + 1, :] = updated[0:1, :]
+        out_ref[:, field, :] = jnp.where(sea, mixed, x)
 
 
 def ocean_update(ocean_mixing, state_by_level, forcing, sea_mask, block=1024):
@@ -90,10 +93,7 @@
     return pl.pallas_call(
         ocean_kernel,
         grid=(cells // block,),
-        out_shape=(
-            jax.ShapeDtypeStruct(state_by_level.shape, jnp.float32),
-            jax.ShapeDtypeStruct((fields, cells), jnp.float32),
-        ),
+        out_shape=jax.ShapeDtypeStruct(state_by_level.shape, jnp.float32),
         in_specs=[
             pl.BlockSpec((levels, levels), lambda i: (0, 0)),
             pl.BlockSpec((levels, 1), lambda i: (0, 0)),
@@ -101,9 +101,11 @@
             pl.BlockSpec((fields, block), lambda i: (0, i)),
             pl.BlockSpec((1, block), lambda i: (0, i)),
         ],
-        out_specs=(
-            pl.BlockSpec((levels, fields, block), lambda i: (0, 0, i)),
-            pl.BlockSpec((fields, block), lambda i: (0, i)),
+        out_specs=pl.BlockSpec((levels, fields, block), lambda i: (0, 0, i)),
+        cost_estimate=pl.CostEstimate(
+            flops=12 * levels * levels * fields * cells,
+            bytes_accessed=8 * levels * fields * cells,
+            transcendentals=0,
         ),
     )(ocean_mixing, ocean_mixing[:, 0:1], state_by_level, forcing, sea_mask.reshape(1, cells))
 
@@ -143,6 +145,9 @@
     window_of_tile = tiles_pc[:, 0] // width
     lanes = tiles_pc % width
 
+    state_by_level = jnp.transpose(ocean_state, (1, 0, 2))
+    base_top = jnp.einsum("m,mfc->fc", ocean_mixing[0], state_by_level, precision=highest)
+
     request = jnp.dot(placement, window_of_tile.astype(jnp.float32), precision=highest)
     request = (request + 0.5).astype(jnp.int32).reshape(devices, slot_tiles // devices)
     asked = lax.all_to_all(request, ("comp", "sub"), split_axis=0, concat_axis=0, tiled=True)
@@ -170,18 +175,16 @@
     at_cells = lane_gather(win_local, lanes).reshape(4, intersections, ocean_cells)
     forcing = jnp.sum(ocean_weight[None] * at_cells, axis=1) / jnp.sum(ocean_weight, axis=0)[None]
 
-    state_by_level = jnp.transpose(ocean_state, (1, 0, 2))
-    updated_by_level, top = ocean_update(ocean_mixing, state_by_level, forcing, sea_mask)
-    ocean_updated = jnp.transpose(updated_by_level, (1, 0, 2))
-
+    sea = sea_mask[None, :] == 1
+    top = jnp.where(sea, base_top + ocean_mixing[0, 0] * forcing, state_by_level[0])
     sea_share = atmos_weight * sea_mask.astype(jnp.float32)[None, :]
     outgoing = jnp.concatenate([sea_share[None] * top[:, None, :], sea_share[None]], axis=0)
     lane_hot = (lanes[:, :, None] == jnp.arange(width, dtype=jnp.int32)[None, None, :]).astype(
-        jnp.float32
-    )
-    partial = jnp.einsum(
-        "ftl,tlc->ftc", outgoing.reshape(5, tile_count, width), lane_hot, precision=high
-    )
+        jnp.bfloat16
+    )
+    pieces = jnp.concatenate(split_kept(outgoing.reshape(5, tile_count, width)), axis=0)
+    partial = jnp.einsum("ftl,tlc->ftc", pieces, lane_hot, preferred_element_type=jnp.float32)
+    partial = partial[:5] + partial[5:]
     send_buffer = jnp.einsum("qt,ftc->fqc", placement, partial, precision=highest)
     returned = lax.all_to_all(
         send_buffer.reshape(5, devices, capacity),
@@ -193,6 +196,8 @@
     summed = jnp.einsum(
         "qw,fqc->fwc", window_hot, returned.reshape(5, slot_tiles, width), precision=highest
     ).reshape(5, columns)
+    updated_by_level = ocean_update(ocean_mixing, state_by_level, forcing, sea_mask)
+    ocean_updated = jnp.transpose(updated_by_level, (1, 0, 2))
     surface_state = (summed[:4] + land_weight[None] * land_surface) / (summed[4] + land_weight)[
         None
     ]

time: 130 us -> 126 us (0.969)
  waiting for transfers between devices: 39.5 us -> 15.5 us
  matrix products: 26 us -> 36.9 us
  starting transfers between devices: 22.1 us -> 27.7 us
  other arithmetic: 12.1 us -> 14.9 us
    all_to_all x1, waiting for transfers between devices: 23.7 us -> 12.2 us  [per_device(): lax.all_to_all(send_buffer.reshape(5, devices, capacity), ('comp', 'sub')...]
    dot_general x1 -> x2, matrix products: 12.6 us -> 22.4 us  [the longest x1 12 us: per_device(): jnp.einsum('m,mfc->fc', ocean_mixing[0], state_by_level, precision=highest)]
    all_to_all x1, waiting for transfers between devices: 11.9 us -> 3.31 us  [per_device(): lax.all_to_all(served.reshape(4, devices, capacity), ('comp', 'sub'), spl...]
    all_to_all x1, waiting for transfers between devices: 3.9 us -> 0.01 us  [per_device(): lax.all_to_all(request, ('comp', 'sub'), split_axis=0, concat_axis=0, til...]
    all_to_all x1, starting transfers between devices: 5.88 us -> 9.76 us  [per_device(): lax.all_to_all(served.reshape(4, devices, capacity), ('comp', 'sub'), spl...]
    select_n x0 -> x1, other arithmetic: none -> 2.33 us  [per_device(): jnp.where(sea, base_top + ocean_mixing[0, 0] * forcing, state_by_level[0])]
    all_to_all x1, starting transfers between devices: 4.76 us -> 6.47 us  [per_device(): lax.all_to_all(send_buffer.reshape(5, devices, capacity), ('comp', 'sub')...]
  transfers between devices with their start and end apart: 3 -> 3, of which waited for: 3 -> 2; matrix products, arithmetic and copies ran while one was open for 14% -> 27% of each run, Pallas kernels for 0% -> 11%
where the time goes in v4:
time: 126 us; the launch traced here: 125 us
  matrix products  36.9 us (29%)
  starting transfers between devices  27.7 us (22%)
  waiting for transfers between devices  15.5 us (12%)
  Pallas kernels  15.4 us (12%)
  other arithmetic  14.9 us (12%)
  local copies, waits for them, and re-layouts  13.3 us (11%)
    pallas_call x1, Pallas kernels, ocean_update(): pl.pallas_call(ocean_kernel, grid=(cells // block,), out_shape=jax.ShapeD...  13.1 us
    all_to_all x1, waiting for transfers between devices, per_device(): lax.all_to_all(send_buffer.reshape(5, devices, capacity), ('comp', 'sub')...  12.2 us
    dot_general x1, matrix products, per_device(): jnp.einsum('m,mfc->fc', ocean_mixing[0], state_by_level, precision=highest)  12 us
    all_to_all x1, starting transfers between devices, per_device(): lax.all_to_all(request, ('comp', 'sub'), split_axis=0, concat_axis=0, til...  11.5 us
    dot_general x1, matrix products, per_device(): jnp.einsum('ftl,tlc->ftc', pieces, lane_hot, preferred_element_type=jnp.f...  10.4 us
    dot_general x4, matrix products, diffuse_atmos(): jnp.dot(atmos_mixing, atmos_profiles[member], preferred_element_type=jnp....  10.2 us
    all_to_all x1, starting transfers between devices, per_device(): lax.all_to_all(served.reshape(4, devices, capacity), ('comp', 'sub'), spl...  9.76 us
    all_to_all x1, starting transfers between devices, per_device(): lax.all_to_all(send_buffer.reshape(5, devices, capacity), ('comp', 'sub')...  6.47 us
  transfers between devices with their start and end apart: 3, of which 2 were waited for; matrix products, arithmetic and copies ran while one was open for 27% of the time, Pallas kernels for 11%

profile of v4, /device:TPU:1, one launch (start us, length us, event | category | flops | bytes accessed | tf_op | source)
XLA Modules:
  0.0 124.6 jit_solution(13256697520618642618)
XLA Ops:
  4.0 11.5 %all-to-all-start = ((s32[128,1,4]{2,1,0:T(1,128)}), s32[128,1,4]{2,1,0:T(1,128)S(1)}, u32[]{:S(2)}, u32[]{:S(2)}) async-start(s32[128,1,4]{2,1,0:T(1,128)} %bitcast.35), calls=%async_computation | async-start | bytes 131072 | tf_op jit(solution)/shard_map/all_to_all | solution.py:153
  17.2 1.2 %fusion.59 = (f32[1,8192]{1,0:T(1,128)S(1)}, f32[1,8192]{1,0:T(1,128)S(1)}, f32[1,8192]{1,0:T(1,128)S(1)}) fusion(f32[4,8192]{1,0:T(4,128)} %param.18), kind=kLoop, calls=%fused_computation.110 | loop fusion | flops 8192 | bytes 229376 | tf_op jit(solution)/shard_map/slice | solution.py:29
  18.4 1.1 slice_convert_fusion
  19.6 1.4 %fusion.52 = (f32[1,8192]{1,0:T(1,128)S(1)}, f32[1,8192]{1,0:T(1,128)S(1)}, f32[1,8192]{1,0:T(1,128)S(1)}, f32[1,8192]{1,0:T(1,128)S(1)}) fusion(f32[4,1,8192]{2,1,0:T(1,128)S(1)} %slice_convert_fusion, f32[4,8192]{1,0:T(4,128)} %param.17), kind=kLoop, calls=%fused_computation.85 | loop fusion | flops 32768 | bytes 393216 | tf_op jit(solution)/shard_map/sub | solution.py:15
  22.2 2.8 %fusion.5 = bf16[1,72,8192]{2,1,0:T(8,128)(2,1)} fusion(bf16[72,72]{1,0:T(8,128)(2,1)S(1)} %copy-done.5, f32[8192]{0:T(1024)S(1)} %bitcast.132, bf16[4,72,8192]{2,1,0:T(8,128)(2,1)} %param.14, f32[72]{0:T(128)S(1)} %convert_reduce_fusion), kind=kOutput, calls=%fused_computation.10 | convolution fusion | flops 86704128 | bytes 2402720 | tf_op jit(solution)/shard_map/dot_general | solution.py:40
  24.9 2.8 %fusion.8 = bf16[1,72,8192]{2,1,0:T(8,128)(2,1)} fusion(bf16[72,72]{1,0:T(8,128)(2,1)S(1)} %copy-done.5, f32[8192]{0:T(1024)S(1)} %bitcast.131, f32[72]{0:T(128)S(1)} %convert_reduce_fusion, bf16[4,72,8192]{2,1,0:T(8,128)(2,1)} %param.14), kind=kOutput, calls=%fused_computation.13 | convolution fusion | flops 86704128 | bytes 2402720 | tf_op jit(solution)/shard_map/dot_general | solution.py:40
  28.0 1.2 slice.142
  31.9 1.6 %copy.29 = f32[4,128,512]{2,0,1:T(4,128)} copy(f32[4,128,512]{2,1,0:T(8,128)S(1)} %reshape.126) | data formatting | bytes 2097152 | tf_op jit(solution)/shard_map/reshape | solution.py:165
  33.5 9.8 %all-to-all-start.1 = ((f32[4,128,512]{2,0,1:T(4,128)}), f32[4,128,512]{2,0,1:T(4,128)S(1)}, u32[]{:S(2)}, u32[]{:S(2)}) async-start(f32[4,128,512]{2,0,1:T(4,128)} %copy.29), calls=%async_computation.1 | async-start | bytes 2097152 | tf_op jit(solution)/shard_map/all_to_all | solution.py:164
  43.3 2.8 %fusion.6 = bf16[1,72,8192]{2,1,0:T(8,128)(2,1)} fusion(bf16[72,72]{1,0:T(8,128)(2,1)S(1)} %copy-done.5, f32[8192]{0:T(1024)S(1)} %bitcast.130, bf16[4,72,8192]{2,1,0:T(8,128)(2,1)} %param.14, f32[72]{0:T(128)S(1)} %convert_reduce_fusion), kind=kOutput, calls=%fused_computation.11 | convolution fusion | flops 86704128 | bytes 2402720 | tf_op jit(solution)/shard_map/dot_general | solution.py:40
  46.8 12.0 %fusion.9 = f32[1,4,8192]{2,0,1:T(1,128)S(1)} fusion(f32[60,4,8192]{2,1,0:T(4,128)} %bitcast.117, f32[60,60]{1,0:T(8,128)} %m_ref.1), kind=kOutput, calls=%fused_computation.14 | convolution fusion | flops 23592960 | bytes 7995904 | tf_op jit(solution)/shard_map/m,mfc->fc/dot_general | solution.py:149
  58.8 3.3 %all-to-all-done.1 = f32[4,128,512]{2,0,1:T(4,128)S(1)} async-done(((f32[4,128,512]{2,0,1:T(4,128)}), f32[4,128,512]{2,0,1:T(4,128)S(1)}, u32[]{:S(2)}, u32[]{:S(2)}) %all-to-all-start.1) | async-done | bytes 1048608 | tf_op jit(solution)/shard_map/all_to_all | solution.py:164
  62.5 1.5 %convolution_bitcast_fusion.2.win_ref = f32[4,256,128]{2,1,0:T(8,128)} fusion(f32[4,512,128]{2,1,0:T(8,128)S(1)} %reshape.127, s32[256]{0:T(256)S(1)} %and_select_fusion.1), kind=kOutput, calls=%fused_computation.23 | convolution fusion | flops 805437440 | bytes 1573888 | tf_op jit(solution)/shard_map/qt,fql->ftl/dot_general | solution.py:172
  64.0 2.3 %shard_map.157 = f32[4,256,128]{2,1,0:T(8,128)} custom-call(f32[4,256,128]{2,1,0:T(8,128)} %convolution_bitcast_fusion.2.win_ref, s32[256,128]{1,0:T(8,128)} %add_select_fusion.lanes_ref), custom_call_target="tpu_custom_call" | custom-call | tf_op jit(solution)/shard_map/pallas_call | solution.py:67
  66.3 1.2 %reshape.128 = f32[4,4,8192]{2,1,0:T(4,128)S(1)} reshape(f32[4,256,128]{2,1,0:T(8,128)} %shard_map.157) | data formatting | bytes 1048576 | tf_op jit(solution)/shard_map/reshape | solution.py:175
  67.9 2.3 %fusion.35 = (f32[4,8192]{1,0:T(4,128)S(1)}, f32[4,8192]{1,0:T(4,128)}) fusion(f32[60,4,8192]{2,1,0:T(4,128)} %bitcast.118, f32[1,4,8192]{2,0,1:T(1,128)S(1)} %fusion.9, f32[]{:T(128)} %bitcast.45, pred[8192]{0:T(1024)(128)(4,1)S(1)} %broadcast_compare_fusion, f32[4,8192]{1,0:T(4,128)S(1)} %multiply_reduce_fusion, f32[8192]{0:T(1024)S(1)} %reduce_sum.19), kind=kLoop, calls=%fused_computation.56 | loop fusion | flops 131072 | bytes 696324 | tf_op jit(solution)/shard_map/jit(_where)/select_n | solution.py:179
  71.5 10.4 %fusion.12 = f32[10,256,128]{2,0,1:T(8,128)S(1)} fusion(s32[256,128]{1,0:T(8,128)S(1)} %copy-done.3, bf16[5,256,128]{2,0,1:T(8,128)(2,1)S(1)} %get-tuple-element.10, bf16[5,256,128]{2,0,1:T(8,128)(2,1)S(1)} %get-tuple-element.9), kind=kOutput, calls=%fused_computation.18 | convolution fusion | flops 89391104 | bytes 2097152 | tf_op jit(solution)/shard_map/ftl,tlc->ftc/dot_general | solution.py:186
  82.0 1.2 convolution_bitcast_fusion
  83.8 2.2 %copy.36 = f32[5,128,512]{2,0,1:T(8,128)} copy(f32[5,128,512]{2,1,0:T(8,128)S(1)} %reshape.130) | data formatting | bytes 2621440 | tf_op jit(solution)/shard_map/reshape | solution.py:190
  86.0 6.5 %all-to-all-start.2 = ((f32[5,128,512]{2,0,1:T(8,128)}), f32[5,128,512]{2,0,1:T(8,128)S(1)}, u32[]{:S(2)}, u32[]{:S(2)}) async-start(f32[5,128,512]{2,0,1:T(8,128)} %copy.36), calls=%async_computation.2 | async-start | bytes 4194304 | tf_op jit(solution)/shard_map/all_to_all | solution.py:189
  92.5 1.9 %fusion.7 = bf16[1,72,8192]{2,1,0:T(8,128)(2,1)S(1)} fusion(bf16[72,72]{1,0:T(8,128)(2,1)S(1)} %copy-done.5, f32[8192]{0:T(1024)S(1)} %bitcast.129, bf16[4,72,8192]{2,1,0:T(8,128)(2,1)} %param.14, f32[72]{0:T(128)S(1)} %convert_reduce_fusion), kind=kOutput, calls=%fused_computation.12 | convolution fusion | flops 86704128 | bytes 2402720 | tf_op jit(solution)/shard_map/dot_general | solution.py:40
  94.4 2.5 %pad_maximum_fusion = bf16[4,72,8192]{2,1,0:T(8,128)(2,1)} fusion(bf16[1,72,8192]{2,1,0:T(8,128)(2,1)S(1)} %copy-done, bf16[1,72,8192]{2,1,0:T(8,128)(2,1)S(1)} %copy-done.2, bf16[1,72,8192]{2,1,0:T(8,128)(2,1)S(1)} %fusion.7, bf16[1,72,8192]{2,1,0:T(8,128)(2,1)S(1)} %copy-done.1), kind=kLoop, calls=%fused_computation.17 | loop fusion | flops 7077888 | bytes 9437184 | tf_op jit(solution)/shard_map/stack | solution.py:44
  96.9 13.1 %shard_map.158 = f32[60,4,8192]{2,1,0:T(4,128)} custom-call(f32[60,60]{1,0:T(8,128)} %m_ref.1, f32[60,1]{1,0:T(8,128)} %bitcast.128, f32[60,4,8192]{2,1,0:T(4,128)} %bitcast.119, f32[4,8192]{1,0:T(4,128)} %get-tuple-element.4.forcing_ref, s32[1,8192]{1,0:T(1,128)} %bitcast.122), custom_call_target="tpu_custom_call" | custom-call | flops 1415577600 | bytes 15728640 | tf_op jit(solution)/shard_map/pallas_call | solution.py:93
  110.0 12.2 %all-to-all-done.2 = f32[5,128,512]{2,0,1:T(8,128)S(1)} async-done(((f32[5,128,512]{2,0,1:T(8,128)}), f32[5,128,512]{2,0,1:T(8,128)S(1)}, u32[]{:S(2)}, u32[]{:S(2)}) %all-to-all-start.2) | async-done | bytes 1310752 | tf_op jit(solution)/shard_map/all_to_all | solution.py:189
  (65 shorter events, 14.8 us)
Async XLA Ops:
  0.6 21.5 %copy-start.5 = (bf16[72,72]{1,0:T(8,128)(2,1)S(1)}, bf16[72,72]{1,0:T(8,128)(2,1)}, u32[]{:S(2)}) copy-start(bf16[72,72]{1,0:T(8,128)(2,1)} %param.15) | copy-start | bytes 31108
  0.6 21.4 %copy-start.9 = (f32[4,8192]{1,0:T(4,128)S(1)}, f32[4,8192]{1,0:T(4,128)}, u32[]{:S(2)}) copy-start(f32[4,8192]{1,0:T(4,128)} %param.27) | copy-start | bytes 393220
  4.0 25.3 %all-to-all-start = ((s32[128,1,4]{2,1,0:T(1,128)}), s32[128,1,4]{2,1,0:T(1,128)S(1)}, u32[]{:S(2)}, u32[]{:S(2)}) async-start(s32[128,1,4]{2,1,0:T(1,128)} %bitcast.35), calls=%async_computation | async-start | bytes 131072 | tf_op jit(solution)/shard_map/all_to_all | solution.py:153
  22.1 7.1 %copy-start.4 = (f32[4,8192]{1,0:T(4,128)S(1)}, f32[4,8192]{1,0:T(4,128)}, u32[]{:S(2)}) copy-start(f32[4,8192]{1,0:T(4,128)} %param.26) | copy-start | bytes 393220
  33.5 12.5 %copy-start.6 = (s32[8192]{0:T(1024)S(1)}, s32[8192]{0:T(1024)}, u32[]{:S(2)}) copy-start(s32[8192]{0:T(1024)} %param.23) | copy-start | bytes 98308
  33.5 28.6 %all-to-all-start.1 = ((f32[4,128,512]{2,0,1:T(4,128)}), f32[4,128,512]{2,0,1:T(4,128)S(1)}, u32[]{:S(2)}, u32[]{:S(2)}) async-start(f32[4,128,512]{2,0,1:T(4,128)} %copy.29), calls=%async_computation.1 | async-start | bytes 2097152 | tf_op jit(solution)/shard_map/all_to_all | solution.py:164
  70.3 1.2 copy-start.3
  86.0 8.4 %copy-start = (bf16[1,72,8192]{2,1,0:T(8,128)(2,1)S(1)}, bf16[1,72,8192]{2,1,0:T(8,128)(2,1)}, u32[]{:S(2)}) copy-start(bf16[1,72,8192]{2,1,0:T(8,128)(2,1)} %fusion.5) | copy-start | bytes 3538948
  86.0 36.2 %all-to-all-start.2 = ((f32[5,128,512]{2,0,1:T(8,128)}), f32[5,128,512]{2,0,1:T(8,128)S(1)}, u32[]{:S(2)}, u32[]{:S(2)}) async-start(f32[5,128,512]{2,0,1:T(8,128)} %copy.36), calls=%async_computation.2 | async-start | bytes 4194304 | tf_op jit(solution)/shard_map/all_to_all | solution.py:189
  92.4 1.9 %copy-start.1 = (bf16[1,72,8192]{2,1,0:T(8,128)(2,1)S(1)}, bf16[1,72,8192]{2,1,0:T(8,128)(2,1)}, u32[]{:S(2)}) copy-start(bf16[1,72,8192]{2,1,0:T(8,128)(2,1)} %fusion.8) | copy-start | bytes 3538948
  92.5 2.0 %copy-start.2 = (bf16[1,72,8192]{2,1,0:T(8,128)(2,1)S(1)}, bf16[1,72,8192]{2,1,0:T(8,128)(2,1)}, u32[]{:S(2)}) copy-start(bf16[1,72,8192]{2,1,0:T(8,128)(2,1)} %fusion.6) | copy-start | bytes 3538948
  122.9 0.8 copy-start.7
  122.9 0.9 copy-start.8

commit v5 on v4

--- a/solution.py
+++ b/solution.py
@@ -108,6 +108,32 @@
             transcendentals=0,
         ),
     )(ocean_mixing, ocean_mixing[:, 0:1], state_by_level, forcing, sea_mask.reshape(1, cells))
+
+
+def top_level_kernel(row_ref, x_ref, out_ref):
+    total = row_ref[0] * x_ref[0]
+    for level in range(1, x_ref.shape[0]):
+        total = total + row_ref[level] * x_ref[level]
+    out_ref[...] = total
+
+
+def top_level_mix(first_row, state_by_level, block=2048):
+    levels, fields, cells = state_by_level.shape
+    return pl.pallas_call(
+        top_level_kernel,
+        grid=(cells // block,),
+        out_shape=jax.ShapeDtypeStruct((fields, cells), jnp.float32),
+        in_specs=[
+            pl.BlockSpec(memory_space=pltpu.SMEM),
+            pl.BlockSpec((levels, fields, block), lambda i: (0, 0, i)),
+        ],
+        out_specs=pl.BlockSpec((fields, block), lambda i: (0, i)),
+        cost_estimate=pl.CostEstimate(
+            flops=2 * levels * fields * cells,
+            bytes_accessed=4 * (levels + 1) * fields * cells,
+            transcendentals=0,
+        ),
+    )(first_row, state_by_level)
 
 
 def per_device(
@@ -146,7 +172,7 @@
     lanes = tiles_pc % width
 
     state_by_level = jnp.transpose(ocean_state, (1, 0, 2))
-    base_top = jnp.einsum("m,mfc->fc", ocean_mixing[0], state_by_level, precision=highest)
+    base_top = top_level_mix(ocean_mixing[0], state_by_level)
 
     request = jnp.dot(placement, window_of_tile.astype(jnp.float32), precision=highest)
     request = (request + 0.5).astype(jnp.int32).reshape(devices, slot_tiles // devices)

time: 126 us -> 124 us (0.984)
  matrix products: 36.9 us -> 24.9 us
  waiting for transfers between devices: 15.5 us -> 22.1 us
  Pallas kernels: 15.4 us -> 20.2 us
  starting transfers between devices: 27.7 us -> 26.2 us
    dot_general x1 -> x0, matrix products: 12 us -> none  [per_device(): jnp.einsum('m,mfc->fc', ocean_mixing[0], state_by_level, precision=highest)]
    all_to_all x1, waiting for transfers between devices: 3.31 us -> 9.79 us  [per_device(): lax.all_to_all(served.reshape(4, devices, capacity), ('comp', 'sub'), spl...]
    pallas_call x0 -> x1, Pallas kernels: none -> 4.83 us  [top_level_mix(): pl.pallas_call(top_level_kernel, grid=(cells // block,), out_shape=jax.Sh...]
    all_to_all x1, starting transfers between devices: 6.47 us -> 4.89 us  [per_device(): lax.all_to_all(send_buffer.reshape(5, devices, capacity), ('comp', 'sub')...]
  transfers between devices with their start and end apart: 3 -> 3, of which waited for: 2 -> 2; matrix products, arithmetic and copies ran while one was open for 27% -> 18% of each run, Pallas kernels for 11% -> 15%
where the time goes in v5:
time: 124 us; the launch traced here: 123 us
  starting transfers between devices  26.2 us (21%)
  matrix products  24.9 us (20%)
  waiting for transfers between devices  22.1 us (18%)
  Pallas kernels  20.2 us (16%)
  local copies, waits for them, and re-layouts  14.5 us (12%)
  other arithmetic  14.1 us (11%)
    pallas_call x1, Pallas kernels, ocean_update(): pl.pallas_call(ocean_kernel, grid=(cells // block,), out_shape=jax.ShapeD...  13.1 us
    all_to_all x1, waiting for transfers between devices, per_device(): lax.all_to_all(send_buffer.reshape(5, devices, capacity), ('comp', 'sub')...  12.3 us
    all_to_all x1, starting transfers between devices, per_device(): lax.all_to_all(request, ('comp', 'sub'), split_axis=0, concat_axis=0, til...  11.5 us
    dot_general x1, matrix products, per_device(): jnp.einsum('ftl,tlc->ftc', pieces, lane_hot, preferred_element_type=jnp.f...  10.4 us
    dot_general x4, matrix products, diffuse_atmos(): jnp.dot(atmos_mixing, atmos_profiles[member], preferred_element_type=jnp....  10.2 us
    all_to_all x1, waiting for transfers between devices, per_device(): lax.all_to_all(served.reshape(4, devices, capacity), ('comp', 'sub'), spl...  9.79 us
    all_to_all x1, starting transfers between devices, per_device(): lax.all_to_all(served.reshape(4, devices, capacity), ('comp', 'sub'), spl...  9.77 us
    all_to_all x1, starting transfers between devices, per_device(): lax.all_to_all(send_buffer.reshape(5, devices, capacity), ('comp', 'sub')...  4.89 us
  transfers between devices with their start and end apart: 3, of which 2 were waited for; matrix products, arithmetic and copies ran while one was open for 18% of the time, Pallas kernels for 15%

profile of v5, /device:TPU:1, one launch (start us, length us, event | category | flops | bytes accessed | tf_op | source)
XLA Modules:
  0.0 123.0 jit_solution(12926988302553963411)
XLA Ops:
  4.0 11.5 %all-to-all-start = ((s32[128,1,4]{2,1,0:T(1,128)}), s32[128,1,4]{2,1,0:T(1,128)S(1)}, u32[]{:S(2)}, u32[]{:S(2)}) async-start(s32[128,1,4]{2,1,0:T(1,128)} %bitcast.35), calls=%async_computation | async-start | bytes 131072 | tf_op jit(solution)/shard_map/all_to_all | solution.py:179
  15.5 1.2 slice_bitcast_fusion.7.row_ref
  17.5 1.2 %fusion.55 = (f32[1,8192]{1,0:T(1,128)S(1)}, f32[1,8192]{1,0:T(1,128)S(1)}, f32[1,8192]{1,0:T(1,128)S(1)}) fusion(f32[4,8192]{1,0:T(4,128)} %param.18), kind=kLoop, calls=%fused_computation.106 | loop fusion | flops 8192 | bytes 229376 | tf_op jit(solution)/shard_map/slice | solution.py:29
  19.9 1.4 %fusion.50 = (f32[1,8192]{1,0:T(1,128)S(1)}, f32[1,8192]{1,0:T(1,128)S(1)}, f32[1,8192]{1,0:T(1,128)S(1)}, f32[1,8192]{1,0:T(1,128)S(1)}) fusion(f32[4,1,8192]{2,1,0:T(1,128)S(1)} %slice_convert_fusion, f32[4,8192]{1,0:T(4,128)} %param.17), kind=kLoop, calls=%fused_computation.82 | loop fusion | flops 32768 | bytes 393216 | tf_op jit(solution)/shard_map/sub | solution.py:15
  22.6 1.3 %slice.142 = f32[1,1]{1,0:T(1,128)} slice(f32[60,60]{1,0:T(8,128)} %m_ref.1), slice={[0:1], [0:1]} | slice | bytes 8 | tf_op jit(solution)/shard_map/slice | solution.py:205
  24.3 4.8 %shard_map.159 = f32[4,8192]{1,0:T(4,128)} custom-call(f32[60]{0:T(128)} %slice_bitcast_fusion.7.row_ref, f32[60,4,8192]{2,1,0:T(4,128)} %bitcast.110), custom_call_target="tpu_custom_call" | custom-call | flops 3932160 | bytes 7995392 | tf_op jit(solution)/shard_map/pallas_call | solution.py:122
  31.7 1.6 %copy.29 = f32[4,128,512]{2,0,1:T(4,128)} copy(f32[4,128,512]{2,1,0:T(8,128)S(1)} %reshape.126) | data formatting | bytes 2097152 | tf_op jit(solution)/shard_map/reshape | solution.py:191
  33.3 9.8 %all-to-all-start.1 = ((f32[4,128,512]{2,0,1:T(4,128)}), f32[4,128,512]{2,0,1:T(4,128)S(1)}, u32[]{:S(2)}, u32[]{:S(2)}) async-start(f32[4,128,512]{2,0,1:T(4,128)} %copy.29), calls=%async_computation.1 | async-start | bytes 2097152 | tf_op jit(solution)/shard_map/all_to_all | solution.py:190
  43.1 2.8 %fusion.5 = bf16[1,72,8192]{2,1,0:T(8,128)(2,1)} fusion(bf16[72,72]{1,0:T(8,128)(2,1)S(1)} %copy-done.6, f32[8192]{0:T(1024)S(1)} %bitcast.125, bf16[4,72,8192]{2,1,0:T(8,128)(2,1)} %param.14, f32[72]{0:T(128)S(1)} %convert_reduce_fusion), kind=kOutput, calls=%fused_computation.10 | convolution fusion | flops 86704128 | bytes 2402720 | tf_op jit(solution)/shard_map/dot_general | solution.py:40
  45.9 2.8 %fusion.8 = bf16[1,72,8192]{2,1,0:T(8,128)(2,1)} fusion(bf16[72,72]{1,0:T(8,128)(2,1)S(1)} %copy-done.6, f32[8192]{0:T(1024)S(1)} %bitcast.124, f32[72]{0:T(128)S(1)} %convert_reduce_fusion, bf16[4,72,8192]{2,1,0:T(8,128)(2,1)} %param.14), kind=kOutput, calls=%fused_computation.13 | convolution fusion | flops 86704128 | bytes 2402720 | tf_op jit(solution)/shard_map/dot_general | solution.py:40
  48.6 2.8 %fusion.6 = bf16[1,72,8192]{2,1,0:T(8,128)(2,1)} fusion(bf16[72,72]{1,0:T(8,128)(2,1)S(1)} %copy-done.6, f32[8192]{0:T(1024)S(1)} %bitcast.123, bf16[4,72,8192]{2,1,0:T(8,128)(2,1)} %param.14, f32[72]{0:T(128)S(1)} %convert_reduce_fusion), kind=kOutput, calls=%fused_computation.11 | convolution fusion | flops 86704128 | bytes 2402720 | tf_op jit(solution)/shard_map/dot_general | solution.py:40
  52.1 9.8 %all-to-all-done.1 = f32[4,128,512]{2,0,1:T(4,128)S(1)} async-done(((f32[4,128,512]{2,0,1:T(4,128)}), f32[4,128,512]{2,0,1:T(4,128)S(1)}, u32[]{:S(2)}, u32[]{:S(2)}) %all-to-all-start.1) | async-done | bytes 1048608 | tf_op jit(solution)/shard_map/all_to_all | solution.py:190
  62.3 1.5 %convolution_bitcast_fusion.2.win_ref = f32[4,256,128]{2,1,0:T(8,128)} fusion(f32[4,512,128]{2,1,0:T(8,128)S(1)} %reshape.127, s32[256]{0:T(256)S(1)} %and_select_fusion.1), kind=kOutput, calls=%fused_computation.21 | convolution fusion | flops 805437440 | bytes 1573888 | tf_op jit(solution)/shard_map/qt,fql->ftl/dot_general | solution.py:198
  63.9 2.3 %shard_map.157 = f32[4,256,128]{2,1,0:T(8,128)} custom-call(f32[4,256,128]{2,1,0:T(8,128)} %convolution_bitcast_fusion.2.win_ref, s32[256,128]{1,0:T(8,128)} %add_select_fusion.lanes_ref), custom_call_target="tpu_custom_call" | custom-call | tf_op jit(solution)/shard_map/pallas_call | solution.py:67
  66.1 1.2 %reshape.128 = f32[4,4,8192]{2,1,0:T(4,128)S(1)} reshape(f32[4,256,128]{2,1,0:T(8,128)} %shard_map.157) | data formatting | bytes 1048576 | tf_op jit(solution)/shard_map/reshape | solution.py:201
  67.8 2.3 %fusion.33 = (f32[4,8192]{1,0:T(4,128)S(1)}, f32[4,8192]{1,0:T(4,128)}) fusion(f32[60,4,8192]{2,1,0:T(4,128)} %bitcast.111, f32[4,8192]{1,0:T(4,128)S(1)} %copy-done.3, f32[]{:T(128)} %bitcast.43, pred[8192]{0:T(1024)(128)(4,1)S(1)} %broadcast_compare_fusion, f32[4,8192]{1,0:T(4,128)S(1)} %multiply_reduce_fusion, f32[8192]{0:T(1024)S(1)} %reduce_sum.19), kind=kLoop, calls=%fused_computation.54 | loop fusion | flops 131072 | bytes 696324 | tf_op jit(solution)/shard_map/jit(_where)/select_n | solution.py:205
  71.3 10.4 %fusion.10 = f32[10,256,128]{2,0,1:T(8,128)S(1)} fusion(s32[256,128]{1,0:T(8,128)S(1)} %copy-done.4, bf16[5,256,128]{2,0,1:T(8,128)(2,1)S(1)} %get-tuple-element.10, bf16[5,256,128]{2,0,1:T(8,128)(2,1)S(1)} %get-tuple-element.9), kind=kOutput, calls=%fused_computation.16 | convolution fusion | flops 89391104 | bytes 2097152 | tf_op jit(solution)/shard_map/ftl,tlc->ftc/dot_general | solution.py:212
  81.8 1.2 %convolution_bitcast_fusion = f32[5,512,128]{1,2,0:T(8,128)S(1)} fusion(f32[5,256,128]{2,0,1:T(8,128)S(1)} %slice_add_fusion, s32[256]{0:T(256)S(1)} %and_select_fusion.1), kind=kOutput, calls=%fused_computation.19 | convolution fusion | flops 1006764032 | bytes 1967104 | tf_op jit(solution)/shard_map/qt,ftc->fqc/dot_general | solution.py:214
  83.6 2.2 %copy.36 = f32[5,128,512]{2,0,1:T(8,128)} copy(f32[5,128,512]{2,1,0:T(8,128)S(1)} %reshape.130) | data formatting | bytes 2621440 | tf_op jit(solution)/shard_map/reshape | solution.py:216
  85.8 4.9 %all-to-all-start.2 = ((f32[5,128,512]{2,0,1:T(8,128)}), f32[5,128,512]{2,0,1:T(8,128)S(1)}, u32[]{:S(2)}, u32[]{:S(2)}) async-start(f32[5,128,512]{2,0,1:T(8,128)} %copy.36), calls=%async_computation.2 | async-start | bytes 4194304 | tf_op jit(solution)/shard_map/all_to_all | solution.py:215
  90.7 1.9 %fusion.7 = bf16[1,72,8192]{2,1,0:T(8,128)(2,1)S(1)} fusion(bf16[72,72]{1,0:T(8,128)(2,1)S(1)} %copy-done.6, f32[8192]{0:T(1024)S(1)} %bitcast.122, bf16[4,72,8192]{2,1,0:T(8,128)(2,1)} %param.14, f32[72]{0:T(128)S(1)} %convert_reduce_fusion), kind=kOutput, calls=%fused_computation.12 | convolution fusion | flops 86704128 | bytes 2402720 | tf_op jit(solution)/shard_map/dot_general | solution.py:40
  92.6 2.5 %pad_maximum_fusion = bf16[4,72,8192]{2,1,0:T(8,128)(2,1)} fusion(bf16[1,72,8192]{2,1,0:T(8,128)(2,1)S(1)} %copy-done, bf16[1,72,8192]{2,1,0:T(8,128)(2,1)S(1)} %copy-done.2, bf16[1,72,8192]{2,1,0:T(8,128)(2,1)S(1)} %fusion.7, bf16[1,72,8192]{2,1,0:T(8,128)(2,1)S(1)} %copy-done.1), kind=kLoop, calls=%fused_computation.15 | loop fusion | flops 7077888 | bytes 9437184 | tf_op jit(solution)/shard_map/stack | solution.py:44
  95.1 13.1 %shard_map.158 = f32[60,4,8192]{2,1,0:T(4,128)} custom-call(f32[60,60]{1,0:T(8,128)} %m_ref.1, f32[60,1]{1,0:T(8,128)} %bitcast.121, f32[60,4,8192]{2,1,0:T(4,128)} %bitcast.112, f32[4,8192]{1,0:T(4,128)} %get-tuple-element.4.forcing_ref, s32[1,8192]{1,0:T(1,128)} %bitcast.115), custom_call_target="tpu_custom_call" | custom-call | flops 1415577600 | bytes 15728640 | tf_op jit(solution)/shard_map/pallas_call | solution.py:93
  108.2 12.3 %all-to-all-done.2 = f32[5,128,512]{2,0,1:T(8,128)S(1)} async-done(((f32[5,128,512]{2,0,1:T(8,128)}), f32[5,128,512]{2,0,1:T(8,128)S(1)}, u32[]{:S(2)}, u32[]{:S(2)}) %all-to-all-start.2) | async-done | bytes 1310752 | tf_op jit(solution)/shard_map/all_to_all | solution.py:215
  (68 shorter events, 15.3 us)
Async XLA Ops:
  0.6 21.7 %copy-start.10 = (f32[4,8192]{1,0:T(4,128)S(1)}, f32[4,8192]{1,0:T(4,128)}, u32[]{:S(2)}) copy-start(f32[4,8192]{1,0:T(4,128)} %param.27) | copy-start | bytes 393220
  0.6 21.8 %copy-start.6 = (bf16[72,72]{1,0:T(8,128)(2,1)S(1)}, bf16[72,72]{1,0:T(8,128)(2,1)}, u32[]{:S(2)}) copy-start(bf16[72,72]{1,0:T(8,128)(2,1)} %param.15) | copy-start | bytes 31108
  0.7 23.5 %copy-start.5 = (f32[4,8192]{1,0:T(4,128)S(1)}, f32[4,8192]{1,0:T(4,128)}, u32[]{:S(2)}) copy-start(f32[4,8192]{1,0:T(4,128)} %param.26) | copy-start | bytes 393220
  4.0 25.1 %all-to-all-start = ((s32[128,1,4]{2,1,0:T(1,128)}), s32[128,1,4]{2,1,0:T(1,128)S(1)}, u32[]{:S(2)}, u32[]{:S(2)}) async-start(s32[128,1,4]{2,1,0:T(1,128)} %bitcast.35), calls=%async_computation | async-start | bytes 131072 | tf_op jit(solution)/shard_map/all_to_all | solution.py:179
  33.3 28.6 %all-to-all-start.1 = ((f32[4,128,512]{2,0,1:T(4,128)}), f32[4,128,512]{2,0,1:T(4,128)S(1)}, u32[]{:S(2)}, u32[]{:S(2)}) async-start(f32[4,128,512]{2,0,1:T(4,128)} %copy.29), calls=%async_computation.1 | async-start | bytes 2097152 | tf_op jit(solution)/shard_map/all_to_all | solution.py:190
  45.9 5.5 %copy-start.7 = (s32[8192]{0:T(1024)S(1)}, s32[8192]{0:T(1024)}, u32[]{:S(2)}) copy-start(s32[8192]{0:T(1024)} %param.23) | copy-start | bytes 98308
  62.3 5.4 %copy-start.3 = (f32[4,8192]{1,0:T(4,128)S(1)}, f32[4,8192]{1,0:T(4,128)}, u32[]{:S(2)}) copy-start(f32[4,8192]{1,0:T(4,128)} %shard_map.159) | copy-start | bytes 393220
  70.1 1.2 copy-start.4
  85.8 6.8 %copy-start = (bf16[1,72,8192]{2,1,0:T(8,128)(2,1)S(1)}, bf16[1,72,8192]{2,1,0:T(8,128)(2,1)}, u32[]{:S(2)}) copy-start(bf16[1,72,8192]{2,1,0:T(8,128)(2,1)} %fusion.5) | copy-start | bytes 3538948
  85.8 34.7 %all-to-all-start.2 = ((f32[5,128,512]{2,0,1:T(8,128)}), f32[5,128,512]{2,0,1:T(8,128)S(1)}, u32[]{:S(2)}, u32[]{:S(2)}) async-start(f32[5,128,512]{2,0,1:T(8,128)} %copy.36), calls=%async_computation.2 | async-start | bytes 4194304 | tf_op jit(solution)/shard_map/all_to_all | solution.py:215
  90.7 1.9 %copy-start.1 = (bf16[1,72,8192]{2,1,0:T(8,128)(2,1)S(1)}, bf16[1,72,8192]{2,1,0:T(8,128)(2,1)}, u32[]{:S(2)}) copy-start(bf16[1,72,8192]{2,1,0:T(8,128)(2,1)} %fusion.8) | copy-start | bytes 3538948
  90.7 2.0 %copy-start.2 = (bf16[1,72,8192]{2,1,0:T(8,128)(2,1)S(1)}, bf16[1,72,8192]{2,1,0:T(8,128)(2,1)}, u32[]{:S(2)}) copy-start(bf16[1,72,8192]{2,1,0:T(8,128)(2,1)} %fusion.6) | copy-start | bytes 3538948
  121.3 0.8 copy-start.8
  121.3 0.9 copy-start.9

commit v6 on v5

--- a/solution.py
+++ b/solution.py
@@ -134,6 +134,35 @@
             transcendentals=0,
         ),
     )(first_row, state_by_level)
+
+
+def lane_scatter_kernel(order_ref, keys_ref, last_ref, present_ref, val_ref, out_ref):
+    order = order_ref[...]
+    keys = keys_ref[...]
+    last = last_ref[...]
+    present = present_ref[...] > 0
+    position = lax.broadcasted_iota(jnp.int32, keys.shape, 1)
+    links = []
+    shift = 1
+    while shift < keys.shape[1]:
+        joined = (position >= shift) & (pltpu.roll(keys, shift, 1) == keys)
+        links.append((shift, joined))
+        shift *= 2
+    for field in range(val_ref.shape[0]):
+        run = jnp.take_along_axis(val_ref[field], order, axis=1, mode="promise_in_bounds")
+        for shift, joined in links:
+            run = jnp.where(joined, run + pltpu.roll(run, shift, 1), run)
+        picked = jnp.take_along_axis(run, last, axis=1, mode="promise_in_bounds")
+        out_ref[field] = jnp.where(present, picked, 0.0)
+
+
+def lane_scatter(values, order, keys, last, present):
+    return pl.pallas_call(
+        lane_scatter_kernel,
+        out_shape=jax.ShapeDtypeStruct(values.shape, values.dtype),
+        in_specs=[pl.BlockSpec(memory_space=pltpu.VMEM)] * 5,
+        out_specs=pl.BlockSpec(memory_space=pltpu.VMEM),
+    )(order, keys, last, present, values)
 
 
 def per_device(
@@ -170,6 +199,15 @@
     tiles_pc = parent_column.reshape(tile_count, width)
     window_of_tile = tiles_pc[:, 0] // width
     lanes = tiles_pc % width
+    keys, order = lax.sort(
+        (lanes, lax.broadcasted_iota(jnp.int32, lanes.shape, 1)), dimension=1, num_keys=1
+    )
+    at_most = jnp.sum(
+        (lanes[:, None, :] <= jnp.arange(width, dtype=jnp.int32)[None, :, None]).astype(jnp.int32),
+        axis=2,
+    )
+    present = at_most - jnp.pad(at_most[:, :-1], ((0, 0), (1, 0)))
+    last = jnp.maximum(at_most - 1, 0)
 
     state_by_level = jnp.transpose(ocean_state, (1, 0, 2))
     base_top = top_level_mix(ocean_mixing[0], state_by_level)
@@ -205,12 +243,7 @@
     top = jnp.where(sea, base_top + ocean_mixing[0, 0] * forcing, state_by_level[0])
     sea_share = atmos_weight * sea_mask.astype(jnp.float32)[None, :]
     outgoing = jnp.concatenate([sea_share[None] * top[:, None, :], sea_share[None]], axis=0)
-    lane_hot = (lanes[:, :, None] == jnp.arange(width, dtype=jnp.int32)[None, None, :]).astype(
-        jnp.bfloat16
-    )
-    pieces = jnp.concatenate(split_kept(outgoing.reshape(5, tile_count, width)), axis=0)
-    partial = jnp.einsum("ftl,tlc->ftc", pieces, lane_hot, preferred_element_type=jnp.float32)
-    partial = partial[:5] + partial[5:]
+    partial = lane_scatter(outgoing.reshape(5, tile_count, width), order, keys, last, present)
     send_buffer = jnp.einsum("qt,ftc->fqc", placement, partial, precision=highest)
     returned = lax.all_to_all(
         send_buffer.reshape(5, devices, capacity),

time: 124 us -> 134 us (1.081)
  between operations: 1.04 us -> 14.5 us
  matrix products: 24.9 us -> 15.6 us
  waiting for transfers between devices: 22.1 us -> 13.8 us
  Pallas kernels: 20.2 us -> 26 us
  other arithmetic: 14.1 us -> 18.1 us
  starting transfers between devices: 26.2 us -> 29.3 us
    dot_general x1 -> x0, matrix products: 10.4 us -> none  [per_device(): jnp.einsum('ftl,tlc->ftc', pieces, lane_hot, preferred_element_type=jnp.f...]
    all_to_all x1, waiting for transfers between devices: 9.79 us -> 1.67 us  [per_device(): lax.all_to_all(served.reshape(4, devices, capacity), ('comp', 'sub'), spl...]
    pallas_call x0 -> x1, Pallas kernels: none -> 5.83 us  [lane_scatter(): pl.pallas_call(lane_scatter_kernel, out_shape=jax.ShapeDtypeStruct(values...]
    reduce_sum x0 -> x1, other arithmetic: none -> 4.38 us  [per_device(): jnp.sum((lanes[:, None, :] <= jnp.arange(width, dtype=jnp.int32)[None, :,...]
    all_to_all x1, starting transfers between devices: 4.89 us -> 8.1 us  [per_device(): lax.all_to_all(send_buffer.reshape(5, devices, capacity), ('comp', 'sub')...]
  transfers between devices with their start and end apart: 3 -> 3, of which waited for: 2 -> 2; matrix products, arithmetic and copies ran while one was open for 18% -> 20% of each run, Pallas kernels for 15% -> 14%
where the time goes in v6:
time: 134 us; the launch traced here: 133 us
  starting transfers between devices  29.3 us (22%)
  Pallas kernels  26 us (19%)
  other arithmetic  18.1 us (14%)
  matrix products  15.6 us (12%)
  local copies, waits for them, and re-layouts  15.2 us (11%)
  between operations  14.5 us (11%)
  waiting for transfers between devices  13.8 us (10%)
    pallas_call x1, Pallas kernels, ocean_update(): pl.pallas_call(ocean_kernel, grid=(cells // block,), out_shape=jax.ShapeD...  13.1 us
    all_to_all x1, waiting for transfers between devices, per_device(): lax.all_to_all(send_buffer.reshape(5, devices, capacity), ('comp', 'sub')...  12.2 us
    all_to_all x1, starting transfers between devices, per_device(): lax.all_to_all(request, ('comp', 'sub'), split_axis=0, concat_axis=0, til...  11.5 us
    dot_general x4, matrix products, diffuse_atmos(): jnp.dot(atmos_mixing, atmos_profiles[member], preferred_element_type=jnp....  10.2 us
    all_to_all x1, starting transfers between devices, per_device(): lax.all_to_all(served.reshape(4, devices, capacity), ('comp', 'sub'), spl...  9.76 us
    all_to_all x1, starting transfers between devices, per_device(): lax.all_to_all(send_buffer.reshape(5, devices, capacity), ('comp', 'sub')...  8.1 us
    pallas_call x1, Pallas kernels, lane_scatter(): pl.pallas_call(lane_scatter_kernel, out_shape=jax.ShapeDtypeStruct(values...  5.83 us
    pallas_call x1, Pallas kernels, top_level_mix(): pl.pallas_call(top_level_kernel, grid=(cells // block,), out_shape=jax.Sh...  4.84 us
  transfers between devices with their start and end apart: 3, of which 2 were waited for; matrix products, arithmetic and copies ran while one was open for 20% of the time, Pallas kernels for 14%

profile of v6, /device:TPU:1, one launch (start us, length us, event | category | flops | bytes accessed | tf_op | source)
XLA Modules:
  0.0 132.5 jit_solution(15465680884843067076)
XLA Ops:
  10.6 11.5 %all-to-all-start = ((s32[128,1,4]{2,1,0:T(1,128)}), s32[128,1,4]{2,1,0:T(1,128)S(1)}, u32[]{:S(2)}, u32[]{:S(2)}) async-start(s32[128,1,4]{2,1,0:T(1,128)} %bitcast.35), calls=%async_computation | async-start | bytes 131072 | tf_op jit(solution)/shard_map/all_to_all | solution.py:217
  24.4 1.2 slice_bitcast_fusion.7.row_ref
  26.4 1.2 fusion.46
  29.4 2.8 %fusion.4 = bf16[1,72,8192]{2,1,0:T(8,128)(2,1)} fusion(bf16[72,72]{1,0:T(8,128)(2,1)S(1)} %copy-done.6, f32[8192]{0:T(1024)S(1)} %bitcast.126, bf16[4,72,8192]{2,1,0:T(8,128)(2,1)} %param.14, f32[72]{0:T(128)S(1)} %convert_reduce_fusion.1), kind=kOutput, calls=%fused_computation.10 | convolution fusion | flops 86704128 | bytes 2402720 | tf_op jit(solution)/shard_map/dot_general | solution.py:40
  34.7 1.6 %copy.39 = f32[4,128,512]{2,0,1:T(4,128)} copy(f32[4,128,512]{2,1,0:T(8,128)S(1)} %reshape.126) | data formatting | bytes 2097152 | tf_op jit(solution)/shard_map/reshape | solution.py:229
  36.4 9.8 %all-to-all-start.1 = ((f32[4,128,512]{2,0,1:T(4,128)}), f32[4,128,512]{2,0,1:T(4,128)S(1)}, u32[]{:S(2)}, u32[]{:S(2)}) async-start(f32[4,128,512]{2,0,1:T(4,128)} %copy.39), calls=%async_computation.1 | async-start | bytes 2097152 | tf_op jit(solution)/shard_map/all_to_all | solution.py:228
  46.1 2.8 %fusion.7 = bf16[1,72,8192]{2,1,0:T(8,128)(2,1)} fusion(bf16[72,72]{1,0:T(8,128)(2,1)S(1)} %copy-done.6, f32[8192]{0:T(1024)S(1)} %bitcast.125, f32[72]{0:T(128)S(1)} %convert_reduce_fusion.1, bf16[4,72,8192]{2,1,0:T(8,128)(2,1)} %param.14), kind=kOutput, calls=%fused_computation.13 | convolution fusion | flops 86704128 | bytes 2402720 | tf_op jit(solution)/shard_map/dot_general | solution.py:40
  48.9 1.3 slice.140
  50.4 4.8 %shard_map.159 = f32[4,8192]{1,0:T(4,128)} custom-call(f32[60]{0:T(128)} %slice_bitcast_fusion.7.row_ref, f32[60,4,8192]{2,1,0:T(4,128)} %bitcast.110), custom_call_target="tpu_custom_call" | custom-call | flops 3932160 | bytes 7995392 | tf_op jit(solution)/shard_map/pallas_call | solution.py:122
  55.3 2.8 %fusion.5 = bf16[1,72,8192]{2,1,0:T(8,128)(2,1)} fusion(bf16[72,72]{1,0:T(8,128)(2,1)S(1)} %copy-done.6, f32[8192]{0:T(1024)S(1)} %bitcast.124, bf16[4,72,8192]{2,1,0:T(8,128)(2,1)} %param.14, f32[72]{0:T(128)S(1)} %convert_reduce_fusion.1), kind=kOutput, calls=%fused_computation.11 | convolution fusion | flops 86704128 | bytes 2402720 | tf_op jit(solution)/shard_map/dot_general | solution.py:40
  58.1 4.4 %convert_reduce_fusion = s32[256,128]{1,0:T(8,128)S(1)} fusion(s32[256,128]{1,0:T(8,128)S(1)} %copy-done.3), kind=kLoop, calls=%fused_computation | loop fusion | flops 12550144 | bytes 262144 | tf_op jit(solution)/shard_map/reduce_sum | solution.py:205
  63.2 1.7 %all-to-all-done.1 = f32[4,128,512]{2,0,1:T(4,128)S(1)} async-done(((f32[4,128,512]{2,0,1:T(4,128)}), f32[4,128,512]{2,0,1:T(4,128)S(1)}, u32[]{:S(2)}, u32[]{:S(2)}) %all-to-all-start.1) | async-done | bytes 1048608 | tf_op jit(solution)/shard_map/all_to_all | solution.py:228
  65.4 1.5 %convolution_bitcast_fusion.2.win_ref = f32[4,256,128]{2,1,0:T(8,128)} fusion(f32[4,512,128]{2,1,0:T(8,128)S(1)} %reshape.127, s32[256]{0:T(256)S(1)} %and_select_fusion.1), kind=kOutput, calls=%fused_computation.17 | convolution fusion | flops 805437440 | bytes 1573888 | tf_op jit(solution)/shard_map/qt,fql->ftl/dot_general | solution.py:236
  66.9 2.3 %shard_map.157 = f32[4,256,128]{2,1,0:T(8,128)} custom-call(f32[4,256,128]{2,1,0:T(8,128)} %convolution_bitcast_fusion.2.win_ref, s32[256,128]{1,0:T(8,128)} %add_select_fusion.lanes_ref), custom_call_target="tpu_custom_call" | custom-call | tf_op jit(solution)/shard_map/pallas_call | solution.py:67
  69.2 1.2 reshape.128
  70.8 2.3 %fusion.25 = (f32[4,8192]{1,0:T(4,128)S(1)}, f32[4,8192]{1,0:T(4,128)}) fusion(f32[60,4,8192]{2,1,0:T(4,128)} %bitcast.111, f32[4,8192]{1,0:T(4,128)S(1)} %copy-done.4, f32[]{:T(128)} %bitcast.43, pred[8192]{0:T(1024)(128)(4,1)S(1)} %broadcast_compare_fusion, f32[4,8192]{1,0:T(4,128)S(1)} %multiply_reduce_fusion, f32[8192]{0:T(1024)S(1)} %reduce_sum.28), kind=kLoop, calls=%fused_computation.44 | loop fusion | flops 131072 | bytes 696324 | tf_op jit(solution)/shard_map/jit(_where)/select_n | solution.py:243
  74.5 5.8 %shard_map.160 = f32[5,256,128]{2,1,0:T(8,128)} custom-call(s32[256,128]{1,0:T(8,128)} %get-tuple-element.5.order_ref, s32[256,128]{1,0:T(8,128)} %get-tuple-element.6.keys_ref, s32[256,128]{1,0:T(8,128)} %get-tuple-element.18.last_ref, s32[256,128]{1,0:T(8,128)} %get-tuple-element.17.present_ref, f32[5,256,128]{2,1,0:T(8,128)} %pad_maximum_fusion.1.val_ref), custom_call_target="tpu_custom_call" | custom-call | tf_op jit(solution)/shard_map/pallas_call | solution.py:160
  80.3 2.3 %convolution_bitcast_fusion = f32[5,512,128]{1,2,0:T(8,128)S(1)} fusion(f32[5,256,128]{2,1,0:T(8,128)} %shard_map.160, s32[256]{0:T(256)S(1)} %and_select_fusion.1), kind=kOutput, calls=%fused_computation.15 | convolution fusion | flops 1006764032 | bytes 1967104 | tf_op jit(solution)/shard_map/qt,ftc->fqc/dot_general | solution.py:247
  83.2 2.2 %copy.45 = f32[5,128,512]{2,0,1:T(8,128)} copy(f32[5,128,512]{2,1,0:T(8,128)S(1)} %reshape.130) | data formatting | bytes 2621440 | tf_op jit(solution)/shard_map/reshape | solution.py:249
  85.4 8.1 %all-to-all-start.2 = ((f32[5,128,512]{2,0,1:T(8,128)}), f32[5,128,512]{2,0,1:T(8,128)S(1)}, u32[]{:S(2)}, u32[]{:S(2)}) async-start(f32[5,128,512]{2,0,1:T(8,128)} %copy.45), calls=%async_computation.2 | async-start | bytes 4194304 | tf_op jit(solution)/shard_map/all_to_all | solution.py:248
  93.5 1.9 %fusion.6 = bf16[1,72,8192]{2,1,0:T(8,128)(2,1)S(1)} fusion(bf16[72,72]{1,0:T(8,128)(2,1)S(1)} %copy-done.6, f32[8192]{0:T(1024)S(1)} %bitcast.123, bf16[4,72,8192]{2,1,0:T(8,128)(2,1)} %param.14, f32[72]{0:T(128)S(1)} %convert_reduce_fusion.1), kind=kOutput, calls=%fused_computation.12 | convolution fusion | flops 86704128 | bytes 2402720 | tf_op jit(solution)/shard_map/dot_general | solution.py:40
  95.5 2.5 %pad_maximum_fusion = bf16[4,72,8192]{2,1,0:T(8,128)(2,1)} fusion(bf16[1,72,8192]{2,1,0:T(8,128)(2,1)S(1)} %copy-done, bf16[1,72,8192]{2,1,0:T(8,128)(2,1)S(1)} %copy-done.2, bf16[1,72,8192]{2,1,0:T(8,128)(2,1)S(1)} %fusion.6, bf16[1,72,8192]{2,1,0:T(8,128)(2,1)S(1)} %copy-done.1), kind=kLoop, calls=%fused_computation.14 | loop fusion | flops 7077888 | bytes 9437184 | tf_op jit(solution)/shard_map/stack | solution.py:44
  98.0 13.1 %shard_map.158 = f32[60,4,8192]{2,1,0:T(4,128)} custom-call(f32[60,60]{1,0:T(8,128)} %m_ref.1, f32[60,1]{1,0:T(8,128)} %bitcast.122, f32[60,4,8192]{2,1,0:T(4,128)} %bitcast.112, f32[4,8192]{1,0:T(4,128)} %get-tuple-element.8.forcing_ref, s32[1,8192]{1,0:T(1,128)} %bitcast.116), custom_call_target="tpu_custom_call" | custom-call | flops 1415577600 | bytes 15728640 | tf_op jit(solution)/shard_map/pallas_call | solution.py:93
  111.1 12.2 %all-to-all-done.2 = f32[5,128,512]{2,0,1:T(8,128)S(1)} async-done(((f32[5,128,512]{2,0,1:T(8,128)}), f32[5,128,512]{2,0,1:T(8,128)S(1)}, u32[]{:S(2)}, u32[]{:S(2)}) %all-to-all-start.2) | async-done | bytes 1310752 | tf_op jit(solution)/shard_map/all_to_all | solution.py:248
  (77 shorter events, 16.9 us)
Async XLA Ops:
  7.2 22.2 %copy-start.6 = (bf16[72,72]{1,0:T(8,128)(2,1)S(1)}, bf16[72,72]{1,0:T(8,128)(2,1)}, u32[]{:S(2)}) copy-start(bf16[72,72]{1,0:T(8,128)(2,1)} %param.15) | copy-start | bytes 31108
  7.2 21.6 %copy-start.9 = (f32[4,8192]{1,0:T(4,128)S(1)}, f32[4,8192]{1,0:T(4,128)}, u32[]{:S(2)}) copy-start(f32[4,8192]{1,0:T(4,128)} %param.17) | copy-start | bytes 393220
  7.2 21.8 %copy-start.12 = (f32[8192]{0:T(1024)S(1)}, f32[8192]{0:T(1024)}, u32[]{:S(2)}) copy-start(f32[8192]{0:T(1024)} %param.16) | copy-start | bytes 98308
  7.2 22.1 %copy-start.11 = (f32[4,8192]{1,0:T(4,128)S(1)}, f32[4,8192]{1,0:T(4,128)}, u32[]{:S(2)}) copy-start(f32[4,8192]{1,0:T(4,128)} %param.27) | copy-start | bytes 393220
  10.6 21.6 %all-to-all-start = ((s32[128,1,4]{2,1,0:T(1,128)}), s32[128,1,4]{2,1,0:T(1,128)S(1)}, u32[]{:S(2)}, u32[]{:S(2)}) async-start(s32[128,1,4]{2,1,0:T(1,128)} %bitcast.35), calls=%async_computation | async-start | bytes 131072 | tf_op jit(solution)/shard_map/all_to_all | solution.py:217
  22.1 52.4 %sort.17.cloned.1.call-start = ((), (), s32[]{:S(2)}) async-start(), calls=%async_computation.3 | async-start | bytes 786464 | tf_op jit(solution)/shard_map/sort | solution.py:202
  36.4 14.0 %copy-start.5 = (f32[4,8192]{1,0:T(4,128)S(1)}, f32[4,8192]{1,0:T(4,128)}, u32[]{:S(2)}) copy-start(f32[4,8192]{1,0:T(4,128)} %param.26) | copy-start | bytes 393220
  36.4 28.6 %all-to-all-start.1 = ((f32[4,128,512]{2,0,1:T(4,128)}), f32[4,128,512]{2,0,1:T(4,128)S(1)}, u32[]{:S(2)}, u32[]{:S(2)}) async-start(f32[4,128,512]{2,0,1:T(4,128)} %copy.39), calls=%async_computation.1 | async-start | bytes 2097152 | tf_op jit(solution)/shard_map/all_to_all | solution.py:228
  55.3 2.8 %copy-start.7 = (s32[8192]{0:T(1024)S(1)}, s32[8192]{0:T(1024)}, u32[]{:S(2)}) copy-start(s32[8192]{0:T(1024)} %param.23) | copy-start | bytes 98308
  55.3 2.8 %copy-start.3 = (s32[256,128]{1,0:T(8,128)S(1)}, s32[256,128]{1,0:T(8,128)}, u32[]{:S(2)}) copy-start(s32[256,128]{1,0:T(8,128)} %add_select_fusion.lanes_ref) | copy-start | bytes 393220
  65.3 5.5 %copy-start.4 = (f32[4,8192]{1,0:T(4,128)S(1)}, f32[4,8192]{1,0:T(4,128)}, u32[]{:S(2)}) copy-start(f32[4,8192]{1,0:T(4,128)} %shard_map.159) | copy-start | bytes 393220
  85.4 10.0 %copy-start = (bf16[1,72,8192]{2,1,0:T(8,128)(2,1)S(1)}, bf16[1,72,8192]{2,1,0:T(8,128)(2,1)}, u32[]{:S(2)}) copy-start(bf16[1,72,8192]{2,1,0:T(8,128)(2,1)} %fusion.4) | copy-start | bytes 3538948
  85.4 37.8 %all-to-all-start.2 = ((f32[5,128,512]{2,0,1:T(8,128)}), f32[5,128,512]{2,0,1:T(8,128)S(1)}, u32[]{:S(2)}, u32[]{:S(2)}) async-start(f32[5,128,512]{2,0,1:T(8,128)} %copy.45), calls=%async_computation.2 | async-start | bytes 4194304 | tf_op jit(solution)/shard_map/all_to_all | solution.py:248
  93.5 1.9 %copy-start.1 = (bf16[1,72,8192]{2,1,0:T(8,128)(2,1)S(1)}, bf16[1,72,8192]{2,1,0:T(8,128)(2,1)}, u32[]{:S(2)}) copy-start(bf16[1,72,8192]{2,1,0:T(8,128)(2,1)} %fusion.7) | copy-start | bytes 3538948
  93.5 2.0 %copy-start.2 = (bf16[1,72,8192]{2,1,0:T(8,128)(2,1)S(1)}, bf16[1,72,8192]{2,1,0:T(8,128)(2,1)}, u32[]{:S(2)}) copy-start(bf16[1,72,8192]{2,1,0:T(8,128)(2,1)} %fusion.5) | copy-start | bytes 3538948
  124.0 0.8 copy-start.8
  124.0 0.9 copy-start.10
Sparse Core Ops, SparseCore 0:
  25.2 9.9 sort.19.cloned.1.call-done
  (1 shorter events, 0.0 us)

commit v7 on v6

--- a/solution.py
+++ b/solution.py
@@ -163,6 +163,36 @@
         in_specs=[pl.BlockSpec(memory_space=pltpu.VMEM)] * 5,
         out_specs=pl.BlockSpec(memory_space=pltpu.VMEM),
     )(order, keys, last, present, values)
+
+
+def lane_sort_kernel(key_ref, sorted_ref):
+    values = key_ref[...]
+    count = values.shape[1]
+    position = lax.broadcasted_iota(jnp.int32, values.shape, 1)
+    block = 2
+    while block <= count:
+        stride = block // 2
+        while stride >= 1:
+            lower = (position & stride) == 0
+            partner = jnp.where(
+                lower, pltpu.roll(values, count - stride, 1), pltpu.roll(values, stride, 1)
+            )
+            keep_min = lower == ((position & block) == 0)
+            values = jnp.where(
+                keep_min, jnp.minimum(values, partner), jnp.maximum(values, partner)
+            )
+            stride //= 2
+        block *= 2
+    sorted_ref[...] = values
+
+
+def lane_sort(keys):
+    return pl.pallas_call(
+        lane_sort_kernel,
+        out_shape=jax.ShapeDtypeStruct(keys.shape, keys.dtype),
+        in_specs=[pl.BlockSpec(memory_space=pltpu.VMEM)],
+        out_specs=pl.BlockSpec(memory_space=pltpu.VMEM),
+    )(keys)
 
 
 def per_device(
@@ -199,9 +229,8 @@
     tiles_pc = parent_column.reshape(tile_count, width)
     window_of_tile = tiles_pc[:, 0] // width
     lanes = tiles_pc % width
-    keys, order = lax.sort(
-        (lanes, lax.broadcasted_iota(jnp.int32, lanes.shape, 1)), dimension=1, num_keys=1
-    )
+    ranked = lane_sort(lanes * width + lax.broadcasted_iota(jnp.int32, lanes.shape, 1))
+    keys, order = ranked // width, ranked % width
     at_most = jnp.sum(
         (lanes[:, None, :] <= jnp.arange(width, dtype=jnp.int32)[None, :, None]).astype(jnp.int32),
         axis=2,

time: 134 us -> 125 us (0.933)
  between operations: 14.5 us -> 1.04 us
  Pallas kernels: 26 us -> 30.5 us
  starting transfers between devices: 29.3 us -> 31 us
  waiting for transfers between devices: 13.8 us -> 12.2 us
    pallas_call x0 -> x1, Pallas kernels: none -> 4.44 us  [lane_sort(): pl.pallas_call(lane_sort_kernel, out_shape=jax.ShapeDtypeStruct(keys.shap...]
    all_to_all x1, waiting for transfers between devices: 1.67 us -> 0.01 us  [per_device(): lax.all_to_all(served.reshape(4, devices, capacity), ('comp', 'sub'), spl...]
    all_to_all x1, starting transfers between devices: 8.1 us -> 9.76 us  [per_device(): lax.all_to_all(send_buffer.reshape(5, devices, capacity), ('comp', 'sub')...]
  transfers between devices with their start and end apart: 3 -> 3, of which waited for: 2 -> 1; matrix products, arithmetic and copies ran while one was open for 20% -> 22% of each run, Pallas kernels for 14% -> 18%
where the time goes in v7:
time: 125 us; the launch traced here: 124 us
  starting transfers between devices  31 us (25%)
  Pallas kernels  30.5 us (24%)
  other arithmetic  19.4 us (16%)
  matrix products  15.6 us (12%)
  local copies, waits for them, and re-layouts  14.5 us (12%)
  waiting for transfers between devices  12.2 us (10%)
    pallas_call x1, Pallas kernels, ocean_update(): pl.pallas_call(ocean_kernel, grid=(cells // block,), out_shape=jax.ShapeD...  13.1 us
    all_to_all x1, waiting for transfers between devices, per_device(): lax.all_to_all(send_buffer.reshape(5, devices, capacity), ('comp', 'sub')...  12.2 us
    all_to_all x1, starting transfers between devices, per_device(): lax.all_to_all(request, ('comp', 'sub'), split_axis=0, concat_axis=0, til...  11.5 us
    dot_general x4, matrix products, diffuse_atmos(): jnp.dot(atmos_mixing, atmos_profiles[member], preferred_element_type=jnp....  10.2 us
    all_to_all x1, starting transfers between devices, per_device(): lax.all_to_all(served.reshape(4, devices, capacity), ('comp', 'sub'), spl...  9.76 us
    all_to_all x1, starting transfers between devices, per_device(): lax.all_to_all(send_buffer.reshape(5, devices, capacity), ('comp', 'sub')...  9.76 us
    pallas_call x1, Pallas kernels, lane_scatter(): pl.pallas_call(lane_scatter_kernel, out_shape=jax.ShapeDtypeStruct(values...  5.83 us
    pallas_call x1, Pallas kernels, top_level_mix(): pl.pallas_call(top_level_kernel, grid=(cells // block,), out_shape=jax.Sh...  4.84 us
  transfers between devices with their start and end apart: 3, of which 1 were waited for; matrix products, arithmetic and copies ran while one was open for 22% of the time, Pallas kernels for 18%

profile of v7, /device:TPU:1, one launch (start us, length us, event | category | flops | bytes accessed | tf_op | source)
XLA Modules:
  0.0 124.2 jit_solution(7467534696130712631)
XLA Ops:
  4.0 11.5 %all-to-all-start = ((s32[128,1,4]{2,1,0:T(1,128)}), s32[128,1,4]{2,1,0:T(1,128)S(1)}, u32[]{:S(2)}, u32[]{:S(2)}) async-start(s32[128,1,4]{2,1,0:T(1,128)} %bitcast.35), calls=%async_computation | async-start | bytes 131072 | tf_op jit(solution)/shard_map/all_to_all | solution.py:246
  17.1 1.3 %slice_bitcast_fusion.7.row_ref = f32[60]{0:T(128)} fusion(f32[60,60]{1,0:T(8,128)} %m_ref.1), kind=kLoop, calls=%fused_computation.103 | loop fusion | bytes 480 | tf_op jit(solution)/shard_map/squeeze | solution.py:242
  19.2 1.2 %fusion.48 = (f32[1,8192]{1,0:T(1,128)S(1)}, f32[1,8192]{1,0:T(1,128)S(1)}, f32[1,8192]{1,0:T(1,128)S(1)}) fusion(f32[4,8192]{1,0:T(4,128)} %param.18), kind=kLoop, calls=%fused_computation.106 | loop fusion | flops 8192 | bytes 229376 | tf_op jit(solution)/shard_map/slice | solution.py:29
  21.6 1.4 %fusion.44 = (f32[1,8192]{1,0:T(1,128)S(1)}, f32[1,8192]{1,0:T(1,128)S(1)}, f32[1,8192]{1,0:T(1,128)S(1)}, f32[1,8192]{1,0:T(1,128)S(1)}) fusion(f32[4,1,8192]{2,1,0:T(1,128)S(1)} %slice_convert_fusion, f32[4,8192]{1,0:T(4,128)} %param.17), kind=kLoop, calls=%fused_computation.83 | loop fusion | flops 32768 | bytes 393216 | tf_op jit(solution)/shard_map/sub | solution.py:15
  23.4 2.8 %fusion.4 = bf16[1,72,8192]{2,1,0:T(8,128)(2,1)} fusion(bf16[72,72]{1,0:T(8,128)(2,1)S(1)} %copy-done.7, f32[8192]{0:T(1024)S(1)} %bitcast.126, bf16[4,72,8192]{2,1,0:T(8,128)(2,1)} %param.14, f32[72]{0:T(128)S(1)} %convert_reduce_fusion.1), kind=kOutput, calls=%fused_computation.10 | convolution fusion | flops 86704128 | bytes 2402720 | tf_op jit(solution)/shard_map/dot_general | solution.py:40
  28.7 1.6 %copy.39 = f32[4,128,512]{2,0,1:T(4,128)} copy(f32[4,128,512]{2,1,0:T(8,128)S(1)} %reshape.126) | data formatting | bytes 2097152 | tf_op jit(solution)/shard_map/reshape | solution.py:258
  30.4 9.8 %all-to-all-start.1 = ((f32[4,128,512]{2,0,1:T(4,128)}), f32[4,128,512]{2,0,1:T(4,128)S(1)}, u32[]{:S(2)}, u32[]{:S(2)}) async-start(f32[4,128,512]{2,0,1:T(4,128)} %copy.39), calls=%async_computation.1 | async-start | bytes 2097152 | tf_op jit(solution)/shard_map/all_to_all | solution.py:257
  40.1 2.8 %fusion.7 = bf16[1,72,8192]{2,1,0:T(8,128)(2,1)} fusion(bf16[72,72]{1,0:T(8,128)(2,1)S(1)} %copy-done.7, f32[8192]{0:T(1024)S(1)} %bitcast.125, f32[72]{0:T(128)S(1)} %convert_reduce_fusion.1, bf16[4,72,8192]{2,1,0:T(8,128)(2,1)} %param.14), kind=kOutput, calls=%fused_computation.13 | convolution fusion | flops 86704128 | bytes 2402720 | tf_op jit(solution)/shard_map/dot_general | solution.py:40
  44.3 4.4 %shard_map.159 = s32[256,128]{1,0:T(8,128)} custom-call(s32[256,128]{1,0:T(8,128)} %get-tuple-element.17.key_ref), custom_call_target="tpu_custom_call" | custom-call | tf_op jit(solution)/shard_map/pallas_call | solution.py:190
  48.8 4.8 %shard_map.160 = f32[4,8192]{1,0:T(4,128)} custom-call(f32[60]{0:T(128)} %slice_bitcast_fusion.7.row_ref, f32[60,4,8192]{2,1,0:T(4,128)} %bitcast.110), custom_call_target="tpu_custom_call" | custom-call | flops 3932160 | bytes 7995392 | tf_op jit(solution)/shard_map/pallas_call | solution.py:122
  53.7 2.8 %fusion.5 = bf16[1,72,8192]{2,1,0:T(8,128)(2,1)} fusion(bf16[72,72]{1,0:T(8,128)(2,1)S(1)} %copy-done.7, f32[8192]{0:T(1024)S(1)} %bitcast.124, bf16[4,72,8192]{2,1,0:T(8,128)(2,1)} %param.14, f32[72]{0:T(128)S(1)} %convert_reduce_fusion.1), kind=kOutput, calls=%fused_computation.11 | convolution fusion | flops 86704128 | bytes 2402720 | tf_op jit(solution)/shard_map/dot_general | solution.py:40
  56.5 4.4 %convert_reduce_fusion = s32[256,128]{1,0:T(8,128)S(1)} fusion(s32[256,128]{1,0:T(8,128)S(1)} %get-tuple-element.18.lanes_ref), kind=kLoop, calls=%fused_computation | loop fusion | flops 12550144 | bytes 262144 | tf_op jit(solution)/shard_map/reduce_sum | solution.py:234
  62.2 1.5 %convolution_bitcast_fusion.2.win_ref = f32[4,256,128]{2,1,0:T(8,128)} fusion(f32[4,512,128]{2,1,0:T(8,128)S(1)} %reshape.127, s32[256]{0:T(256)S(1)} %and_select_fusion.1), kind=kOutput, calls=%fused_computation.17 | convolution fusion | flops 805437440 | bytes 1573888 | tf_op jit(solution)/shard_map/qt,fql->ftl/dot_general | solution.py:265
  63.8 2.3 %shard_map.157 = f32[4,256,128]{2,1,0:T(8,128)} custom-call(f32[4,256,128]{2,1,0:T(8,128)} %convolution_bitcast_fusion.2.win_ref, s32[256,128]{1,0:T(8,128)} %copy-done.3), custom_call_target="tpu_custom_call" | custom-call | tf_op jit(solution)/shard_map/pallas_call | solution.py:67
  66.0 1.2 %reshape.128 = f32[4,4,8192]{2,1,0:T(4,128)S(1)} reshape(f32[4,256,128]{2,1,0:T(8,128)} %shard_map.157) | data formatting | bytes 1048576 | tf_op jit(solution)/shard_map/reshape | solution.py:268
  67.7 2.3 %fusion.25 = (f32[4,8192]{1,0:T(4,128)S(1)}, f32[4,8192]{1,0:T(4,128)}) fusion(f32[60,4,8192]{2,1,0:T(4,128)} %bitcast.111, f32[4,8192]{1,0:T(4,128)S(1)} %copy-done.4, f32[]{:T(128)} %bitcast.43, pred[8192]{0:T(1024)(128)(4,1)S(1)} %broadcast_compare_fusion, f32[4,8192]{1,0:T(4,128)S(1)} %multiply_reduce_fusion, f32[8192]{0:T(1024)S(1)} %reduce_sum.28), kind=kLoop, calls=%fused_computation.49 | loop fusion | flops 131072 | bytes 696324 | tf_op jit(solution)/shard_map/jit(_where)/select_n | solution.py:272
  71.3 5.8 %shard_map.161 = f32[5,256,128]{2,1,0:T(8,128)} custom-call(s32[256,128]{1,0:T(8,128)} %get-tuple-element.16.order_ref, s32[256,128]{1,0:T(8,128)} %get-tuple-element.15.keys_ref, s32[256,128]{1,0:T(8,128)} %get-tuple-element.32.last_ref, s32[256,128]{1,0:T(8,128)} %get-tuple-element.33.present_ref, f32[5,256,128]{2,1,0:T(8,128)} %pad_maximum_fusion.1.val_ref), custom_call_target="tpu_custom_call" | custom-call | tf_op jit(solution)/shard_map/pallas_call | solution.py:160
  77.2 2.3 %convolution_bitcast_fusion = f32[5,512,128]{1,2,0:T(8,128)S(1)} fusion(f32[5,256,128]{2,1,0:T(8,128)} %shard_map.161, s32[256]{0:T(256)S(1)} %and_select_fusion.1), kind=kOutput, calls=%fused_computation.15 | convolution fusion | flops 1006764032 | bytes 1967104 | tf_op jit(solution)/shard_map/qt,ftc->fqc/dot_general | solution.py:276
  80.1 2.2 %copy.45 = f32[5,128,512]{2,0,1:T(8,128)} copy(f32[5,128,512]{2,1,0:T(8,128)S(1)} %reshape.130) | data formatting | bytes 2621440 | tf_op jit(solution)/shard_map/reshape | solution.py:278
  82.2 9.8 %all-to-all-start.2 = ((f32[5,128,512]{2,0,1:T(8,128)}), f32[5,128,512]{2,0,1:T(8,128)S(1)}, u32[]{:S(2)}, u32[]{:S(2)}) async-start(f32[5,128,512]{2,0,1:T(8,128)} %copy.45), calls=%async_computation.2 | async-start | bytes 4194304 | tf_op jit(solution)/shard_map/all_to_all | solution.py:277
  92.0 1.9 %fusion.6 = bf16[1,72,8192]{2,1,0:T(8,128)(2,1)S(1)} fusion(bf16[72,72]{1,0:T(8,128)(2,1)S(1)} %copy-done.7, f32[8192]{0:T(1024)S(1)} %bitcast.123, bf16[4,72,8192]{2,1,0:T(8,128)(2,1)} %param.14, f32[72]{0:T(128)S(1)} %convert_reduce_fusion.1), kind=kOutput, calls=%fused_computation.12 | convolution fusion | flops 86704128 | bytes 2402720 | tf_op jit(solution)/shard_map/dot_general | solution.py:40
  94.0 2.5 %pad_maximum_fusion = bf16[4,72,8192]{2,1,0:T(8,128)(2,1)} fusion(bf16[1,72,8192]{2,1,0:T(8,128)(2,1)S(1)} %copy-done, bf16[1,72,8192]{2,1,0:T(8,128)(2,1)S(1)} %copy-done.2, bf16[1,72,8192]{2,1,0:T(8,128)(2,1)S(1)} %fusion.6, bf16[1,72,8192]{2,1,0:T(8,128)(2,1)S(1)} %copy-done.1), kind=kLoop, calls=%fused_computation.14 | loop fusion | flops 7077888 | bytes 9437184 | tf_op jit(solution)/shard_map/stack | solution.py:44
  96.5 13.1 %shard_map.158 = f32[60,4,8192]{2,1,0:T(4,128)} custom-call(f32[60,60]{1,0:T(8,128)} %m_ref.1, f32[60,1]{1,0:T(8,128)} %bitcast.122, f32[60,4,8192]{2,1,0:T(4,128)} %bitcast.112, f32[4,8192]{1,0:T(4,128)} %get-tuple-element.4.forcing_ref, s32[1,8192]{1,0:T(1,128)} %bitcast.116), custom_call_target="tpu_custom_call" | custom-call | flops 1415577600 | bytes 15728640 | tf_op jit(solution)/shard_map/pallas_call | solution.py:93
  109.6 12.2 %all-to-all-done.2 = f32[5,128,512]{2,0,1:T(8,128)S(1)} async-done(((f32[5,128,512]{2,0,1:T(8,128)}), f32[5,128,512]{2,0,1:T(8,128)S(1)}, u32[]{:S(2)}, u32[]{:S(2)}) %all-to-all-start.2) | async-done | bytes 1310752 | tf_op jit(solution)/shard_map/all_to_all | solution.py:277
  (74 shorter events, 17.4 us)
Async XLA Ops:
  0.6 22.8 %copy-start.7 = (bf16[72,72]{1,0:T(8,128)(2,1)S(1)}, bf16[72,72]{1,0:T(8,128)(2,1)}, u32[]{:S(2)}) copy-start(bf16[72,72]{1,0:T(8,128)(2,1)} %param.15) | copy-start | bytes 31108
  0.6 22.4 %copy-start.12 = (f32[8192]{0:T(1024)S(1)}, f32[8192]{0:T(1024)}, u32[]{:S(2)}) copy-start(f32[8192]{0:T(1024)} %param.16) | copy-start | bytes 98308
  0.7 22.7 %copy-start.11 = (f32[4,8192]{1,0:T(4,128)S(1)}, f32[4,8192]{1,0:T(4,128)}, u32[]{:S(2)}) copy-start(f32[4,8192]{1,0:T(4,128)} %param.27) | copy-start | bytes 393220
  4.0 22.1 %all-to-all-start = ((s32[128,1,4]{2,1,0:T(1,128)}), s32[128,1,4]{2,1,0:T(1,128)S(1)}, u32[]{:S(2)}, u32[]{:S(2)}) async-start(s32[128,1,4]{2,1,0:T(1,128)} %bitcast.35), calls=%async_computation | async-start | bytes 131072 | tf_op jit(solution)/shard_map/all_to_all | solution.py:246
  16.2 40.2 %copy-start.3 = (s32[256,128]{1,0:T(8,128)}, s32[256,128]{1,0:T(8,128)S(1)}, u32[]{:S(2)}) copy-start(s32[256,128]{1,0:T(8,128)S(1)} %get-tuple-element.18.lanes_ref) | copy-start | bytes 393220
  30.4 18.4 %copy-start.6 = (f32[4,8192]{1,0:T(4,128)S(1)}, f32[4,8192]{1,0:T(4,128)}, u32[]{:S(2)}) copy-start(f32[4,8192]{1,0:T(4,128)} %param.26) | copy-start | bytes 393220
  30.4 31.4 %all-to-all-start.1 = ((f32[4,128,512]{2,0,1:T(4,128)}), f32[4,128,512]{2,0,1:T(4,128)S(1)}, u32[]{:S(2)}, u32[]{:S(2)}) async-start(f32[4,128,512]{2,0,1:T(4,128)} %copy.39), calls=%async_computation.1 | async-start | bytes 2097152 | tf_op jit(solution)/shard_map/all_to_all | solution.py:257
  53.7 2.8 %copy-start.8 = (s32[8192]{0:T(1024)S(1)}, s32[8192]{0:T(1024)}, u32[]{:S(2)}) copy-start(s32[8192]{0:T(1024)} %param.23) | copy-start | bytes 98308
  53.7 7.2 %copy-start.5 = (s32[256,128]{1,0:T(8,128)S(1)}, s32[256,128]{1,0:T(8,128)}, u32[]{:S(2)}) copy-start(s32[256,128]{1,0:T(8,128)} %shard_map.159) | copy-start | bytes 393220
  62.2 5.4 %copy-start.4 = (f32[4,8192]{1,0:T(4,128)S(1)}, f32[4,8192]{1,0:T(4,128)}, u32[]{:S(2)}) copy-start(f32[4,8192]{1,0:T(4,128)} %shard_map.160) | copy-start | bytes 393220
  82.2 11.7 %copy-start = (bf16[1,72,8192]{2,1,0:T(8,128)(2,1)S(1)}, bf16[1,72,8192]{2,1,0:T(8,128)(2,1)}, u32[]{:S(2)}) copy-start(bf16[1,72,8192]{2,1,0:T(8,128)(2,1)} %fusion.4) | copy-start | bytes 3538948
  82.2 39.5 %all-to-all-start.2 = ((f32[5,128,512]{2,0,1:T(8,128)}), f32[5,128,512]{2,0,1:T(8,128)S(1)}, u32[]{:S(2)}, u32[]{:S(2)}) async-start(f32[5,128,512]{2,0,1:T(8,128)} %copy.45), calls=%async_computation.2 | async-start | bytes 4194304 | tf_op jit(solution)/shard_map/all_to_all | solution.py:277
  92.0 1.9 %copy-start.1 = (bf16[1,72,8192]{2,1,0:T(8,128)(2,1)S(1)}, bf16[1,72,8192]{2,1,0:T(8,128)(2,1)}, u32[]{:S(2)}) copy-start(bf16[1,72,8192]{2,1,0:T(8,128)(2,1)} %fusion.7) | copy-start | bytes 3538948
  92.0 2.0 %copy-start.2 = (bf16[1,72,8192]{2,1,0:T(8,128)(2,1)S(1)}, bf16[1,72,8192]{2,1,0:T(8,128)(2,1)}, u32[]{:S(2)}) copy-start(bf16[1,72,8192]{2,1,0:T(8,128)(2,1)} %fusion.5) | copy-start | bytes 3538948
  122.5 0.8 copy-start.9
  122.5 0.9 copy-start.10

commit v8 on v7

--- a/solution.py
+++ b/solution.py
@@ -261,7 +261,6 @@
         concat_axis=1,
         tiled=True,
     )
-    atmos_updated = diffuse_atmos(atmos_profiles, atmos_mixing, fluxes)
     win_local = jnp.einsum(
         "qt,fql->ftl", placement, arrived.reshape(4, slot_tiles, width), precision=highest
     )
@@ -274,6 +273,8 @@
     outgoing = jnp.concatenate([sea_share[None] * top[:, None, :], sea_share[None]], axis=0)
     partial = lane_scatter(outgoing.reshape(5, tile_count, width), order, keys, last, present)
     send_buffer = jnp.einsum("qt,ftc->fqc", placement, partial, precision=highest)
+    late_profiles, send_buffer = lax.optimization_barrier((atmos_profiles, send_buffer))
+    atmos_updated = diffuse_atmos(late_profiles, atmos_mixing, fluxes)
     returned = lax.all_to_all(
         send_buffer.reshape(5, devices, capacity),
         ("comp", "sub"),

time: 125 us -> 132 us (1.056)
  waiting for transfers between devices: 12.2 us -> 23.8 us
  starting transfers between devices: 31 us -> 26 us
    all_to_all x1, waiting for transfers between devices: 0.01 us -> 18.7 us  [per_device(): lax.all_to_all(served.reshape(4, devices, capacity), ('comp', 'sub'), spl...]
    all_to_all x1, waiting for transfers between devices: 12.2 us -> 5.06 us  [per_device(): lax.all_to_all(send_buffer.reshape(5, devices, capacity), ('comp', 'sub')...]
    all_to_all x1, starting transfers between devices: 9.76 us -> 4.77 us  [per_device(): lax.all_to_all(send_buffer.reshape(5, devices, capacity), ('comp', 'sub')...]
  transfers between devices with their start and end apart: 3 -> 3, of which waited for: 1 -> 2; matrix products, arithmetic and copies ran while one was open for 22% -> 21% of each run, Pallas kernels for 18% -> 17%
where the time goes in v8:
time: 132 us; the launch traced here: 131 us
  Pallas kernels  30.5 us (23%)
  starting transfers between devices  26 us (20%)
  waiting for transfers between devices  23.8 us (18%)
  other arithmetic  20.4 us (15%)
  matrix products  14.5 us (11%)
  local copies, waits for them, and re-layouts  14.4 us (11%)
    all_to_all x1, waiting for transfers between devices, per_device(): lax.all_to_all(served.reshape(4, devices, capacity), ('comp', 'sub'), spl...  18.7 us
    pallas_call x1, Pallas kernels, ocean_update(): pl.pallas_call(ocean_kernel, grid=(cells // block,), out_shape=jax.ShapeD...  13.1 us
    all_to_all x1, starting transfers between devices, per_device(): lax.all_to_all(request, ('comp', 'sub'), split_axis=0, concat_axis=0, til...  11.5 us
    all_to_all x1, starting transfers between devices, per_device(): lax.all_to_all(served.reshape(4, devices, capacity), ('comp', 'sub'), spl...  9.77 us
    dot_general x4, matrix products, diffuse_atmos(): jnp.dot(atmos_mixing, atmos_profiles[member], preferred_element_type=jnp....  9.08 us
    pallas_call x1, Pallas kernels, lane_scatter(): pl.pallas_call(lane_scatter_kernel, out_shape=jax.ShapeDtypeStruct(values...  5.82 us
    all_to_all x1, waiting for transfers between devices, per_device(): lax.all_to_all(send_buffer.reshape(5, devices, capacity), ('comp', 'sub')...  5.06 us
    pallas_call x1, Pallas kernels, top_level_mix(): pl.pallas_call(top_level_kernel, grid=(cells // block,), out_shape=jax.Sh...  4.83 us
  transfers between devices with their start and end apart: 3, of which 2 were waited for; matrix products, arithmetic and copies ran while one was open for 21% of the time, Pallas kernels for 17%

profile of v8, /device:TPU:1, one launch (start us, length us, event | category | flops | bytes accessed | tf_op | source)
XLA Modules:
  0.0 130.6 jit_solution(15322363722787464849)
XLA Ops:
  4.0 11.5 %all-to-all-start = ((s32[128,1,4]{2,1,0:T(1,128)}), s32[128,1,4]{2,1,0:T(1,128)S(1)}, u32[]{:S(2)}, u32[]{:S(2)}) async-start(s32[128,1,4]{2,1,0:T(1,128)} %bitcast.21), calls=%async_computation | async-start | bytes 131072 | tf_op jit(solution)/shard_map/all_to_all | solution.py:246
  21.4 1.4 %fusion.48 = (f32[1,8192]{1,0:T(1,128)S(1)}, f32[1,8192]{1,0:T(1,128)S(1)}, f32[1,8192]{1,0:T(1,128)S(1)}, f32[1,8192]{1,0:T(1,128)S(1)}) fusion(f32[4,1,8192]{2,1,0:T(1,128)S(1)} %slice_convert_fusion, f32[4,8192]{1,0:T(4,128)} %param.17), kind=kLoop, calls=%fused_computation.87 | loop fusion | flops 32768 | bytes 393216 | tf_op jit(solution)/shard_map/sub | solution.py:15
  22.9 4.4 %shard_map.157 = s32[256,128]{1,0:T(8,128)} custom-call(s32[256,128]{1,0:T(8,128)} %get-tuple-element.27.key_ref), custom_call_target="tpu_custom_call" | custom-call | tf_op jit(solution)/shard_map/pallas_call | solution.py:190
  27.3 4.4 %convert_reduce_fusion = s32[256,128]{1,0:T(8,128)S(1)} fusion(s32[256,128]{1,0:T(8,128)S(1)} %get-tuple-element.26.lanes_ref), kind=kLoop, calls=%fused_computation | loop fusion | flops 12550144 | bytes 262144 | tf_op jit(solution)/shard_map/reduce_sum | solution.py:234
  31.8 1.8 %add_select_fusion = (s32[256,128]{1,0:T(8,128)}, s32[256,128]{1,0:T(8,128)}, s32[256,128]{1,0:T(8,128)}, s32[256,128]{1,0:T(8,128)}) fusion(s32[256,128]{1,0:T(8,128)} %shard_map.157, s32[256,128]{1,0:T(8,128)S(1)} %convert_reduce_fusion, s32[256,127]{1,0:T(8,128)S(1)} %bitcast.146), kind=kLoop, calls=%fused_computation.40 | loop fusion | flops 720896 | bytes 916480 | tf_op jit(solution)/shard_map/jit(floor_divide)/jit(_where)/select_n | solution.py:233
  33.9 1.3 slice.111
  35.5 4.8 %shard_map.158 = f32[4,8192]{1,0:T(4,128)} custom-call(f32[60]{0:T(128)} %slice_bitcast_fusion.7.row_ref, f32[60,4,8192]{2,1,0:T(4,128)} %bitcast.142), custom_call_target="tpu_custom_call" | custom-call | flops 3932160 | bytes 7995392 | tf_op jit(solution)/shard_map/pallas_call | solution.py:122
  42.9 1.6 %copy.39 = f32[4,128,512]{2,0,1:T(4,128)} copy(f32[4,128,512]{2,1,0:T(8,128)S(1)} %reshape.124) | data formatting | bytes 2097152 | tf_op jit(solution)/shard_map/reshape | solution.py:258
  44.5 9.8 %all-to-all-start.1 = ((f32[4,128,512]{2,0,1:T(4,128)}), f32[4,128,512]{2,0,1:T(4,128)S(1)}, u32[]{:S(2)}, u32[]{:S(2)}) async-start(f32[4,128,512]{2,0,1:T(4,128)} %copy.39), calls=%async_computation.1 | async-start | bytes 2097152 | tf_op jit(solution)/shard_map/all_to_all | solution.py:257
  54.4 18.7 %all-to-all-done.1 = f32[4,128,512]{2,0,1:T(4,128)S(1)} async-done(((f32[4,128,512]{2,0,1:T(4,128)}), f32[4,128,512]{2,0,1:T(4,128)S(1)}, u32[]{:S(2)}, u32[]{:S(2)}) %all-to-all-start.1) | async-done | bytes 1048608 | tf_op jit(solution)/shard_map/all_to_all | solution.py:257
  73.5 1.5 %convolution_bitcast_fusion.6.win_ref = f32[4,256,128]{2,1,0:T(8,128)} fusion(f32[4,512,128]{2,1,0:T(8,128)S(1)} %reshape.125, s32[256]{0:T(256)S(1)} %and_select_fusion.1), kind=kOutput, calls=%fused_computation.21 | convolution fusion | flops 805437440 | bytes 1573888 | tf_op jit(solution)/shard_map/qt,fql->ftl/dot_general | solution.py:264
  75.0 2.3 %shard_map.159 = f32[4,256,128]{2,1,0:T(8,128)} custom-call(f32[4,256,128]{2,1,0:T(8,128)} %convolution_bitcast_fusion.6.win_ref, s32[256,128]{1,0:T(8,128)} %copy-done.2), custom_call_target="tpu_custom_call" | custom-call | tf_op jit(solution)/shard_map/pallas_call | solution.py:67
  78.9 2.3 %fusion.29 = (f32[4,8192]{1,0:T(4,128)S(1)}, f32[4,8192]{1,0:T(4,128)}) fusion(f32[60,4,8192]{2,1,0:T(4,128)} %bitcast.143, f32[4,8192]{1,0:T(4,128)S(1)} %copy-done.3, f32[]{:T(128)} %bitcast.2, pred[8192]{0:T(1024)(128)(4,1)S(1)} %broadcast_compare_fusion, f32[4,8192]{1,0:T(4,128)S(1)} %multiply_reduce_fusion, f32[8192]{0:T(1024)S(1)} %reduce_sum.29), kind=kLoop, calls=%fused_computation.53 | loop fusion | flops 131072 | bytes 696324 | tf_op jit(solution)/shard_map/jit(_where)/select_n | solution.py:271
  82.6 5.8 %shard_map.160 = f32[5,256,128]{2,1,0:T(8,128)} custom-call(s32[256,128]{1,0:T(8,128)} %get-tuple-element.29.order_ref, s32[256,128]{1,0:T(8,128)} %get-tuple-element.28.keys_ref, s32[256,128]{1,0:T(8,128)} %get-tuple-element.36.last_ref, s32[256,128]{1,0:T(8,128)} %get-tuple-element.37.present_ref, f32[5,256,128]{2,1,0:T(8,128)} %pad_maximum_fusion.1.val_ref), custom_call_target="tpu_custom_call" | custom-call | tf_op jit(solution)/shard_map/pallas_call | solution.py:160
  88.4 2.3 %convolution_bitcast_fusion.4 = f32[5,512,128]{1,2,0:T(8,128)S(1)} fusion(f32[5,256,128]{2,1,0:T(8,128)} %shard_map.160, s32[256]{0:T(256)S(1)} %and_select_fusion.1), kind=kOutput, calls=%fused_computation.19 | convolution fusion | flops 1006764032 | bytes 1967104 | tf_op jit(solution)/shard_map/qt,ftc->fqc/dot_general | solution.py:275
  91.4 2.2 %copy.45 = f32[5,128,512]{2,0,1:T(8,128)} copy(f32[5,128,512]{2,1,0:T(8,128)S(1)} %reshape.127) | data formatting | bytes 2621440 | tf_op jit(solution)/shard_map/reshape | solution.py:279
  93.5 4.8 %all-to-all-start.2 = ((f32[5,128,512]{2,0,1:T(8,128)}), f32[5,128,512]{2,0,1:T(8,128)S(1)}, u32[]{:S(2)}, u32[]{:S(2)}) async-start(f32[5,128,512]{2,0,1:T(8,128)} %copy.45), calls=%async_computation.2 | async-start | bytes 4194304 | tf_op jit(solution)/shard_map/all_to_all | solution.py:278
  98.3 1.7 %fusion.8 = bf16[1,72,8192]{2,1,0:T(8,128)(2,1)S(1)} fusion(bf16[72,72]{1,0:T(8,128)(2,1)S(1)} %copy-done.9, f32[8192]{0:T(1024)S(1)} %bitcast.166, bf16[4,72,8192]{2,1,0:T(8,128)(2,1)} %param.14, f32[72]{0:T(128)S(1)} %convert_reduce_fusion.1), kind=kOutput, calls=%fused_computation.14 | convolution fusion | flops 86704128 | bytes 2402720 | tf_op jit(solution)/shard_map/dot_general | solution.py:40
  100.0 2.7 %fusion.9 = bf16[1,72,8192]{2,1,0:T(8,128)(2,1)} fusion(bf16[72,72]{1,0:T(8,128)(2,1)S(1)} %copy-done.9, f32[8192]{0:T(1024)S(1)} %bitcast.165, bf16[4,72,8192]{2,1,0:T(8,128)(2,1)} %param.14, f32[72]{0:T(128)S(1)} %convert_reduce_fusion.1), kind=kOutput, calls=%fused_computation.15 | convolution fusion | flops 86704128 | bytes 2402720 | tf_op jit(solution)/shard_map/dot_general | solution.py:40
  102.8 2.7 %fusion.10 = bf16[1,72,8192]{2,1,0:T(8,128)(2,1)} fusion(bf16[72,72]{1,0:T(8,128)(2,1)S(1)} %copy-done.9, f32[8192]{0:T(1024)S(1)} %bitcast.164, bf16[4,72,8192]{2,1,0:T(8,128)(2,1)} %param.14, f32[72]{0:T(128)S(1)} %convert_reduce_fusion.1), kind=kOutput, calls=%fused_computation.16 | convolution fusion | flops 86704128 | bytes 2402720 | tf_op jit(solution)/shard_map/dot_general | solution.py:40
  105.5 13.1 %shard_map.161 = f32[60,4,8192]{2,1,0:T(4,128)} custom-call(f32[60,60]{1,0:T(8,128)} %m_ref.1, f32[60,1]{1,0:T(8,128)} %bitcast.154, f32[60,4,8192]{2,1,0:T(4,128)} %bitcast.144, f32[4,8192]{1,0:T(4,128)} %get-tuple-element.8.forcing_ref, s32[1,8192]{1,0:T(1,128)} %bitcast.148), custom_call_target="tpu_custom_call" | custom-call | flops 1415577600 | bytes 15728640 | tf_op jit(solution)/shard_map/pallas_call | solution.py:93
  118.6 1.9 %fusion.11 = bf16[1,72,8192]{2,1,0:T(8,128)(2,1)S(1)} fusion(bf16[72,72]{1,0:T(8,128)(2,1)S(1)} %copy-done.9, f32[8192]{0:T(1024)S(1)} %bitcast.163, f32[72]{0:T(128)S(1)} %convert_reduce_fusion.1, bf16[4,72,8192]{2,1,0:T(8,128)(2,1)} %param.14), kind=kOutput, calls=%fused_computation.17 | convolution fusion | flops 86704128 | bytes 2402720 | tf_op jit(solution)/shard_map/dot_general | solution.py:40
  120.6 2.5 %pad_maximum_fusion = bf16[4,72,8192]{2,1,0:T(8,128)(2,1)} fusion(bf16[1,72,8192]{2,1,0:T(8,128)(2,1)S(1)} %fusion.8, bf16[1,72,8192]{2,1,0:T(8,128)(2,1)S(1)} %copy-done, bf16[1,72,8192]{2,1,0:T(8,128)(2,1)S(1)} %copy-done.1, bf16[1,72,8192]{2,1,0:T(8,128)(2,1)S(1)} %fusion.11), kind=kLoop, calls=%fused_computation.18 | loop fusion | flops 7077888 | bytes 9437184 | tf_op jit(solution)/shard_map/stack | solution.py:44
  123.1 5.1 %all-to-all-done.2 = f32[5,128,512]{2,0,1:T(8,128)S(1)} async-done(((f32[5,128,512]{2,0,1:T(8,128)}), f32[5,128,512]{2,0,1:T(8,128)S(1)}, u32[]{:S(2)}, u32[]{:S(2)}) %all-to-all-start.2) | async-done | bytes 1310752 | tf_op jit(solution)/shard_map/all_to_all | solution.py:278
  (68 shorter events, 19.0 us)
Async XLA Ops:
  0.6 22.2 %copy-start.8 = (f32[8192]{0:T(1024)S(1)}, f32[8192]{0:T(1024)}, u32[]{:S(2)}) copy-start(f32[8192]{0:T(1024)} %param.16) | copy-start | bytes 98308
  0.6 31.1 %copy-start.7 = (f32[4,8192]{1,0:T(4,128)S(1)}, f32[4,8192]{1,0:T(4,128)}, u32[]{:S(2)}) copy-start(f32[4,8192]{1,0:T(4,128)} %param.27) | copy-start | bytes 393220
  2.8 30.9 %copy-start.9 = (bf16[72,72]{1,0:T(8,128)(2,1)S(1)}, bf16[72,72]{1,0:T(8,128)(2,1)}, u32[]{:S(2)}) copy-start(bf16[72,72]{1,0:T(8,128)(2,1)} %param.15) | copy-start | bytes 31108
  4.0 36.3 %all-to-all-start = ((s32[128,1,4]{2,1,0:T(1,128)}), s32[128,1,4]{2,1,0:T(1,128)S(1)}, u32[]{:S(2)}, u32[]{:S(2)}) async-start(s32[128,1,4]{2,1,0:T(1,128)} %bitcast.21), calls=%async_computation | async-start | bytes 131072 | tf_op jit(solution)/shard_map/all_to_all | solution.py:246
  15.5 19.8 %copy-start.4 = (f32[4,8192]{1,0:T(4,128)S(1)}, f32[4,8192]{1,0:T(4,128)}, u32[]{:S(2)}) copy-start(f32[4,8192]{1,0:T(4,128)} %param.26) | copy-start | bytes 393220
  17.8 22.5 %copy-start.2 = (s32[256,128]{1,0:T(8,128)}, s32[256,128]{1,0:T(8,128)S(1)}, u32[]{:S(2)}) copy-start(s32[256,128]{1,0:T(8,128)S(1)} %get-tuple-element.26.lanes_ref) | copy-start | bytes 393220
  44.5 28.6 %all-to-all-start.1 = ((f32[4,128,512]{2,0,1:T(4,128)}), f32[4,128,512]{2,0,1:T(4,128)S(1)}, u32[]{:S(2)}, u32[]{:S(2)}) async-start(f32[4,128,512]{2,0,1:T(4,128)} %copy.39), calls=%async_computation.1 | async-start | bytes 2097152 | tf_op jit(solution)/shard_map/all_to_all | solution.py:257
  73.5 5.4 %copy-start.3 = (f32[4,8192]{1,0:T(4,128)S(1)}, f32[4,8192]{1,0:T(4,128)}, u32[]{:S(2)}) copy-start(f32[4,8192]{1,0:T(4,128)} %shard_map.158) | copy-start | bytes 393220
  93.5 34.6 %all-to-all-start.2 = ((f32[5,128,512]{2,0,1:T(8,128)}), f32[5,128,512]{2,0,1:T(8,128)S(1)}, u32[]{:S(2)}, u32[]{:S(2)}) async-start(f32[5,128,512]{2,0,1:T(8,128)} %copy.45), calls=%async_computation.2 | async-start | bytes 4194304 | tf_op jit(solution)/shard_map/all_to_all | solution.py:278
  118.6 1.9 %copy-start = (bf16[1,72,8192]{2,1,0:T(8,128)(2,1)S(1)}, bf16[1,72,8192]{2,1,0:T(8,128)(2,1)}, u32[]{:S(2)}) copy-start(bf16[1,72,8192]{2,1,0:T(8,128)(2,1)} %fusion.9) | copy-start | bytes 3538948
  118.6 2.0 %copy-start.1 = (bf16[1,72,8192]{2,1,0:T(8,128)(2,1)S(1)}, bf16[1,72,8192]{2,1,0:T(8,128)(2,1)}, u32[]{:S(2)}) copy-start(bf16[1,72,8192]{2,1,0:T(8,128)(2,1)} %fusion.10) | copy-start | bytes 3538948
  128.9 0.8 copy-start.5
  128.9 0.9 copy-start.6

commit v9 on v8

--- a/solution.py
+++ b/solution.py
@@ -229,17 +229,8 @@
     tiles_pc = parent_column.reshape(tile_count, width)
     window_of_tile = tiles_pc[:, 0] // width
     lanes = tiles_pc % width
-    ranked = lane_sort(lanes * width + lax.broadcasted_iota(jnp.int32, lanes.shape, 1))
-    keys, order = ranked // width, ranked % width
-    at_most = jnp.sum(
-        (lanes[:, None, :] <= jnp.arange(width, dtype=jnp.int32)[None, :, None]).astype(jnp.int32),
-        axis=2,
-    )
-    present = at_most - jnp.pad(at_most[:, :-1], ((0, 0), (1, 0)))
-    last = jnp.maximum(at_most - 1, 0)
 
     state_by_level = jnp.transpose(ocean_state, (1, 0, 2))
-    base_top = top_level_mix(ocean_mixing[0], state_by_level)
 
     request = jnp.dot(placement, window_of_tile.astype(jnp.float32), precision=highest)
     request = (request + 0.5).astype(jnp.int32).reshape(devices, slot_tiles // devices)
@@ -254,6 +245,16 @@
     served = jnp.einsum(
         "qw,fwl->fql", window_hot, column_forcing.reshape(4, windows, width), precision=highest
     )
+    late_lanes, late_state, served = lax.optimization_barrier((lanes, state_by_level, served))
+    base_top = top_level_mix(ocean_mixing[0], late_state)
+    ranked = lane_sort(late_lanes * width + lax.broadcasted_iota(jnp.int32, late_lanes.shape, 1))
+    keys, order = ranked // width, ranked % width
+    at_most = jnp.sum(
+        (late_lanes[:, None, :] <= jnp.arange(width, dtype=jnp.int32)[None, :, None]).astype(jnp.int32),
+        axis=2,
+    )
+    present = at_most - jnp.pad(at_most[:, :-1], ((0, 0), (1, 0)))
+    last = jnp.maximum(at_most - 1, 0)
     arrived = lax.all_to_all(
         served.reshape(4, devices, capacity),
         ("comp", "sub"),

time: 132 us -> 116 us (0.88)
  waiting for transfers between devices: 23.8 us -> 9.88 us
  other arithmetic: 20.4 us -> 18.8 us
    all_to_all x1, waiting for transfers between devices: 18.7 us -> 1.74 us  [per_device(): lax.all_to_all(served.reshape(4, devices, capacity), ('comp', 'sub'), spl...]
    all_to_all x1, starting transfers between devices: 4.77 us -> 8.03 us  [per_device(): lax.all_to_all(send_buffer.reshape(5, devices, capacity), ('comp', 'sub')...]
    all_to_all x1, starting transfers between devices: 9.77 us -> 6.57 us  [per_device(): lax.all_to_all(served.reshape(4, devices, capacity), ('comp', 'sub'), spl...]
    all_to_all x1, waiting for transfers between devices: 0.01 us -> 3.19 us  [per_device(): lax.all_to_all(request, ('comp', 'sub'), split_axis=0, concat_axis=0, til...]
  transfers between devices with their start and end apart: 3 -> 3, of which waited for: 2 -> 3; matrix products, arithmetic and copies ran while one was open for 21% -> 22% of each run, Pallas kernels for 17% -> 19%
where the time goes in v9:
time: 116 us; the launch traced here: 115 us
  Pallas kernels  30.5 us (26%)
  starting transfers between devices  26.1 us (22%)
  other arithmetic  18.8 us (16%)
  local copies, waits for them, and re-layouts  14.5 us (12%)
  matrix products  14.5 us (12%)
  waiting for transfers between devices  9.88 us (9%)
    pallas_call x1, Pallas kernels, ocean_update(): pl.pallas_call(ocean_kernel, grid=(cells // block,), out_shape=jax.ShapeD...  13.1 us
    all_to_all x1, starting transfers between devices, per_device(): lax.all_to_all(request, ('comp', 'sub'), split_axis=0, concat_axis=0, til...  11.5 us
    dot_general x4, matrix products, diffuse_atmos(): jnp.dot(atmos_mixing, atmos_profiles[member], preferred_element_type=jnp....  9.08 us
    all_to_all x1, starting transfers between devices, per_device(): lax.all_to_all(send_buffer.reshape(5, devices, capacity), ('comp', 'sub')...  8.03 us
    all_to_all x1, starting transfers between devices, per_device(): lax.all_to_all(served.reshape(4, devices, capacity), ('comp', 'sub'), spl...  6.57 us
    pallas_call x1, Pallas kernels, lane_scatter(): pl.pallas_call(lane_scatter_kernel, out_shape=jax.ShapeDtypeStruct(values...  5.82 us
    all_to_all x1, waiting for transfers between devices, per_device(): lax.all_to_all(send_buffer.reshape(5, devices, capacity), ('comp', 'sub')...  4.94 us
    pallas_call x1, Pallas kernels, top_level_mix(): pl.pallas_call(top_level_kernel, grid=(cells // block,), out_shape=jax.Sh...  4.86 us
  transfers between devices with their start and end apart: 3, of which 3 were waited for; matrix products, arithmetic and copies ran while one was open for 22% of the time, Pallas kernels for 19%

profile of v9, /device:TPU:1, one launch (start us, length us, event | category | flops | bytes accessed | tf_op | source)
XLA Modules:
  0.0 115.3 jit_solution(17083678254442889142)
XLA Ops:
  4.0 11.5 %all-to-all-start = ((s32[128,1,4]{2,1,0:T(1,128)}), s32[128,1,4]{2,1,0:T(1,128)S(1)}, u32[]{:S(2)}, u32[]{:S(2)}) async-start(s32[128,1,4]{2,1,0:T(1,128)} %bitcast.19), calls=%async_computation | async-start | bytes 131072 | tf_op jit(solution)/shard_map/all_to_all | solution.py:237
  18.8 1.4 %fusion.48 = (f32[1,8192]{1,0:T(1,128)S(1)}, f32[1,8192]{1,0:T(1,128)S(1)}, f32[1,8192]{1,0:T(1,128)S(1)}, f32[1,8192]{1,0:T(1,128)S(1)}) fusion(f32[4,1,8192]{2,1,0:T(1,128)S(1)} %slice_convert_fusion, f32[4,8192]{1,0:T(4,128)} %param.17), kind=kLoop, calls=%fused_computation.87 | loop fusion | flops 32768 | bytes 393216 | tf_op jit(solution)/shard_map/sub | solution.py:15
  21.8 3.2 %all-to-all-done = s32[128,1,4]{2,1,0:T(1,128)S(1)} async-done(((s32[128,1,4]{2,1,0:T(1,128)}), s32[128,1,4]{2,1,0:T(1,128)S(1)}, u32[]{:S(2)}, u32[]{:S(2)}) %all-to-all-start) | async-done | bytes 2080 | tf_op jit(solution)/shard_map/all_to_all | solution.py:237
  27.6 1.6 %copy.39 = f32[4,128,512]{2,0,1:T(4,128)} copy(f32[4,128,512]{2,1,0:T(8,128)S(1)} %reshape.104) | data formatting | bytes 2097152 | tf_op jit(solution)/shard_map/reshape | solution.py:259
  29.3 6.6 %all-to-all-start.1 = ((f32[4,128,512]{2,0,1:T(4,128)}), f32[4,128,512]{2,0,1:T(4,128)S(1)}, u32[]{:S(2)}, u32[]{:S(2)}) async-start(f32[4,128,512]{2,0,1:T(4,128)} %copy.39), calls=%async_computation.1 | async-start | bytes 2097152 | tf_op jit(solution)/shard_map/all_to_all | solution.py:258
  36.0 1.3 %slice.130 = f32[1,1]{1,0:T(1,128)} slice(f32[60,60]{1,0:T(8,128)} %m_ref.1), slice={[0:1], [0:1]} | slice | bytes 8 | tf_op jit(solution)/shard_map/slice | solution.py:272
  38.3 4.4 %shard_map.157 = s32[256,128]{1,0:T(8,128)} custom-call(s32[256,128]{1,0:T(8,128)} %iota_add_fusion.key_ref), custom_call_target="tpu_custom_call" | custom-call | tf_op jit(solution)/shard_map/pallas_call | solution.py:190
  42.7 4.9 %shard_map.158 = f32[4,8192]{1,0:T(4,128)} custom-call(f32[60]{0:T(128)} %slice_bitcast_fusion.7.row_ref, f32[60,4,8192]{2,1,0:T(4,128)} %bitcast.142), custom_call_target="tpu_custom_call" | custom-call | flops 3932160 | bytes 7995392 | tf_op jit(solution)/shard_map/pallas_call | solution.py:122
  47.6 4.4 %convert_reduce_fusion = s32[256,128]{1,0:T(8,128)S(1)} fusion(s32[256,128]{1,0:T(8,128)S(1)} %add_select_fusion.2.lanes_ref), kind=kLoop, calls=%fused_computation | loop fusion | flops 12550144 | bytes 262144 | tf_op jit(solution)/shard_map/reduce_sum | solution.py:252
  52.9 1.7 %all-to-all-done.1 = f32[4,128,512]{2,0,1:T(4,128)S(1)} async-done(((f32[4,128,512]{2,0,1:T(4,128)}), f32[4,128,512]{2,0,1:T(4,128)S(1)}, u32[]{:S(2)}, u32[]{:S(2)}) %all-to-all-start.1) | async-done | bytes 1048608 | tf_op jit(solution)/shard_map/all_to_all | solution.py:258
  55.1 1.5 %convolution_bitcast_fusion.6.win_ref = f32[4,256,128]{2,1,0:T(8,128)} fusion(f32[4,512,128]{2,1,0:T(8,128)S(1)} %reshape.105, s32[256]{0:T(256)S(1)} %and_select_fusion.1), kind=kOutput, calls=%fused_computation.21 | convolution fusion | flops 805437440 | bytes 1573888 | tf_op jit(solution)/shard_map/qt,fql->ftl/dot_general | solution.py:265
  56.6 2.3 %shard_map.159 = f32[4,256,128]{2,1,0:T(8,128)} custom-call(f32[4,256,128]{2,1,0:T(8,128)} %convolution_bitcast_fusion.6.win_ref, s32[256,128]{1,0:T(8,128)} %copy-done), custom_call_target="tpu_custom_call" | custom-call | tf_op jit(solution)/shard_map/pallas_call | solution.py:67
  60.5 2.3 %fusion.29 = (f32[4,8192]{1,0:T(4,128)S(1)}, f32[4,8192]{1,0:T(4,128)}) fusion(f32[60,4,8192]{2,1,0:T(4,128)} %bitcast.143, f32[4,8192]{1,0:T(4,128)S(1)} %copy-done.3, f32[]{:T(128)} %bitcast.23, pred[8192]{0:T(1024)(128)(4,1)S(1)} %broadcast_compare_fusion, f32[4,8192]{1,0:T(4,128)S(1)} %multiply_reduce_fusion, f32[8192]{0:T(1024)S(1)} %reduce_sum.29), kind=kLoop, calls=%fused_computation.53 | loop fusion | flops 131072 | bytes 696324 | tf_op jit(solution)/shard_map/jit(_where)/select_n | solution.py:272
  64.2 5.8 %shard_map.160 = f32[5,256,128]{2,1,0:T(8,128)} custom-call(s32[256,128]{1,0:T(8,128)} %get-tuple-element.30.order_ref, s32[256,128]{1,0:T(8,128)} %get-tuple-element.29.keys_ref, s32[256,128]{1,0:T(8,128)} %get-tuple-element.40.last_ref, s32[256,128]{1,0:T(8,128)} %get-tuple-element.41.present_ref, f32[5,256,128]{2,1,0:T(8,128)} %pad_maximum_fusion.1.val_ref), custom_call_target="tpu_custom_call" | custom-call | tf_op jit(solution)/shard_map/pallas_call | solution.py:160
  70.0 2.3 %convolution_bitcast_fusion.4 = f32[5,512,128]{1,2,0:T(8,128)S(1)} fusion(f32[5,256,128]{2,1,0:T(8,128)} %shard_map.160, s32[256]{0:T(256)S(1)} %and_select_fusion.1), kind=kOutput, calls=%fused_computation.19 | convolution fusion | flops 1006764032 | bytes 1967104 | tf_op jit(solution)/shard_map/qt,ftc->fqc/dot_general | solution.py:276
  72.9 2.2 %copy.45 = f32[5,128,512]{2,0,1:T(8,128)} copy(f32[5,128,512]{2,1,0:T(8,128)S(1)} %reshape.107) | data formatting | bytes 2621440 | tf_op jit(solution)/shard_map/reshape | solution.py:280
  75.1 8.0 %all-to-all-start.2 = ((f32[5,128,512]{2,0,1:T(8,128)}), f32[5,128,512]{2,0,1:T(8,128)S(1)}, u32[]{:S(2)}, u32[]{:S(2)}) async-start(f32[5,128,512]{2,0,1:T(8,128)} %copy.45), calls=%async_computation.2 | async-start | bytes 4194304 | tf_op jit(solution)/shard_map/all_to_all | solution.py:279
  83.1 1.7 %fusion.8 = bf16[1,72,8192]{2,1,0:T(8,128)(2,1)S(1)} fusion(bf16[72,72]{1,0:T(8,128)(2,1)S(1)} %copy-done.11, f32[8192]{0:T(1024)S(1)} %bitcast.166, bf16[4,72,8192]{2,1,0:T(8,128)(2,1)} %param.14, f32[72]{0:T(128)S(1)} %convert_reduce_fusion.1), kind=kOutput, calls=%fused_computation.14 | convolution fusion | flops 86704128 | bytes 2402720 | tf_op jit(solution)/shard_map/dot_general | solution.py:40
  84.9 2.7 %fusion.9 = bf16[1,72,8192]{2,1,0:T(8,128)(2,1)} fusion(bf16[72,72]{1,0:T(8,128)(2,1)S(1)} %copy-done.11, f32[8192]{0:T(1024)S(1)} %bitcast.165, bf16[4,72,8192]{2,1,0:T(8,128)(2,1)} %param.14, f32[72]{0:T(128)S(1)} %convert_reduce_fusion.1), kind=kOutput, calls=%fused_computation.15 | convolution fusion | flops 86704128 | bytes 2402720 | tf_op jit(solution)/shard_map/dot_general | solution.py:40
  87.6 2.7 %fusion.10 = bf16[1,72,8192]{2,1,0:T(8,128)(2,1)} fusion(bf16[72,72]{1,0:T(8,128)(2,1)S(1)} %copy-done.11, f32[8192]{0:T(1024)S(1)} %bitcast.164, bf16[4,72,8192]{2,1,0:T(8,128)(2,1)} %param.14, f32[72]{0:T(128)S(1)} %convert_reduce_fusion.1), kind=kOutput, calls=%fused_computation.16 | convolution fusion | flops 86704128 | bytes 2402720 | tf_op jit(solution)/shard_map/dot_general | solution.py:40
  90.4 13.1 %shard_map.161 = f32[60,4,8192]{2,1,0:T(4,128)} custom-call(f32[60,60]{1,0:T(8,128)} %m_ref.1, f32[60,1]{1,0:T(8,128)} %bitcast.154, f32[60,4,8192]{2,1,0:T(4,128)} %bitcast.144, f32[4,8192]{1,0:T(4,128)} %get-tuple-element.14.forcing_ref, s32[1,8192]{1,0:T(1,128)} %bitcast.148), custom_call_target="tpu_custom_call" | custom-call | flops 1415577600 | bytes 15728640 | tf_op jit(solution)/shard_map/pallas_call | solution.py:93
  103.4 1.9 %fusion.11 = bf16[1,72,8192]{2,1,0:T(8,128)(2,1)S(1)} fusion(bf16[72,72]{1,0:T(8,128)(2,1)S(1)} %copy-done.11, f32[8192]{0:T(1024)S(1)} %bitcast.163, f32[72]{0:T(128)S(1)} %convert_reduce_fusion.1, bf16[4,72,8192]{2,1,0:T(8,128)(2,1)} %param.14), kind=kOutput, calls=%fused_computation.17 | convolution fusion | flops 86704128 | bytes 2402720 | tf_op jit(solution)/shard_map/dot_general | solution.py:40
  105.4 2.5 %pad_maximum_fusion = bf16[4,72,8192]{2,1,0:T(8,128)(2,1)} fusion(bf16[1,72,8192]{2,1,0:T(8,128)(2,1)S(1)} %fusion.8, bf16[1,72,8192]{2,1,0:T(8,128)(2,1)S(1)} %copy-done.1, bf16[1,72,8192]{2,1,0:T(8,128)(2,1)S(1)} %copy-done.2, bf16[1,72,8192]{2,1,0:T(8,128)(2,1)S(1)} %fusion.11), kind=kLoop, calls=%fused_computation.18 | loop fusion | flops 7077888 | bytes 9437184 | tf_op jit(solution)/shard_map/stack | solution.py:44
  107.9 4.9 %all-to-all-done.2 = f32[5,128,512]{2,0,1:T(8,128)S(1)} async-done(((f32[5,128,512]{2,0,1:T(8,128)}), f32[5,128,512]{2,0,1:T(8,128)S(1)}, u32[]{:S(2)}, u32[]{:S(2)}) %all-to-all-start.2) | async-done | bytes 1310752 | tf_op jit(solution)/shard_map/all_to_all | solution.py:279
  (73 shorter events, 19.3 us)
Async XLA Ops:
  0.6 19.6 %copy-start.10 = (f32[8192]{0:T(1024)S(1)}, f32[8192]{0:T(1024)}, u32[]{:S(2)}) copy-start(f32[8192]{0:T(1024)} %param.16) | copy-start | bytes 98308
  0.6 19.9 %copy-start.9 = (f32[4,8192]{1,0:T(4,128)S(1)}, f32[4,8192]{1,0:T(4,128)}, u32[]{:S(2)}) copy-start(f32[4,8192]{1,0:T(4,128)} %param.27) | copy-start | bytes 393220
  4.0 21.0 %all-to-all-start = ((s32[128,1,4]{2,1,0:T(1,128)}), s32[128,1,4]{2,1,0:T(1,128)S(1)}, u32[]{:S(2)}, u32[]{:S(2)}) async-start(s32[128,1,4]{2,1,0:T(1,128)} %bitcast.19), calls=%async_computation | async-start | bytes 131072 | tf_op jit(solution)/shard_map/all_to_all | solution.py:237
  15.6 32.0 %copy-start = (s32[256,128]{1,0:T(8,128)}, s32[256,128]{1,0:T(8,128)S(1)}, u32[]{:S(2)}) copy-start(s32[256,128]{1,0:T(8,128)S(1)} %add_select_fusion.2.lanes_ref) | copy-start | bytes 393220
  27.6 8.3 %copy-start.11 = (bf16[72,72]{1,0:T(8,128)(2,1)S(1)}, bf16[72,72]{1,0:T(8,128)(2,1)}, u32[]{:S(2)}) copy-start(bf16[72,72]{1,0:T(8,128)(2,1)} %param.15) | copy-start | bytes 31108
  27.6 9.9 %copy-start.5 = (f32[4,8192]{1,0:T(4,128)S(1)}, f32[4,8192]{1,0:T(4,128)}, u32[]{:S(2)}) copy-start(f32[4,8192]{1,0:T(4,128)} %param.26) | copy-start | bytes 393220
  27.6 10.0 %copy-start.6 = (s32[8192]{0:T(1024)S(1)}, s32[8192]{0:T(1024)}, u32[]{:S(2)}) copy-start(s32[8192]{0:T(1024)} %param.23) | copy-start | bytes 98308
  29.3 25.4 %all-to-all-start.1 = ((f32[4,128,512]{2,0,1:T(4,128)}), f32[4,128,512]{2,0,1:T(4,128)S(1)}, u32[]{:S(2)}, u32[]{:S(2)}) async-start(f32[4,128,512]{2,0,1:T(4,128)} %copy.39), calls=%async_computation.1 | async-start | bytes 2097152 | tf_op jit(solution)/shard_map/all_to_all | solution.py:258
  42.7 9.2 %copy-start.4 = (s32[256,128]{1,0:T(8,128)S(1)}, s32[256,128]{1,0:T(8,128)}, u32[]{:S(2)}) copy-start(s32[256,128]{1,0:T(8,128)} %shard_map.157) | copy-start | bytes 393220
  55.1 5.4 %copy-start.3 = (f32[4,8192]{1,0:T(4,128)S(1)}, f32[4,8192]{1,0:T(4,128)}, u32[]{:S(2)}) copy-start(f32[4,8192]{1,0:T(4,128)} %shard_map.158) | copy-start | bytes 393220
  75.1 37.7 %all-to-all-start.2 = ((f32[5,128,512]{2,0,1:T(8,128)}), f32[5,128,512]{2,0,1:T(8,128)S(1)}, u32[]{:S(2)}, u32[]{:S(2)}) async-start(f32[5,128,512]{2,0,1:T(8,128)} %copy.45), calls=%async_computation.2 | async-start | bytes 4194304 | tf_op jit(solution)/shard_map/all_to_all | solution.py:279
  103.4 1.9 %copy-start.1 = (bf16[1,72,8192]{2,1,0:T(8,128)(2,1)S(1)}, bf16[1,72,8192]{2,1,0:T(8,128)(2,1)}, u32[]{:S(2)}) copy-start(bf16[1,72,8192]{2,1,0:T(8,128)(2,1)} %fusion.9) | copy-start | bytes 3538948
  103.4 2.0 %copy-start.2 = (bf16[1,72,8192]{2,1,0:T(8,128)(2,1)S(1)}, bf16[1,72,8192]{2,1,0:T(8,128)(2,1)}, u32[]{:S(2)}) copy-start(bf16[1,72,8192]{2,1,0:T(8,128)(2,1)} %fusion.10) | copy-start | bytes 3538948
  113.6 0.8 copy-start.7
  113.6 0.9 copy-start.8

commit v10 on v9

--- a/solution.py
+++ b/solution.py
@@ -243,7 +243,7 @@
     fluxes = surface_fluxes(atmos_profiles, drag_factor, surface_before, downward_fluxes)
     column_forcing = forcing_rows(fluxes)
     served = jnp.einsum(
-        "qw,fwl->fql", window_hot, column_forcing.reshape(4, windows, width), precision=highest
+        "qw,fwl->qfl", window_hot, column_forcing.reshape(4, windows, width), precision=highest
     )
     late_lanes, late_state, served = lax.optimization_barrier((lanes, state_by_level, served))
     base_top = top_level_mix(ocean_mixing[0], late_state)
@@ -256,14 +256,10 @@
     present = at_most - jnp.pad(at_most[:, :-1], ((0, 0), (1, 0)))
     last = jnp.maximum(at_most - 1, 0)
     arrived = lax.all_to_all(
-        served.reshape(4, devices, capacity),
-        ("comp", "sub"),
-        split_axis=1,
-        concat_axis=1,
-        tiled=True,
+        served.reshape(devices, -1), ("comp", "sub"), split_axis=0, concat_axis=0, tiled=True
     )
     win_local = jnp.einsum(
-        "qt,fql->ftl", placement, arrived.reshape(4, slot_tiles, width), precision=highest
+        "qt,qfl->ftl", placement, arrived.reshape(slot_tiles, 4, width), precision=highest
     )
     at_cells = lane_gather(win_local, lanes).reshape(4, intersections, ocean_cells)
     forcing = jnp.sum(ocean_weight[None] * at_cells, axis=1) / jnp.sum(ocean_weight, axis=0)[None]
@@ -273,18 +269,14 @@
     sea_share = atmos_weight * sea_mask.astype(jnp.float32)[None, :]
     outgoing = jnp.concatenate([sea_share[None] * top[:, None, :], sea_share[None]], axis=0)
     partial = lane_scatter(outgoing.reshape(5, tile_count, width), order, keys, last, present)
-    send_buffer = jnp.einsum("qt,ftc->fqc", placement, partial, precision=highest)
+    send_buffer = jnp.einsum("qt,ftc->qfc", placement, partial, precision=highest)
     late_profiles, send_buffer = lax.optimization_barrier((atmos_profiles, send_buffer))
     atmos_updated = diffuse_atmos(late_profiles, atmos_mixing, fluxes)
     returned = lax.all_to_all(
-        send_buffer.reshape(5, devices, capacity),
-        ("comp", "sub"),
-        split_axis=1,
-        concat_axis=1,
-        tiled=True,
+        send_buffer.reshape(devices, -1), ("comp", "sub"), split_axis=0, concat_axis=0, tiled=True
     )
     summed = jnp.einsum(
-        "qw,fqc->fwc", window_hot, returned.reshape(5, slot_tiles, width), precision=highest
+        "qw,qfc->fwc", window_hot, returned.reshape(slot_tiles, 5, width), precision=highest
     ).reshape(5, columns)
     updated_by_level = ocean_update(ocean_mixing, state_by_level, forcing, sea_mask)
     ocean_updated = jnp.transpose(updated_by_level, (1, 0, 2))

time: 116 us -> 114 us (0.983)
  waiting for transfers between devices: 9.88 us -> 4.98 us
  other arithmetic: 18.8 us -> 22.8 us
    all_to_all x2, waiting for transfers between devices: 6.69 us -> 1.79 us  [the longest x1 1.79 us: per_device(): lax.all_to_all(served.reshape(devices, -1), ('comp', 'sub'), split_axis=0...]
    reshape x6 -> x1, local copies, waits for them, and re-layouts: 4.32 us -> 0.68 us  [per_device(): returned.reshape(slot_tiles, 5, width)]
    all_to_all x0 -> x1, other arithmetic: none -> 3.11 us  [per_device(): lax.all_to_all(send_buffer.reshape(devices, -1), ('comp', 'sub'), split_a...]
    optimization_barrier x1, local copies, waits for them, and re-layouts: 0.32 us -> 1.65 us  [per_device(): lax.optimization_barrier((lanes, state_by_level, served))]
    all_to_all x2 -> x1, local copies, waits for them, and re-layouts: 1.1 us -> 2.36 us  [per_device(): lax.all_to_all(send_buffer.reshape(devices, -1), ('comp', 'sub'), split_a...]
  transfers between devices with their start and end apart: 3 -> 3, of which waited for: 3 -> 2; matrix products, arithmetic and copies ran while one was open for 22% -> 22% of each run, Pallas kernels for 19% -> 20%
where the time goes in v10:
time: 114 us; the launch traced here: 113 us
  Pallas kernels  30.5 us (27%)
  starting transfers between devices  26.1 us (23%)
  other arithmetic  22.8 us (20%)
  matrix products  14.2 us (12%)
  local copies, waits for them, and re-layouts  13.7 us (12%)
  waiting for transfers between devices  4.98 us (4%)
    pallas_call x1, Pallas kernels, ocean_update(): pl.pallas_call(ocean_kernel, grid=(cells // block,), out_shape=jax.ShapeD...  13.1 us
    all_to_all x1, starting transfers between devices, per_device(): lax.all_to_all(request, ('comp', 'sub'), split_axis=0, concat_axis=0, til...  11.5 us
    dot_general x4, matrix products, diffuse_atmos(): jnp.dot(atmos_mixing, atmos_profiles[member], preferred_element_type=jnp....  9.09 us
    all_to_all x1, starting transfers between devices, per_device(): lax.all_to_all(send_buffer.reshape(devices, -1), ('comp', 'sub'), split_a...  7.99 us
    all_to_all x1, starting transfers between devices, per_device(): lax.all_to_all(served.reshape(devices, -1), ('comp', 'sub'), split_axis=0...  6.57 us
    pallas_call x1, Pallas kernels, lane_scatter(): pl.pallas_call(lane_scatter_kernel, out_shape=jax.ShapeDtypeStruct(values...  5.82 us
    pallas_call x1, Pallas kernels, top_level_mix(): pl.pallas_call(top_level_kernel, grid=(cells // block,), out_shape=jax.Sh...  4.86 us
    pallas_call x1, Pallas kernels, lane_sort(): pl.pallas_call(lane_sort_kernel, out_shape=jax.ShapeDtypeStruct(keys.shap...  4.44 us
  transfers between devices with their start and end apart: 3, of which 2 were waited for; matrix products, arithmetic and copies ran while one was open for 22% of the time, Pallas kernels for 20%

profile of v10, /device:TPU:1, one launch (start us, length us, event | category | flops | bytes accessed | tf_op | source)
XLA Modules:
  0.0 113.3 jit_solution(1864873833041217089)
XLA Ops:
  4.0 11.5 %all-to-all-start = ((s32[128,1,4]{2,1,0:T(1,128)}), s32[128,1,4]{2,1,0:T(1,128)S(1)}, u32[]{:S(2)}, u32[]{:S(2)}) async-start(s32[128,1,4]{2,1,0:T(1,128)} %bitcast.5), calls=%async_computation | async-start | bytes 131072 | tf_op jit(solution)/shard_map/all_to_all | solution.py:237
  18.8 1.4 %fusion.56 = (f32[1,8192]{1,0:T(1,128)S(1)}, f32[1,8192]{1,0:T(1,128)S(1)}, f32[1,8192]{1,0:T(1,128)S(1)}, f32[1,8192]{1,0:T(1,128)S(1)}) fusion(f32[4,1,8192]{2,1,0:T(1,128)S(1)} %slice_convert_fusion, f32[4,8192]{1,0:T(4,128)} %param.17), kind=kLoop, calls=%fused_computation.90 | loop fusion | flops 32768 | bytes 393216 | tf_op jit(solution)/shard_map/sub | solution.py:15
  21.8 3.2 %all-to-all-done = s32[128,1,4]{2,1,0:T(1,128)S(1)} async-done(((s32[128,1,4]{2,1,0:T(1,128)}), s32[128,1,4]{2,1,0:T(1,128)S(1)}, u32[]{:S(2)}, u32[]{:S(2)}) %all-to-all-start) | async-done | bytes 2080 | tf_op jit(solution)/shard_map/all_to_all | solution.py:237
  27.1 1.6 %copy.35 = f32[512,4,128]{2,1,0:T(4,128)} copy(f32[512,4,128]{2,0,1:T(8,128)S(1)} %fusion.37) | data formatting | bytes 2097152 | tf_op jit(solution)/shard_map/optimization_barrier | solution.py:248
  28.8 6.6 %all-to-all-start.1 = ((f32[128,1,2048]{2,1,0:T(1,128)}), f32[128,1,2048]{2,1,0:T(1,128)S(1)}, u32[]{:S(2)}, u32[]{:S(2)}) async-start(f32[128,1,2048]{2,1,0:T(1,128)} %bitcast.24), calls=%async_computation.1 | async-start | bytes 2097152 | tf_op jit(solution)/shard_map/all_to_all | solution.py:258
  37.8 4.4 %shard_map.157 = s32[256,128]{1,0:T(8,128)} custom-call(s32[256,128]{1,0:T(8,128)} %iota_add_fusion.key_ref), custom_call_target="tpu_custom_call" | custom-call | tf_op jit(solution)/shard_map/pallas_call | solution.py:190
  42.2 4.9 %shard_map.158 = f32[4,8192]{1,0:T(4,128)} custom-call(f32[60]{0:T(128)} %slice_bitcast_fusion.7.row_ref, f32[60,4,8192]{2,1,0:T(4,128)} %bitcast.138), custom_call_target="tpu_custom_call" | custom-call | flops 3932160 | bytes 7995392 | tf_op jit(solution)/shard_map/pallas_call | solution.py:122
  47.1 4.4 %convert_reduce_fusion = s32[256,128]{1,0:T(8,128)S(1)} fusion(s32[256,128]{1,0:T(8,128)S(1)} %add_select_fusion.2.lanes_ref), kind=kLoop, calls=%fused_computation | loop fusion | flops 12550144 | bytes 262144 | tf_op jit(solution)/shard_map/reduce_sum | solution.py:252
  52.4 1.8 %all-to-all-done.1 = f32[128,1,2048]{2,1,0:T(1,128)S(1)} async-done(((f32[128,1,2048]{2,1,0:T(1,128)}), f32[128,1,2048]{2,1,0:T(1,128)S(1)}, u32[]{:S(2)}, u32[]{:S(2)}) %all-to-all-start.1) | async-done | bytes 1048608 | tf_op jit(solution)/shard_map/all_to_all | solution.py:258
  54.2 1.5 %convolution_bitcast_fusion.4.win_ref = f32[4,256,128]{2,1,0:T(8,128)} fusion(f32[512,4,128]{2,1,0:T(4,128)S(1)} %bitcast.142, s32[256]{0:T(256)S(1)} %and_select_fusion.1), kind=kOutput, calls=%fused_computation.21 | convolution fusion | flops 805437440 | bytes 1573888 | tf_op jit(solution)/shard_map/qt,qfl->ftl/dot_general | solution.py:261
  55.7 2.3 %shard_map.159 = f32[4,256,128]{2,1,0:T(8,128)} custom-call(f32[4,256,128]{2,1,0:T(8,128)} %convolution_bitcast_fusion.4.win_ref, s32[256,128]{1,0:T(8,128)} %copy-done), custom_call_target="tpu_custom_call" | custom-call | tf_op jit(solution)/shard_map/pallas_call | solution.py:67
  59.6 2.3 %fusion.36 = (f32[4,8192]{1,0:T(4,128)S(1)}, f32[4,8192]{1,0:T(4,128)}) fusion(f32[60,4,8192]{2,1,0:T(4,128)} %bitcast.139, f32[4,8192]{1,0:T(4,128)S(1)} %copy-done.3, f32[]{:T(128)} %bitcast.23, pred[8192]{0:T(1024)(128)(4,1)S(1)} %broadcast_compare_fusion, f32[4,8192]{1,0:T(4,128)S(1)} %multiply_reduce_fusion, f32[8192]{0:T(1024)S(1)} %reduce_sum.29), kind=kLoop, calls=%fused_computation.55 | loop fusion | flops 131072 | bytes 696324 | tf_op jit(solution)/shard_map/jit(_where)/select_n | solution.py:268
  63.3 5.8 %shard_map.160 = f32[5,256,128]{2,1,0:T(8,128)} custom-call(s32[256,128]{1,0:T(8,128)} %get-tuple-element.30.order_ref, s32[256,128]{1,0:T(8,128)} %get-tuple-element.29.keys_ref, s32[256,128]{1,0:T(8,128)} %get-tuple-element.40.last_ref, s32[256,128]{1,0:T(8,128)} %get-tuple-element.41.present_ref, f32[5,256,128]{2,1,0:T(8,128)} %pad_maximum_fusion.1.val_ref), custom_call_target="tpu_custom_call" | custom-call | tf_op jit(solution)/shard_map/pallas_call | solution.py:160
  69.1 2.0 %fusion.28 = f32[512,5,128]{2,0,1:T(8,128)S(1)} fusion(f32[5,256,128]{2,1,0:T(8,128)} %shard_map.160, s32[256]{0:T(256)S(1)} %and_select_fusion.1), kind=kOutput, calls=%fused_computation.37 | convolution fusion | flops 1006764032 | bytes 1967104 | tf_op jit(solution)/shard_map/qt,ftc->qfc/dot_general | solution.py:272
  71.9 2.4 %all_to_all.24 = f32[128,1,2560]{2,1,0:T(1,128)} reshape(f32[512,5,128]{2,1,0:T(8,128)S(1)} %copy.39) | data formatting | bytes 2621440 | tf_op jit(solution)/shard_map/all_to_all | solution.py:275
  74.2 8.0 %all-to-all-start.2 = ((f32[128,1,2560]{2,1,0:T(1,128)}), f32[128,1,2560]{2,1,0:T(1,128)S(1)}, u32[]{:S(2)}, u32[]{:S(2)}) async-start(f32[128,1,2560]{2,1,0:T(1,128)} %all_to_all.24), calls=%async_computation.2 | async-start | bytes 2621440 | tf_op jit(solution)/shard_map/all_to_all | solution.py:275
  82.2 1.7 %fusion.8 = bf16[1,72,8192]{2,1,0:T(8,128)(2,1)S(1)} fusion(bf16[72,72]{1,0:T(8,128)(2,1)S(1)} %copy-done.10, f32[8192]{0:T(1024)S(1)} %bitcast.163, bf16[4,72,8192]{2,1,0:T(8,128)(2,1)} %param.14, f32[72]{0:T(128)S(1)} %convert_reduce_fusion.1), kind=kOutput, calls=%fused_computation.14 | convolution fusion | flops 86704128 | bytes 2402720 | tf_op jit(solution)/shard_map/dot_general | solution.py:40
  84.0 2.7 %fusion.9 = bf16[1,72,8192]{2,1,0:T(8,128)(2,1)} fusion(bf16[72,72]{1,0:T(8,128)(2,1)S(1)} %copy-done.10, f32[8192]{0:T(1024)S(1)} %bitcast.162, bf16[4,72,8192]{2,1,0:T(8,128)(2,1)} %param.14, f32[72]{0:T(128)S(1)} %convert_reduce_fusion.1), kind=kOutput, calls=%fused_computation.15 | convolution fusion | flops 86704128 | bytes 2402720 | tf_op jit(solution)/shard_map/dot_general | solution.py:40
  86.7 2.7 %fusion.10 = bf16[1,72,8192]{2,1,0:T(8,128)(2,1)} fusion(bf16[72,72]{1,0:T(8,128)(2,1)S(1)} %copy-done.10, f32[8192]{0:T(1024)S(1)} %bitcast.161, bf16[4,72,8192]{2,1,0:T(8,128)(2,1)} %param.14, f32[72]{0:T(128)S(1)} %convert_reduce_fusion.1), kind=kOutput, calls=%fused_computation.16 | convolution fusion | flops 86704128 | bytes 2402720 | tf_op jit(solution)/shard_map/dot_general | solution.py:40
  89.5 13.1 %shard_map.161 = f32[60,4,8192]{2,1,0:T(4,128)} custom-call(f32[60,60]{1,0:T(8,128)} %m_ref.1, f32[60,1]{1,0:T(8,128)} %bitcast.151, f32[60,4,8192]{2,1,0:T(4,128)} %bitcast.140, f32[4,8192]{1,0:T(4,128)} %get-tuple-element.14.forcing_ref, s32[1,8192]{1,0:T(1,128)} %bitcast.145), custom_call_target="tpu_custom_call" | custom-call | flops 1415577600 | bytes 15728640 | tf_op jit(solution)/shard_map/pallas_call | solution.py:93
  102.6 1.9 %fusion.11 = bf16[1,72,8192]{2,1,0:T(8,128)(2,1)S(1)} fusion(bf16[72,72]{1,0:T(8,128)(2,1)S(1)} %copy-done.10, f32[8192]{0:T(1024)S(1)} %bitcast.160, f32[72]{0:T(128)S(1)} %convert_reduce_fusion.1, bf16[4,72,8192]{2,1,0:T(8,128)(2,1)} %param.14), kind=kOutput, calls=%fused_computation.17 | convolution fusion | flops 86704128 | bytes 2402720 | tf_op jit(solution)/shard_map/dot_general | solution.py:40
  104.5 2.5 %pad_maximum_fusion = bf16[4,72,8192]{2,1,0:T(8,128)(2,1)} fusion(bf16[1,72,8192]{2,1,0:T(8,128)(2,1)S(1)} %fusion.8, bf16[1,72,8192]{2,1,0:T(8,128)(2,1)S(1)} %copy-done.1, bf16[1,72,8192]{2,1,0:T(8,128)(2,1)S(1)} %copy-done.2, bf16[1,72,8192]{2,1,0:T(8,128)(2,1)S(1)} %fusion.11), kind=kLoop, calls=%fused_computation.18 | loop fusion | flops 7077888 | bytes 9437184 | tf_op jit(solution)/shard_map/stack | solution.py:44
  107.0 3.1 %reduce.3 = f32[128,2560]{1,0:T(8,128)S(1)} reduce(f32[128,1,2560]{2,1,0:T(1,128)S(1)} %all-to-all-done.2, f32[]{:T(128)} %constant.66), dimensions={1}, to_apply=%all_to_all.23.reduce_sub_computation | reduce | bytes 2621444 | tf_op jit(solution)/shard_map/all_to_all | solution.py:275
  111.6 1.7 %fusion.35 = f32[4,8192]{1,0:T(4,128)} fusion(f32[1,4,64,128]{3,2,1,0:T(8,128)S(1)} %slice_bitcast_fusion, f32[4,8192]{1,0:T(4,128)} %param.20, f32[8192]{0:T(1024)S(1)} %fusion.52, f32[8192]{0:T(1024)S(1)} %copy-done.7), kind=kLoop, calls=%fused_computation.52 | loop fusion | flops 98304 | bytes 458752 | tf_op jit(solution)/shard_map/div | solution.py:283
  (66 shorter events, 18.8 us)
Async XLA Ops:
  0.6 19.6 %copy-start.9 = (f32[8192]{0:T(1024)S(1)}, f32[8192]{0:T(1024)}, u32[]{:S(2)}) copy-start(f32[8192]{0:T(1024)} %param.16) | copy-start | bytes 98308
  0.6 19.9 %copy-start.8 = (f32[4,8192]{1,0:T(4,128)S(1)}, f32[4,8192]{1,0:T(4,128)}, u32[]{:S(2)}) copy-start(f32[4,8192]{1,0:T(4,128)} %param.27) | copy-start | bytes 393220
  4.0 21.0 %all-to-all-start = ((s32[128,1,4]{2,1,0:T(1,128)}), s32[128,1,4]{2,1,0:T(1,128)S(1)}, u32[]{:S(2)}, u32[]{:S(2)}) async-start(s32[128,1,4]{2,1,0:T(1,128)} %bitcast.5), calls=%async_computation | async-start | bytes 131072 | tf_op jit(solution)/shard_map/all_to_all | solution.py:237
  15.6 31.5 %copy-start = (s32[256,128]{1,0:T(8,128)}, s32[256,128]{1,0:T(8,128)S(1)}, u32[]{:S(2)}) copy-start(s32[256,128]{1,0:T(8,128)S(1)} %add_select_fusion.2.lanes_ref) | copy-start | bytes 393220
  27.1 8.3 %copy-start.10 = (bf16[72,72]{1,0:T(8,128)(2,1)S(1)}, bf16[72,72]{1,0:T(8,128)(2,1)}, u32[]{:S(2)}) copy-start(bf16[72,72]{1,0:T(8,128)(2,1)} %param.15) | copy-start | bytes 31108
  27.1 9.9 %copy-start.5 = (f32[4,8192]{1,0:T(4,128)S(1)}, f32[4,8192]{1,0:T(4,128)}, u32[]{:S(2)}) copy-start(f32[4,8192]{1,0:T(4,128)} %param.26) | copy-start | bytes 393220
  27.1 10.0 %copy-start.6 = (s32[8192]{0:T(1024)S(1)}, s32[8192]{0:T(1024)}, u32[]{:S(2)}) copy-start(s32[8192]{0:T(1024)} %param.23) | copy-start | bytes 98308
  28.8 25.4 %all-to-all-start.1 = ((f32[128,1,2048]{2,1,0:T(1,128)}), f32[128,1,2048]{2,1,0:T(1,128)S(1)}, u32[]{:S(2)}, u32[]{:S(2)}) async-start(f32[128,1,2048]{2,1,0:T(1,128)} %bitcast.24), calls=%async_computation.1 | async-start | bytes 2097152 | tf_op jit(solution)/shard_map/all_to_all | solution.py:258
  42.2 9.2 %copy-start.4 = (s32[256,128]{1,0:T(8,128)S(1)}, s32[256,128]{1,0:T(8,128)}, u32[]{:S(2)}) copy-start(s32[256,128]{1,0:T(8,128)} %shard_map.157) | copy-start | bytes 393220
  52.4 7.2 %copy-start.3 = (f32[4,8192]{1,0:T(4,128)S(1)}, f32[4,8192]{1,0:T(4,128)}, u32[]{:S(2)}) copy-start(f32[4,8192]{1,0:T(4,128)} %shard_map.158) | copy-start | bytes 393220
  74.2 32.8 %all-to-all-start.2 = ((f32[128,1,2560]{2,1,0:T(1,128)}), f32[128,1,2560]{2,1,0:T(1,128)S(1)}, u32[]{:S(2)}, u32[]{:S(2)}) async-start(f32[128,1,2560]{2,1,0:T(1,128)} %all_to_all.24), calls=%async_computation.2 | async-start | bytes 2621440 | tf_op jit(solution)/shard_map/all_to_all | solution.py:275
  102.6 1.9 %copy-start.1 = (bf16[1,72,8192]{2,1,0:T(8,128)(2,1)S(1)}, bf16[1,72,8192]{2,1,0:T(8,128)(2,1)}, u32[]{:S(2)}) copy-start(bf16[1,72,8192]{2,1,0:T(8,128)(2,1)} %fusion.9) | copy-start | bytes 3538948
  102.6 2.0 %copy-start.2 = (bf16[1,72,8192]{2,1,0:T(8,128)(2,1)S(1)}, bf16[1,72,8192]{2,1,0:T(8,128)(2,1)}, u32[]{:S(2)}) copy-start(bf16[1,72,8192]{2,1,0:T(8,128)(2,1)} %fusion.10) | copy-start | bytes 3538948
  110.1 1.4 %copy-start.7 = (f32[8192]{0:T(1024)S(1)}, f32[8192]{0:T(1024)}, u32[]{:S(2)}) copy-start(f32[8192]{0:T(1024)} %param.19) | copy-start | bytes 98308

commit v11 on v10

--- a/solution.py
+++ b/solution.py
@@ -32,16 +32,36 @@
     )
 
 
-def diffuse_atmos(atmos_profiles, atmos_mixing, fluxes):
-    lowest = atmos_mixing[:, -1].astype(jnp.float32)
+def atmos_kernel(mix_ref, low_ref, tend_ref, x_ref, out_ref):
+    mix = mix_ref[...]
+    low = low_ref[...]
+    for member in range(x_ref.shape[0]):
+        mixed = jnp.dot(mix, x_ref[member], preferred_element_type=jnp.float32)
+        mixed = mixed + low * tend_ref[member : member + 1, :]
+        out_ref[member] = mixed.astype(out_ref.dtype)
+
+
+def diffuse_atmos(atmos_profiles, atmos_mixing, fluxes, block=2048):
+    members, levels, columns = atmos_profiles.shape
+    lowest = atmos_mixing[:, -1:].astype(jnp.float32)
     tendency = couple_rate * jnp.stack([fluxes[0], fluxes[1], -fluxes[2], -fluxes[3]])
-    result = []
-    for member in range(4):
-        mixed_rows = jnp.dot(
-            atmos_mixing, atmos_profiles[member], preferred_element_type=jnp.float32
-        )
-        result.append(mixed_rows + lowest[:, None] * tendency[member][None, :])
-    return jnp.stack(result).astype(jnp.bfloat16)
+    return pl.pallas_call(
+        atmos_kernel,
+        grid=(columns // block,),
+        out_shape=jax.ShapeDtypeStruct(atmos_profiles.shape, jnp.bfloat16),
+        in_specs=[
+            pl.BlockSpec((levels, levels), lambda i: (0, 0)),
+            pl.BlockSpec((levels, 1), lambda i: (0, 0)),
+            pl.BlockSpec((members, block), lambda i: (0, i)),
+            pl.BlockSpec((members, levels, block), lambda i: (0, 0, i)),
+        ],
+        out_specs=pl.BlockSpec((members, levels, block), lambda i: (0, 0, i)),
+        cost_estimate=pl.CostEstimate(
+            flops=2 * members * levels * levels * columns,
+            bytes_accessed=4 * members * levels * columns,
+            transcendentals=0,
+        ),
+    )(atmos_mixing, lowest, tendency, atmos_profiles)
 
 
 def forcing_rows(fluxes):

time: 114 us -> 111 us (0.974)
  matrix products: 14.2 us -> 5.14 us
  Pallas kernels: 30.5 us -> 36.4 us
  waiting for transfers between devices: 4.98 us -> 6.35 us
  other arithmetic: 22.8 us -> 21.5 us
    dot_general x4 -> x0, matrix products: 9.09 us -> none  [diffuse_atmos(): jnp.dot(atmos_mixing, atmos_profiles[member], preferred_element_type=jnp....]
    pallas_call x0 -> x1, Pallas kernels: none -> 5.95 us  [diffuse_atmos(): pl.pallas_call(atmos_kernel, grid=(columns // block,), out_shape=jax.Shap...]
    another operation x1 -> x0, other arithmetic: 2.48 us -> none  [diffuse_atmos(): return jnp.stack(result).astype(jnp.bfloat16)]
    all_to_all x1, waiting for transfers between devices: 3.19 us -> 4.7 us  [per_device(): lax.all_to_all(request, ('comp', 'sub'), split_axis=0, concat_axis=0, til...]
    all_to_all x1, starting transfers between devices: 6.57 us -> 5.08 us  [per_device(): lax.all_to_all(served.reshape(devices, -1), ('comp', 'sub'), split_axis=0...]
  transfers between devices with their start and end apart: 3 -> 3, of which waited for: 2 -> 3; matrix products, arithmetic and copies ran while one was open for 22% -> 14% of each run, Pallas kernels for 20% -> 26%
where the time goes in v11:
time: 111 us; the launch traced here: 110 us
  Pallas kernels  36.4 us (33%)
  starting transfers between devices  25.6 us (23%)
  other arithmetic  21.5 us (19%)
  local copies, waits for them, and re-layouts  13.5 us (12%)
  waiting for transfers between devices  6.35 us (6%)
  matrix products  5.14 us (5%)
    pallas_call x1, Pallas kernels, ocean_update(): pl.pallas_call(ocean_kernel, grid=(cells // block,), out_shape=jax.ShapeD...  13.1 us
    all_to_all x1, starting transfers between devices, per_device(): lax.all_to_all(request, ('comp', 'sub'), split_axis=0, concat_axis=0, til...  11.5 us
    all_to_all x1, starting transfers between devices, per_device(): lax.all_to_all(send_buffer.reshape(devices, -1), ('comp', 'sub'), split_a...  9.06 us
    pallas_call x1, Pallas kernels, diffuse_atmos(): pl.pallas_call(atmos_kernel, grid=(columns // block,), out_shape=jax.Shap...  5.95 us
    pallas_call x1, Pallas kernels, lane_scatter(): pl.pallas_call(lane_scatter_kernel, out_shape=jax.ShapeDtypeStruct(values...  5.82 us
    all_to_all x1, starting transfers between devices, per_device(): lax.all_to_all(served.reshape(devices, -1), ('comp', 'sub'), split_axis=0...  5.08 us
    pallas_call x1, Pallas kernels, top_level_mix(): pl.pallas_call(top_level_kernel, grid=(cells // block,), out_shape=jax.Sh...  4.86 us
    all_to_all x1, waiting for transfers between devices, per_device(): lax.all_to_all(request, ('comp', 'sub'), split_axis=0, concat_axis=0, til...  4.7 us
  transfers between devices with their start and end apart: 3, of which 3 were waited for; matrix products, arithmetic and copies ran while one was open for 14% of the time, Pallas kernels for 26%

profile of v11, /device:TPU:1, one launch (start us, length us, event | category | flops | bytes accessed | tf_op | source)
XLA Modules:
  0.0 109.5 jit_solution(8837320379135313542)
XLA Ops:
  4.0 11.5 %all-to-all-start = ((s32[128,1,4]{2,1,0:T(1,128)}), s32[128,1,4]{2,1,0:T(1,128)S(1)}, u32[]{:S(2)}, u32[]{:S(2)}) async-start(s32[128,1,4]{2,1,0:T(1,128)} %bitcast.17), calls=%async_computation | async-start | bytes 131072 | tf_op jit(solution)/shard_map/all_to_all | solution.py:257
  16.4 1.2 %fusion.40 = (f32[1,8192]{1,0:T(1,128)S(1)}, f32[1,8192]{1,0:T(1,128)S(1)}, f32[1,8192]{1,0:T(1,128)S(1)}) fusion(f32[4,8192]{1,0:T(4,128)} %param.18), kind=kLoop, calls=%fused_computation.88 | loop fusion | flops 8192 | bytes 229376 | tf_op jit(solution)/shard_map/slice | solution.py:29
  17.6 1.1 %slice_convert_fusion = f32[4,1,8192]{2,1,0:T(1,128)S(1)} fusion(bf16[4,72,8192]{2,1,0:T(8,128)(2,1)} %x_ref), kind=kLoop, calls=%fused_computation.46 | loop fusion | flops 32768 | bytes 196608 | tf_op jit(solution)/shard_map/convert_element_type | solution.py:14
  18.8 1.4 %fusion.36 = (f32[1,8192]{1,0:T(1,128)S(1)}, f32[1,8192]{1,0:T(1,128)S(1)}, f32[1,8192]{1,0:T(1,128)S(1)}, f32[1,8192]{1,0:T(1,128)S(1)}) fusion(f32[4,1,8192]{2,1,0:T(1,128)S(1)} %slice_convert_fusion, f32[4,8192]{1,0:T(4,128)} %param.17), kind=kLoop, calls=%fused_computation.64 | loop fusion | flops 32768 | bytes 393216 | tf_op jit(solution)/shard_map/sub | solution.py:15
  20.3 4.7 %all-to-all-done = s32[128,1,4]{2,1,0:T(1,128)S(1)} async-done(((s32[128,1,4]{2,1,0:T(1,128)}), s32[128,1,4]{2,1,0:T(1,128)S(1)}, u32[]{:S(2)}, u32[]{:S(2)}) %all-to-all-start) | async-done | bytes 2080 | tf_op jit(solution)/shard_map/all_to_all | solution.py:257
  27.1 1.6 %copy.35 = f32[512,4,128]{2,1,0:T(4,128)} copy(f32[512,4,128]{2,0,1:T(8,128)S(1)} %fusion.17) | data formatting | bytes 2097152 | tf_op jit(solution)/shard_map/optimization_barrier | solution.py:268
  28.8 5.1 %all-to-all-start.1 = ((f32[128,1,2048]{2,1,0:T(1,128)}), f32[128,1,2048]{2,1,0:T(1,128)S(1)}, u32[]{:S(2)}, u32[]{:S(2)}) async-start(f32[128,1,2048]{2,1,0:T(1,128)} %bitcast.28), calls=%async_computation.1 | async-start | bytes 2097152 | tf_op jit(solution)/shard_map/all_to_all | solution.py:278
  33.9 1.3 %slice_bitcast_fusion.7.row_ref = f32[60]{0:T(128)} fusion(f32[60,60]{1,0:T(8,128)} %m_ref.1), kind=kLoop, calls=%fused_computation.85 | loop fusion | bytes 480 | tf_op jit(solution)/shard_map/squeeze | solution.py:269
  35.1 1.2 %slice.107 = f32[1,1]{1,0:T(1,128)} slice(f32[60,60]{1,0:T(8,128)} %m_ref.1), slice={[0:1], [0:1]} | slice | bytes 8 | tf_op jit(solution)/shard_map/slice | solution.py:288
  37.3 4.4 %shard_map.157 = s32[256,128]{1,0:T(8,128)} custom-call(s32[256,128]{1,0:T(8,128)} %iota_add_fusion.key_ref), custom_call_target="tpu_custom_call" | custom-call | tf_op jit(solution)/shard_map/pallas_call | solution.py:210
  41.8 4.9 %shard_map.158 = f32[4,8192]{1,0:T(4,128)} custom-call(f32[60]{0:T(128)} %slice_bitcast_fusion.7.row_ref, f32[60,4,8192]{2,1,0:T(4,128)} %bitcast.78), custom_call_target="tpu_custom_call" | custom-call | flops 3932160 | bytes 7995392 | tf_op jit(solution)/shard_map/pallas_call | solution.py:142
  46.6 4.4 %convert_reduce_fusion = s32[256,128]{1,0:T(8,128)S(1)} fusion(s32[256,128]{1,0:T(8,128)S(1)} %add_select_fusion.2.lanes_ref), kind=kLoop, calls=%fused_computation | loop fusion | flops 12550144 | bytes 262144 | tf_op jit(solution)/shard_map/reduce_sum | solution.py:272
  52.6 1.5 %convolution_bitcast_fusion.win_ref = f32[4,256,128]{2,1,0:T(8,128)} fusion(f32[512,4,128]{2,1,0:T(4,128)S(1)} %bitcast.82, s32[256]{0:T(256)S(1)} %and_select_fusion.1), kind=kOutput, calls=%fused_computation.4 | convolution fusion | flops 805437440 | bytes 1573888 | tf_op jit(solution)/shard_map/qt,qfl->ftl/dot_general | solution.py:281
  54.2 2.3 %shard_map.159 = f32[4,256,128]{2,1,0:T(8,128)} custom-call(f32[4,256,128]{2,1,0:T(8,128)} %convolution_bitcast_fusion.win_ref, s32[256,128]{1,0:T(8,128)} %copy-done), custom_call_target="tpu_custom_call" | custom-call | tf_op jit(solution)/shard_map/pallas_call | solution.py:87
  56.5 1.2 %reshape.109 = f32[4,4,8192]{2,1,0:T(4,128)S(1)} reshape(f32[4,256,128]{2,1,0:T(8,128)} %shard_map.159) | data formatting | bytes 1048576 | tf_op jit(solution)/shard_map/reshape | solution.py:284
  58.1 2.3 %fusion.16 = (f32[4,8192]{1,0:T(4,128)S(1)}, f32[4,8192]{1,0:T(4,128)}) fusion(f32[60,4,8192]{2,1,0:T(4,128)} %bitcast.79, f32[4,8192]{1,0:T(4,128)S(1)} %copy-done.1, f32[]{:T(128)} %bitcast.27, pred[8192]{0:T(1024)(128)(4,1)S(1)} %broadcast_compare_fusion, f32[4,8192]{1,0:T(4,128)S(1)} %multiply_reduce_fusion, f32[8192]{0:T(1024)S(1)} %reduce_sum.29), kind=kLoop, calls=%fused_computation.30 | loop fusion | flops 131072 | bytes 696324 | tf_op jit(solution)/shard_map/jit(_where)/select_n | solution.py:288
  61.8 5.8 %shard_map.160 = f32[5,256,128]{2,1,0:T(8,128)} custom-call(s32[256,128]{1,0:T(8,128)} %get-tuple-element.26.order_ref, s32[256,128]{1,0:T(8,128)} %get-tuple-element.25.keys_ref, s32[256,128]{1,0:T(8,128)} %get-tuple-element.36.last_ref, s32[256,128]{1,0:T(8,128)} %get-tuple-element.37.present_ref, f32[5,256,128]{2,1,0:T(8,128)} %pad_maximum_fusion.val_ref), custom_call_target="tpu_custom_call" | custom-call | tf_op jit(solution)/shard_map/pallas_call | solution.py:180
  67.6 2.0 %fusion.8 = f32[512,5,128]{2,0,1:T(8,128)S(1)} fusion(f32[5,256,128]{2,1,0:T(8,128)} %shard_map.160, s32[256]{0:T(256)S(1)} %and_select_fusion.1), kind=kOutput, calls=%fused_computation.12 | convolution fusion | flops 1006764032 | bytes 1967104 | tf_op jit(solution)/shard_map/qt,ftc->qfc/dot_general | solution.py:292
  70.4 2.4 %all_to_all.24 = f32[128,1,2560]{2,1,0:T(1,128)} reshape(f32[512,5,128]{2,1,0:T(8,128)S(1)} %copy.39) | data formatting | bytes 2621440 | tf_op jit(solution)/shard_map/all_to_all | solution.py:295
  72.7 9.1 %all-to-all-start.2 = ((f32[128,1,2560]{2,1,0:T(1,128)}), f32[128,1,2560]{2,1,0:T(1,128)S(1)}, u32[]{:S(2)}, u32[]{:S(2)}) async-start(f32[128,1,2560]{2,1,0:T(1,128)} %all_to_all.24), calls=%async_computation.2 | async-start | bytes 2621440 | tf_op jit(solution)/shard_map/all_to_all | solution.py:295
  83.3 5.9 %shard_map.161 = bf16[4,72,8192]{2,1,0:T(8,128)(2,1)} custom-call(bf16[72,72]{1,0:T(8,128)(2,1)} %mix_ref.1, f32[72,1]{1,0:T(8,128)} %slice_convert_fusion.1.low_ref, f32[4,8192]{1,0:T(4,128)} %maximum_multiply_fusion.tend_ref, bf16[4,72,8192]{2,1,0:T(8,128)(2,1)} %x_ref), custom_call_target="tpu_custom_call" | custom-call | flops 339738624 | bytes 9437184 | tf_op jit(solution)/shard_map/pallas_call | solution.py:48
  89.2 13.1 %shard_map.162 = f32[60,4,8192]{2,1,0:T(4,128)} custom-call(f32[60,60]{1,0:T(8,128)} %m_ref.1, f32[60,1]{1,0:T(8,128)} %bitcast.91, f32[60,4,8192]{2,1,0:T(4,128)} %bitcast.80, f32[4,8192]{1,0:T(4,128)} %get-tuple-element.14.forcing_ref, s32[1,8192]{1,0:T(1,128)} %bitcast.85), custom_call_target="tpu_custom_call" | custom-call | flops 1415577600 | bytes 15728640 | tf_op jit(solution)/shard_map/pallas_call | solution.py:113
  103.3 3.1 %reduce.2 = f32[128,2560]{1,0:T(8,128)S(1)} reduce(f32[128,1,2560]{2,1,0:T(1,128)S(1)} %all-to-all-done.2, f32[]{:T(128)} %constant.66), dimensions={1}, to_apply=%all_to_all.23.reduce_sub_computation | reduce | bytes 2621444 | tf_op jit(solution)/shard_map/all_to_all | solution.py:295
  107.8 1.7 %fusion.15 = f32[4,8192]{1,0:T(4,128)} fusion(f32[1,4,64,128]{3,2,1,0:T(8,128)S(1)} %slice_bitcast_fusion, f32[4,8192]{1,0:T(4,128)} %param.20, f32[8192]{0:T(1024)S(1)} %fusion.32, f32[8192]{0:T(1024)S(1)} %copy-done.5), kind=kLoop, calls=%fused_computation.27 | loop fusion | flops 98304 | bytes 458752 | tf_op jit(solution)/shard_map/div | solution.py:303
  (57 shorter events, 15.3 us)
Async XLA Ops:
  0.6 19.6 %copy-start.8 = (f32[8192]{0:T(1024)S(1)}, f32[8192]{0:T(1024)}, u32[]{:S(2)}) copy-start(f32[8192]{0:T(1024)} %param.16) | copy-start | bytes 98308
  0.6 19.6 %copy-start.6 = (f32[4,8192]{1,0:T(4,128)S(1)}, f32[4,8192]{1,0:T(4,128)}, u32[]{:S(2)}) copy-start(f32[4,8192]{1,0:T(4,128)} %param.27) | copy-start | bytes 393220
  4.0 21.0 %all-to-all-start = ((s32[128,1,4]{2,1,0:T(1,128)}), s32[128,1,4]{2,1,0:T(1,128)S(1)}, u32[]{:S(2)}, u32[]{:S(2)}) async-start(s32[128,1,4]{2,1,0:T(1,128)} %bitcast.17), calls=%async_computation | async-start | bytes 131072 | tf_op jit(solution)/shard_map/all_to_all | solution.py:257
  15.6 31.1 %copy-start = (s32[256,128]{1,0:T(8,128)}, s32[256,128]{1,0:T(8,128)S(1)}, u32[]{:S(2)}) copy-start(s32[256,128]{1,0:T(8,128)S(1)} %add_select_fusion.2.lanes_ref) | copy-start | bytes 393220
  27.1 9.4 %copy-start.3 = (f32[4,8192]{1,0:T(4,128)S(1)}, f32[4,8192]{1,0:T(4,128)}, u32[]{:S(2)}) copy-start(f32[4,8192]{1,0:T(4,128)} %param.26) | copy-start | bytes 393220
  27.1 9.5 %copy-start.4 = (s32[8192]{0:T(1024)S(1)}, s32[8192]{0:T(1024)}, u32[]{:S(2)}) copy-start(s32[8192]{0:T(1024)} %param.23) | copy-start | bytes 98308
  28.8 23.9 %all-to-all-start.1 = ((f32[128,1,2048]{2,1,0:T(1,128)}), f32[128,1,2048]{2,1,0:T(1,128)S(1)}, u32[]{:S(2)}, u32[]{:S(2)}) async-start(f32[128,1,2048]{2,1,0:T(1,128)} %bitcast.28), calls=%async_computation.1 | async-start | bytes 2097152 | tf_op jit(solution)/shard_map/all_to_all | solution.py:278
  41.8 9.2 %copy-start.2 = (s32[256,128]{1,0:T(8,128)S(1)}, s32[256,128]{1,0:T(8,128)}, u32[]{:S(2)}) copy-start(s32[256,128]{1,0:T(8,128)} %shard_map.157) | copy-start | bytes 393220
  52.6 5.4 %copy-start.1 = (f32[4,8192]{1,0:T(4,128)S(1)}, f32[4,8192]{1,0:T(4,128)}, u32[]{:S(2)}) copy-start(f32[4,8192]{1,0:T(4,128)} %shard_map.158) | copy-start | bytes 393220
  72.7 9.1 %copy-start.7 = (bf16[72,72]{1,0:T(8,128)(2,1)S(1)}, bf16[72,72]{1,0:T(8,128)(2,1)}, u32[]{:S(2)}) copy-start(bf16[72,72]{1,0:T(8,128)(2,1)} %mix_ref.1) | copy-start | bytes 31108
  72.7 30.5 %all-to-all-start.2 = ((f32[128,1,2560]{2,1,0:T(1,128)}), f32[128,1,2560]{2,1,0:T(1,128)S(1)}, u32[]{:S(2)}, u32[]{:S(2)}) async-start(f32[128,1,2560]{2,1,0:T(1,128)} %all_to_all.24), calls=%async_computation.2 | async-start | bytes 2621440 | tf_op jit(solution)/shard_map/all_to_all | solution.py:295
  106.4 1.4 %copy-start.5 = (f32[8192]{0:T(1024)S(1)}, f32[8192]{0:T(1024)}, u32[]{:S(2)}) copy-start(f32[8192]{0:T(1024)} %param.19) | copy-start | bytes 98308

commit v12 on v11

--- a/solution.py
+++ b/solution.py
@@ -213,6 +213,64 @@
         in_specs=[pl.BlockSpec(memory_space=pltpu.VMEM)],
         out_specs=pl.BlockSpec(memory_space=pltpu.VMEM),
     )(keys)
+
+
+def return_prep_kernel(
+    m00_ref, win_ref, lanes_ref, weight_ref, share_ref, base_ref, top0_ref, sea_ref,
+    order_ref, keys_ref, last_ref, present_ref, partial_ref, forcing_ref,
+):
+    lanes = lanes_ref[...]
+    parts = base_ref.shape[1]
+    split = weight_ref.shape[0] // parts
+    weight = weight_ref[...].reshape(split, parts, lanes.shape[1])
+    total_weight = jnp.sum(weight, axis=0)
+    share = share_ref[...]
+    sea = sea_ref[...] == 1
+    order = order_ref[...]
+    keys = keys_ref[...]
+    last = last_ref[...]
+    present = present_ref[...] > 0
+    position = lax.broadcasted_iota(jnp.int32, keys.shape, 1)
+    links = []
+    shift = 1
+    while shift < keys.shape[1]:
+        joined = (position >= shift) & (pltpu.roll(keys, shift, 1) == keys)
+        links.append((shift, joined))
+        shift *= 2
+
+    def scatter(values):
+        run = jnp.take_along_axis(values, order, axis=1, mode="promise_in_bounds")
+        for step, joined in links:
+            run = jnp.where(joined, run + pltpu.roll(run, step, 1), run)
+        picked = jnp.take_along_axis(run, last, axis=1, mode="promise_in_bounds")
+        return jnp.where(present, picked, 0.0)
+
+    for field in range(win_ref.shape[0]):
+        cells = jnp.take_along_axis(win_ref[field], lanes, axis=1, mode="promise_in_bounds")
+        cells = cells.reshape(split, parts, lanes.shape[1])
+        forcing = jnp.sum(weight * cells, axis=0) / total_weight
+        forcing_ref[field] = forcing
+        top = jnp.where(sea, base_ref[field] + m00_ref[0] * forcing, top0_ref[field])
+        values = (share.reshape(split, parts, lanes.shape[1]) * top[None]).reshape(share.shape)
+        partial_ref[field] = scatter(values)
+    partial_ref[win_ref.shape[0]] = scatter(share)
+
+
+def return_prep(m00, win, lanes, weight, share, base, top0, sea, order, keys, last, present):
+    fields = win.shape[0]
+    return pl.pallas_call(
+        return_prep_kernel,
+        out_shape=(
+            jax.ShapeDtypeStruct((fields + 1,) + lanes.shape, jnp.float32),
+            jax.ShapeDtypeStruct(base.shape, jnp.float32),
+        ),
+        in_specs=[pl.BlockSpec(memory_space=pltpu.SMEM)]
+        + [pl.BlockSpec(memory_space=pltpu.VMEM)] * 11,
+        out_specs=(
+            pl.BlockSpec(memory_space=pltpu.VMEM),
+            pl.BlockSpec(memory_space=pltpu.VMEM),
+        ),
+    )(m00, win, lanes, weight, share, base, top0, sea, order, keys, last, present)
 
 
 def per_device(
@@ -281,14 +339,23 @@
     win_local = jnp.einsum(
         "qt,qfl->ftl", placement, arrived.reshape(slot_tiles, 4, width), precision=highest
     )
-    at_cells = lane_gather(win_local, lanes).reshape(4, intersections, ocean_cells)
-    forcing = jnp.sum(ocean_weight[None] * at_cells, axis=1) / jnp.sum(ocean_weight, axis=0)[None]
-
-    sea = sea_mask[None, :] == 1
-    top = jnp.where(sea, base_top + ocean_mixing[0, 0] * forcing, state_by_level[0])
+    parts = ocean_cells // width
     sea_share = atmos_weight * sea_mask.astype(jnp.float32)[None, :]
-    outgoing = jnp.concatenate([sea_share[None] * top[:, None, :], sea_share[None]], axis=0)
-    partial = lane_scatter(outgoing.reshape(5, tile_count, width), order, keys, last, present)
+    partial, forcing = return_prep(
+        ocean_mixing[0, 0:1],
+        win_local,
+        late_lanes,
+        ocean_weight.reshape(tile_count, width),
+        sea_share.reshape(tile_count, width),
+        base_top.reshape(4, parts, width),
+        late_state[0].reshape(4, parts, width),
+        sea_mask.reshape(parts, width),
+        order,
+        keys,
+        last,
+        present,
+    )
+    forcing = forcing.reshape(4, ocean_cells)
     send_buffer = jnp.einsum("qt,ftc->qfc", placement, partial, precision=highest)
     late_profiles, send_buffer = lax.optimization_barrier((atmos_profiles, send_buffer))
     atmos_updated = diffuse_atmos(late_profiles, atmos_mixing, fluxes)

time: 111 us -> 108 us (0.973)
  waiting for transfers between devices: 6.35 us -> 1.9 us
  other arithmetic: 21.5 us -> 17.8 us
  starting transfers between devices: 25.6 us -> 29.3 us
  local copies, waits for them, and re-layouts: 13.5 us -> 16.4 us
    all_to_all x1, waiting for transfers between devices: 4.7 us -> 0.7 us  [per_device(): lax.all_to_all(request, ('comp', 'sub'), split_axis=0, concat_axis=0, til...]
    all_to_all x1, starting transfers between devices: 5.08 us -> 9.06 us  [per_device(): lax.all_to_all(served.reshape(devices, -1), ('comp', 'sub'), split_axis=0...]
    select_n x1 -> x0, other arithmetic: 2.27 us -> none  [per_device(): jnp.where(sea, base_top + ocean_mixing[0, 0] * forcing, state_by_level[0])]
    unnamed x20, local copies, waits for them, and re-layouts: 0.13 us -> 1.77 us
    another operation x0 -> x1, local copies, waits for them, and re-layouts: none -> 1.63 us  [per_device(): late_state[0].reshape(4, parts, width)]
    pallas_call x2 -> x1, Pallas kernels: 8.1 us -> 7.14 us  [return_prep(): pl.pallas_call(return_prep_kernel, out_shape=(jax.ShapeDtypeStruct((field...]
  transfers between devices with their start and end apart: 3 -> 3, of which waited for: 3 -> 3; matrix products, arithmetic and copies ran while one was open for 14% -> 18% of each run, Pallas kernels for 26% -> 26%
where the time goes in v12:
time: 108 us; the launch traced here: 107 us
  Pallas kernels  35.5 us (33%)
  starting transfers between devices  29.3 us (27%)
  other arithmetic  17.8 us (16%)
  local copies, waits for them, and re-layouts  16.4 us (15%)
  matrix products  5.14 us (5%)
  waiting for transfers between devices  1.9 us (2%)
    pallas_call x1, Pallas kernels, ocean_update(): pl.pallas_call(ocean_kernel, grid=(cells // block,), out_shape=jax.ShapeD...  13.1 us
    all_to_all x1, starting transfers between devices, per_device(): lax.all_to_all(request, ('comp', 'sub'), split_axis=0, concat_axis=0, til...  11.5 us
    all_to_all x1, starting transfers between devices, per_device(): lax.all_to_all(served.reshape(devices, -1), ('comp', 'sub'), split_axis=0...  9.06 us
    all_to_all x1, starting transfers between devices, per_device(): lax.all_to_all(send_buffer.reshape(devices, -1), ('comp', 'sub'), split_a...  8.77 us
    pallas_call x1, Pallas kernels, return_prep(): pl.pallas_call(return_prep_kernel, out_shape=(jax.ShapeDtypeStruct((field...  7.14 us
    pallas_call x1, Pallas kernels, diffuse_atmos(): pl.pallas_call(atmos_kernel, grid=(columns // block,), out_shape=jax.Shap...  5.95 us
    pallas_call x1, Pallas kernels, top_level_mix(): pl.pallas_call(top_level_kernel, grid=(cells // block,), out_shape=jax.Sh...  4.86 us
    pallas_call x1, Pallas kernels, lane_sort(): pl.pallas_call(lane_sort_kernel, out_shape=jax.ShapeDtypeStruct(keys.shap...  4.43 us
  transfers between devices with their start and end apart: 3, of which 3 were waited for; matrix products, arithmetic and copies ran while one was open for 18% of the time, Pallas kernels for 26%

profile of v12, /device:TPU:1, one launch (start us, length us, event | category | flops | bytes accessed | tf_op | source)
XLA Modules:
  0.0 107.0 jit_solution(13791271358550239329)
XLA Ops:
  0.7 1.0 reshape.108
  1.8 1.0 reshape.107
  4.0 11.5 %all-to-all-start = ((s32[128,1,4]{2,1,0:T(1,128)}), s32[128,1,4]{2,1,0:T(1,128)S(1)}, u32[]{:S(2)}, u32[]{:S(2)}) async-start(s32[128,1,4]{2,1,0:T(1,128)} %bitcast.18), calls=%async_computation | async-start | bytes 131072 | tf_op jit(solution)/shard_map/all_to_all | solution.py:315
  16.4 1.2 %fusion.39 = (f32[1,8192]{1,0:T(1,128)S(1)}, f32[1,8192]{1,0:T(1,128)S(1)}, f32[1,8192]{1,0:T(1,128)S(1)}) fusion(f32[4,8192]{1,0:T(4,128)} %param.18), kind=kLoop, calls=%fused_computation.85 | loop fusion | flops 8192 | bytes 229376 | tf_op jit(solution)/shard_map/slice | solution.py:29
  17.6 1.1 %slice_convert_fusion = f32[4,1,8192]{2,1,0:T(1,128)S(1)} fusion(bf16[4,72,8192]{2,1,0:T(8,128)(2,1)} %x_ref), kind=kLoop, calls=%fused_computation.45 | loop fusion | flops 32768 | bytes 196608 | tf_op jit(solution)/shard_map/convert_element_type | solution.py:14
  18.8 1.4 %fusion.35 = (f32[1,8192]{1,0:T(1,128)S(1)}, f32[1,8192]{1,0:T(1,128)S(1)}, f32[1,8192]{1,0:T(1,128)S(1)}, f32[1,8192]{1,0:T(1,128)S(1)}) fusion(f32[4,1,8192]{2,1,0:T(1,128)S(1)} %slice_convert_fusion, f32[4,8192]{1,0:T(4,128)} %param.17), kind=kLoop, calls=%fused_computation.62 | loop fusion | flops 32768 | bytes 393216 | tf_op jit(solution)/shard_map/sub | solution.py:15
  20.3 1.3 %slice_bitcast_fusion.7.row_ref = f32[60]{0:T(128)} fusion(f32[60,60]{1,0:T(8,128)} %m_ref.1), kind=kLoop, calls=%fused_computation.82 | loop fusion | bytes 480 | tf_op jit(solution)/shard_map/squeeze | solution.py:327
  21.6 1.2 %slice.100 = f32[1,1]{1,0:T(1,128)} slice(f32[60,60]{1,0:T(8,128)} %m_ref.1), slice={[0:1], [0:1]} | slice | bytes 8 | tf_op jit(solution)/shard_map/slice | solution.py:345
  27.1 1.6 %copy.35 = f32[512,4,128]{2,1,0:T(4,128)} copy(f32[512,4,128]{2,0,1:T(8,128)S(1)} %fusion.16) | data formatting | bytes 2097152 | tf_op jit(solution)/shard_map/optimization_barrier | solution.py:326
  28.8 9.1 %all-to-all-start.1 = ((f32[128,1,2048]{2,1,0:T(1,128)}), f32[128,1,2048]{2,1,0:T(1,128)S(1)}, u32[]{:S(2)}, u32[]{:S(2)}) async-start(f32[128,1,2048]{2,1,0:T(1,128)} %bitcast.27), calls=%async_computation.1 | async-start | bytes 2097152 | tf_op jit(solution)/shard_map/all_to_all | solution.py:336
  38.5 4.4 %shard_map.158 = s32[256,128]{1,0:T(8,128)} custom-call(s32[256,128]{1,0:T(8,128)} %iota_add_fusion.key_ref), custom_call_target="tpu_custom_call" | custom-call | tf_op jit(solution)/shard_map/pallas_call | solution.py:210
  42.9 4.9 %shard_map.157 = f32[4,8192]{1,0:T(4,128)} custom-call(f32[60]{0:T(128)} %slice_bitcast_fusion.7.row_ref, f32[60,4,8192]{2,1,0:T(4,128)} %bitcast.87), custom_call_target="tpu_custom_call" | custom-call | flops 3932160 | bytes 7995392 | tf_op jit(solution)/shard_map/pallas_call | solution.py:142
  48.7 1.6 %copy_bitcast_fusion.1 = (f32[4,64,128]{2,1,0:T(8,128)}, f32[4,64,128]{2,1,0:T(8,128)}) fusion(f32[1,4,64,128]{3,1,2,0:T(4,128)S(1)} %slice_bitcast_fusion.1, f32[1,4,64,128]{3,1,2,0:T(4,128)} %bitcast.94), kind=kLoop, calls=%fused_computation.26 | loop fusion | bytes 524288 | tf_op jit(solution)/shard_map/reshape;squeeze | solution.py:351
  50.3 4.4 %convert_reduce_fusion = s32[256,128]{1,0:T(8,128)S(1)} fusion(s32[256,128]{1,0:T(8,128)S(1)} %add_select_fusion.2.lanes_ref), kind=kLoop, calls=%fused_computation | loop fusion | flops 12550144 | bytes 262144 | tf_op jit(solution)/shard_map/reduce_sum | solution.py:330
  55.6 1.0 all-to-all-done.1
  56.6 1.5 %convolution_bitcast_fusion.win_ref = f32[4,256,128]{2,1,0:T(8,128)} fusion(f32[512,4,128]{2,1,0:T(4,128)S(1)} %bitcast.91, s32[256]{0:T(256)S(1)} %and_select_fusion.1), kind=kOutput, calls=%fused_computation.4 | convolution fusion | flops 805437440 | bytes 1573888 | tf_op jit(solution)/shard_map/qt,qfl->ftl/dot_general | solution.py:339
  58.2 7.1 %shard_map.159 = (f32[5,256,128]{2,1,0:T(8,128)}, f32[4,64,128]{2,1,0:T(8,128)}) custom-call(f32[1]{0:T(128)} %bitcast.14.m00_ref, f32[4,256,128]{2,1,0:T(8,128)} %convolution_bitcast_fusion.win_ref, s32[256,128]{1,0:T(8,128)} %copy-done, f32[256,128]{1,0:T(8,128)} %reshape.110.weight_ref, f32[256,128]{1,0:T(8,128)} %reshape.111.share_ref, ...), custom_call_target="tpu_custom_call" | custom-call | tf_op jit(solution)/shard_map/pallas_call | solution.py:261
  65.3 2.0 %fusion.8 = f32[512,5,128]{2,0,1:T(8,128)S(1)} fusion(f32[5,256,128]{2,1,0:T(8,128)} %get-tuple-element.13, s32[256]{0:T(256)S(1)} %and_select_fusion.1), kind=kOutput, calls=%fused_computation.10 | convolution fusion | flops 1006764032 | bytes 1967104 | tf_op jit(solution)/shard_map/qt,ftc->qfc/dot_general | solution.py:359
  68.1 2.4 %all_to_all.24 = f32[128,1,2560]{2,1,0:T(1,128)} reshape(f32[512,5,128]{2,1,0:T(8,128)S(1)} %copy.39) | data formatting | bytes 2621440 | tf_op jit(solution)/shard_map/all_to_all | solution.py:362
  70.5 8.8 %all-to-all-start.2 = ((f32[128,1,2560]{2,1,0:T(1,128)}), f32[128,1,2560]{2,1,0:T(1,128)S(1)}, u32[]{:S(2)}, u32[]{:S(2)}) async-start(f32[128,1,2560]{2,1,0:T(1,128)} %all_to_all.24), calls=%async_computation.2 | async-start | bytes 2621440 | tf_op jit(solution)/shard_map/all_to_all | solution.py:362
  81.5 6.0 %shard_map.160 = bf16[4,72,8192]{2,1,0:T(8,128)(2,1)} custom-call(bf16[72,72]{1,0:T(8,128)(2,1)} %mix_ref.1, f32[72,1]{1,0:T(8,128)} %slice_convert_fusion.1.low_ref, f32[4,8192]{1,0:T(4,128)} %maximum_multiply_fusion.tend_ref, bf16[4,72,8192]{2,1,0:T(8,128)(2,1)} %x_ref), custom_call_target="tpu_custom_call" | custom-call | flops 339738624 | bytes 9437184 | tf_op jit(solution)/shard_map/pallas_call | solution.py:48
  87.4 13.1 %shard_map.161 = f32[60,4,8192]{2,1,0:T(4,128)} custom-call(f32[60,60]{1,0:T(8,128)} %m_ref.1, f32[60,1]{1,0:T(8,128)} %bitcast.103, f32[60,4,8192]{2,1,0:T(4,128)} %bitcast.89, f32[4,8192]{1,0:T(4,128)} %bitcast.93, s32[1,8192]{1,0:T(1,128)} %bitcast.97), custom_call_target="tpu_custom_call" | custom-call | flops 1415577600 | bytes 15728640 | tf_op jit(solution)/shard_map/pallas_call | solution.py:113
  100.7 3.1 %reduce.2 = f32[128,2560]{1,0:T(8,128)S(1)} reduce(f32[128,1,2560]{2,1,0:T(1,128)S(1)} %all-to-all-done.2, f32[]{:T(128)} %constant.63), dimensions={1}, to_apply=%all_to_all.23.reduce_sub_computation | reduce | bytes 2621444 | tf_op jit(solution)/shard_map/all_to_all | solution.py:362
  105.3 1.7 %fusion.15 = f32[4,8192]{1,0:T(4,128)} fusion(f32[1,4,64,128]{3,2,1,0:T(8,128)S(1)} %slice_bitcast_fusion, f32[4,8192]{1,0:T(4,128)} %param.20, f32[8192]{0:T(1024)S(1)} %fusion.31, f32[8192]{0:T(1024)S(1)} %copy-done.2), kind=kLoop, calls=%fused_computation.24 | loop fusion | flops 98304 | bytes 458752 | tf_op jit(solution)/shard_map/div | solution.py:370
  (48 shorter events, 13.6 us)
Async XLA Ops:
  0.6 19.6 %copy-start.7 = (f32[8192]{0:T(1024)S(1)}, f32[8192]{0:T(1024)}, u32[]{:S(2)}) copy-start(f32[8192]{0:T(1024)} %param.16) | copy-start | bytes 98308
  0.6 19.6 %copy-start.3 = (f32[4,8192]{1,0:T(4,128)S(1)}, f32[4,8192]{1,0:T(4,128)}, u32[]{:S(2)}) copy-start(f32[4,8192]{1,0:T(4,128)} %param.27) | copy-start | bytes 393220
  0.7 22.9 %copy-start.4 = (f32[4,8192]{1,0:T(4,128)S(1)}, f32[4,8192]{1,0:T(4,128)}, u32[]{:S(2)}) copy-start(f32[4,8192]{1,0:T(4,128)} %param.26) | copy-start | bytes 393220
  4.0 21.0 %all-to-all-start = ((s32[128,1,4]{2,1,0:T(1,128)}), s32[128,1,4]{2,1,0:T(1,128)S(1)}, u32[]{:S(2)}, u32[]{:S(2)}) async-start(s32[128,1,4]{2,1,0:T(1,128)} %bitcast.18), calls=%async_computation | async-start | bytes 131072 | tf_op jit(solution)/shard_map/all_to_all | solution.py:315
  15.6 34.7 %copy-start = (s32[256,128]{1,0:T(8,128)}, s32[256,128]{1,0:T(8,128)S(1)}, u32[]{:S(2)}) copy-start(s32[256,128]{1,0:T(8,128)S(1)} %add_select_fusion.2.lanes_ref) | copy-start | bytes 393220
  28.8 27.9 %all-to-all-start.1 = ((f32[128,1,2048]{2,1,0:T(1,128)}), f32[128,1,2048]{2,1,0:T(1,128)S(1)}, u32[]{:S(2)}, u32[]{:S(2)}) async-start(f32[128,1,2048]{2,1,0:T(1,128)} %bitcast.27), calls=%async_computation.1 | async-start | bytes 2097152 | tf_op jit(solution)/shard_map/all_to_all | solution.py:336
  42.9 11.8 %copy-start.1 = (s32[256,128]{1,0:T(8,128)S(1)}, s32[256,128]{1,0:T(8,128)}, u32[]{:S(2)}) copy-start(s32[256,128]{1,0:T(8,128)} %shard_map.158) | copy-start | bytes 393220
  70.5 8.8 %copy-start.6 = (bf16[72,72]{1,0:T(8,128)(2,1)S(1)}, bf16[72,72]{1,0:T(8,128)(2,1)}, u32[]{:S(2)}) copy-start(bf16[72,72]{1,0:T(8,128)(2,1)} %mix_ref.1) | copy-start | bytes 31108
  70.5 10.3 %copy-start.5 = (f32[4,64,128]{2,1,0:T(8,128)S(1)}, f32[4,64,128]{2,1,0:T(8,128)}, u32[]{:S(2)}) copy-start(f32[4,64,128]{2,1,0:T(8,128)} %get-tuple-element.15) | copy-start | bytes 393220
  70.5 30.2 %all-to-all-start.2 = ((f32[128,1,2560]{2,1,0:T(1,128)}), f32[128,1,2560]{2,1,0:T(1,128)S(1)}, u32[]{:S(2)}, u32[]{:S(2)}) async-start(f32[128,1,2560]{2,1,0:T(1,128)} %all_to_all.24), calls=%async_computation.2 | async-start | bytes 2621440 | tf_op jit(solution)/shard_map/all_to_all | solution.py:362
  103.8 1.4 %copy-start.2 = (f32[8192]{0:T(1024)S(1)}, f32[8192]{0:T(1024)}, u32[]{:S(2)}) copy-start(f32[8192]{0:T(1024)} %param.19) | copy-start | bytes 98308

commit v13 on v12

--- a/solution.py
+++ b/solution.py
@@ -108,7 +108,7 @@
         out_ref[:, field, :] = jnp.where(sea, mixed, x)
 
 
-def ocean_update(ocean_mixing, state_by_level, forcing, sea_mask, block=1024):
+def ocean_update(ocean_mixing, state_by_level, forcing, sea_mask, block=2048):
     levels, fields, cells = state_by_level.shape
     return pl.pallas_call(
         ocean_kernel,
@@ -137,7 +137,7 @@
     out_ref[...] = total
 
 
-def top_level_mix(first_row, state_by_level, block=2048):
+def top_level_mix(first_row, state_by_level, block=4096):
     levels, fields, cells = state_by_level.shape
     return pl.pallas_call(
         top_level_kernel,

time: 108 us -> 107 us (level)
  waiting for transfers between devices: 1.9 us -> 3.7 us
  Pallas kernels: 35.5 us -> 33.7 us
    all_to_all x1, waiting for transfers between devices: 0.19 us -> 1.42 us  [per_device(): lax.all_to_all(send_buffer.reshape(devices, -1), ('comp', 'sub'), split_a...]
    pallas_call x1, Pallas kernels: 13.1 us -> 11.9 us  [ocean_update(): pl.pallas_call(ocean_kernel, grid=(cells // block,), out_shape=jax.ShapeD...]
  transfers between devices with their start and end apart: 3 -> 3, of which waited for: 3 -> 3; matrix products, arithmetic and copies ran while one was open for 18% -> 18% of each run, Pallas kernels for 26% -> 25%
where the time goes in v13:
time: 107 us; the launch traced here: 106 us
  Pallas kernels  33.7 us (31%)
  starting transfers between devices  28.8 us (27%)
  other arithmetic  17.8 us (17%)
  local copies, waits for them, and re-layouts  16.4 us (15%)
  matrix products  5.14 us (5%)
  waiting for transfers between devices  3.7 us (3%)
    pallas_call x1, Pallas kernels, ocean_update(): pl.pallas_call(ocean_kernel, grid=(cells // block,), out_shape=jax.ShapeD...  11.9 us
    all_to_all x1, starting transfers between devices, per_device(): lax.all_to_all(request, ('comp', 'sub'), split_axis=0, concat_axis=0, til...  11.5 us
    all_to_all x1, starting transfers between devices, per_device(): lax.all_to_all(served.reshape(devices, -1), ('comp', 'sub'), split_axis=0...  9.06 us
    all_to_all x1, starting transfers between devices, per_device(): lax.all_to_all(send_buffer.reshape(devices, -1), ('comp', 'sub'), split_a...  8.19 us
    pallas_call x1, Pallas kernels, return_prep(): pl.pallas_call(return_prep_kernel, out_shape=(jax.ShapeDtypeStruct((field...  7.14 us
    pallas_call x1, Pallas kernels, diffuse_atmos(): pl.pallas_call(atmos_kernel, grid=(columns // block,), out_shape=jax.Shap...  5.93 us
    pallas_call x1, Pallas kernels, lane_sort(): pl.pallas_call(lane_sort_kernel, out_shape=jax.ShapeDtypeStruct(keys.shap...  4.43 us
    reduce_sum x1, other arithmetic, per_device(): jnp.sum((late_lanes[:, None, :] <= jnp.arange(width, dtype=jnp.int32)[Non...  4.38 us
  transfers between devices with their start and end apart: 3, of which 3 were waited for; matrix products, arithmetic and copies ran while one was open for 18% of the time, Pallas kernels for 25%

profile of v13, /device:TPU:1, one launch (start us, length us, event | category | flops | bytes accessed | tf_op | source)
XLA Modules:
  0.0 106.4 jit_solution(2302875482536367049)
XLA Ops:
  0.7 1.0 reshape.108
  4.0 11.5 %all-to-all-start = ((s32[128,1,4]{2,1,0:T(1,128)}), s32[128,1,4]{2,1,0:T(1,128)S(1)}, u32[]{:S(2)}, u32[]{:S(2)}) async-start(s32[128,1,4]{2,1,0:T(1,128)} %bitcast.18), calls=%async_computation | async-start | bytes 131072 | tf_op jit(solution)/shard_map/all_to_all | solution.py:315
  16.4 1.2 %fusion.39 = (f32[1,8192]{1,0:T(1,128)S(1)}, f32[1,8192]{1,0:T(1,128)S(1)}, f32[1,8192]{1,0:T(1,128)S(1)}) fusion(f32[4,8192]{1,0:T(4,128)} %param.18), kind=kLoop, calls=%fused_computation.85 | loop fusion | flops 8192 | bytes 229376 | tf_op jit(solution)/shard_map/slice | solution.py:29
  17.6 1.1 %slice_convert_fusion = f32[4,1,8192]{2,1,0:T(1,128)S(1)} fusion(bf16[4,72,8192]{2,1,0:T(8,128)(2,1)} %x_ref), kind=kLoop, calls=%fused_computation.45 | loop fusion | flops 32768 | bytes 196608 | tf_op jit(solution)/shard_map/convert_element_type | solution.py:14
  18.8 1.4 %fusion.35 = (f32[1,8192]{1,0:T(1,128)S(1)}, f32[1,8192]{1,0:T(1,128)S(1)}, f32[1,8192]{1,0:T(1,128)S(1)}, f32[1,8192]{1,0:T(1,128)S(1)}) fusion(f32[4,1,8192]{2,1,0:T(1,128)S(1)} %slice_convert_fusion, f32[4,8192]{1,0:T(4,128)} %param.17), kind=kLoop, calls=%fused_computation.62 | loop fusion | flops 32768 | bytes 393216 | tf_op jit(solution)/shard_map/sub | solution.py:15
  20.3 1.3 %slice_bitcast_fusion.7.row_ref = f32[60]{0:T(128)} fusion(f32[60,60]{1,0:T(8,128)} %m_ref.1), kind=kLoop, calls=%fused_computation.82 | loop fusion | bytes 480 | tf_op jit(solution)/shard_map/squeeze | solution.py:327
  21.6 1.2 %slice.100 = f32[1,1]{1,0:T(1,128)} slice(f32[60,60]{1,0:T(8,128)} %m_ref.1), slice={[0:1], [0:1]} | slice | bytes 8 | tf_op jit(solution)/shard_map/slice | solution.py:345
  27.1 1.6 %copy.35 = f32[512,4,128]{2,1,0:T(4,128)} copy(f32[512,4,128]{2,0,1:T(8,128)S(1)} %fusion.16) | data formatting | bytes 2097152 | tf_op jit(solution)/shard_map/optimization_barrier | solution.py:326
  28.8 9.1 %all-to-all-start.1 = ((f32[128,1,2048]{2,1,0:T(1,128)}), f32[128,1,2048]{2,1,0:T(1,128)S(1)}, u32[]{:S(2)}, u32[]{:S(2)}) async-start(f32[128,1,2048]{2,1,0:T(1,128)} %bitcast.27), calls=%async_computation.1 | async-start | bytes 2097152 | tf_op jit(solution)/shard_map/all_to_all | solution.py:336
  38.5 4.4 %shard_map.158 = s32[256,128]{1,0:T(8,128)} custom-call(s32[256,128]{1,0:T(8,128)} %iota_add_fusion.key_ref), custom_call_target="tpu_custom_call" | custom-call | tf_op jit(solution)/shard_map/pallas_call | solution.py:210
  42.9 4.3 %shard_map.157 = f32[4,8192]{1,0:T(4,128)} custom-call(f32[60]{0:T(128)} %slice_bitcast_fusion.7.row_ref, f32[60,4,8192]{2,1,0:T(4,128)} %bitcast.87), custom_call_target="tpu_custom_call" | custom-call | flops 3932160 | bytes 7995392 | tf_op jit(solution)/shard_map/pallas_call | solution.py:142
  48.1 1.6 %copy_bitcast_fusion.1 = (f32[4,64,128]{2,1,0:T(8,128)}, f32[4,64,128]{2,1,0:T(8,128)}) fusion(f32[1,4,64,128]{3,1,2,0:T(4,128)S(1)} %slice_bitcast_fusion.1, f32[1,4,64,128]{3,1,2,0:T(4,128)} %bitcast.94), kind=kLoop, calls=%fused_computation.26 | loop fusion | bytes 524288 | tf_op jit(solution)/shard_map/reshape;squeeze | solution.py:351
  49.8 4.4 %convert_reduce_fusion = s32[256,128]{1,0:T(8,128)S(1)} fusion(s32[256,128]{1,0:T(8,128)S(1)} %add_select_fusion.2.lanes_ref), kind=kLoop, calls=%fused_computation | loop fusion | flops 12550144 | bytes 262144 | tf_op jit(solution)/shard_map/reduce_sum | solution.py:330
  55.0 1.6 %all-to-all-done.1 = f32[128,1,2048]{2,1,0:T(1,128)S(1)} async-done(((f32[128,1,2048]{2,1,0:T(1,128)}), f32[128,1,2048]{2,1,0:T(1,128)S(1)}, u32[]{:S(2)}, u32[]{:S(2)}) %all-to-all-start.1) | async-done | bytes 1048608 | tf_op jit(solution)/shard_map/all_to_all | solution.py:336
  56.6 1.5 %convolution_bitcast_fusion.win_ref = f32[4,256,128]{2,1,0:T(8,128)} fusion(f32[512,4,128]{2,1,0:T(4,128)S(1)} %bitcast.91, s32[256]{0:T(256)S(1)} %and_select_fusion.1), kind=kOutput, calls=%fused_computation.4 | convolution fusion | flops 805437440 | bytes 1573888 | tf_op jit(solution)/shard_map/qt,qfl->ftl/dot_general | solution.py:339
  58.2 7.1 %shard_map.159 = (f32[5,256,128]{2,1,0:T(8,128)}, f32[4,64,128]{2,1,0:T(8,128)}) custom-call(f32[1]{0:T(128)} %bitcast.14.m00_ref, f32[4,256,128]{2,1,0:T(8,128)} %convolution_bitcast_fusion.win_ref, s32[256,128]{1,0:T(8,128)} %copy-done, f32[256,128]{1,0:T(8,128)} %reshape.110.weight_ref, f32[256,128]{1,0:T(8,128)} %reshape.111.share_ref, ...), custom_call_target="tpu_custom_call" | custom-call | tf_op jit(solution)/shard_map/pallas_call | solution.py:261
  65.3 2.0 %fusion.8 = f32[512,5,128]{2,0,1:T(8,128)S(1)} fusion(f32[5,256,128]{2,1,0:T(8,128)} %get-tuple-element.13, s32[256]{0:T(256)S(1)} %and_select_fusion.1), kind=kOutput, calls=%fused_computation.10 | convolution fusion | flops 1006764032 | bytes 1967104 | tf_op jit(solution)/shard_map/qt,ftc->qfc/dot_general | solution.py:359
  68.1 2.4 %all_to_all.24 = f32[128,1,2560]{2,1,0:T(1,128)} reshape(f32[512,5,128]{2,1,0:T(8,128)S(1)} %copy.39) | data formatting | bytes 2621440 | tf_op jit(solution)/shard_map/all_to_all | solution.py:362
  70.5 8.2 %all-to-all-start.2 = ((f32[128,1,2560]{2,1,0:T(1,128)}), f32[128,1,2560]{2,1,0:T(1,128)S(1)}, u32[]{:S(2)}, u32[]{:S(2)}) async-start(f32[128,1,2560]{2,1,0:T(1,128)} %all_to_all.24), calls=%async_computation.2 | async-start | bytes 2621440 | tf_op jit(solution)/shard_map/all_to_all | solution.py:362
  80.9 5.9 %shard_map.160 = bf16[4,72,8192]{2,1,0:T(8,128)(2,1)} custom-call(bf16[72,72]{1,0:T(8,128)(2,1)} %mix_ref.1, f32[72,1]{1,0:T(8,128)} %slice_convert_fusion.1.low_ref, f32[4,8192]{1,0:T(4,128)} %maximum_multiply_fusion.tend_ref, bf16[4,72,8192]{2,1,0:T(8,128)(2,1)} %x_ref), custom_call_target="tpu_custom_call" | custom-call | flops 339738624 | bytes 9437184 | tf_op jit(solution)/shard_map/pallas_call | solution.py:48
  86.8 11.9 %shard_map.161 = f32[60,4,8192]{2,1,0:T(4,128)} custom-call(f32[60,60]{1,0:T(8,128)} %m_ref.1, f32[60,1]{1,0:T(8,128)} %bitcast.103, f32[60,4,8192]{2,1,0:T(4,128)} %bitcast.89, f32[4,8192]{1,0:T(4,128)} %bitcast.93, s32[1,8192]{1,0:T(1,128)} %bitcast.97), custom_call_target="tpu_custom_call" | custom-call | flops 1415577600 | bytes 15728640 | tf_op jit(solution)/shard_map/pallas_call | solution.py:113
  98.7 1.4 %all-to-all-done.2 = f32[128,1,2560]{2,1,0:T(1,128)S(1)} async-done(((f32[128,1,2560]{2,1,0:T(1,128)}), f32[128,1,2560]{2,1,0:T(1,128)S(1)}, u32[]{:S(2)}, u32[]{:S(2)}) %all-to-all-start.2) | async-done | bytes 1310752 | tf_op jit(solution)/shard_map/all_to_all | solution.py:362
  100.1 3.1 %reduce.2 = f32[128,2560]{1,0:T(8,128)S(1)} reduce(f32[128,1,2560]{2,1,0:T(1,128)S(1)} %all-to-all-done.2, f32[]{:T(128)} %constant.63), dimensions={1}, to_apply=%all_to_all.23.reduce_sub_computation | reduce | bytes 2621444 | tf_op jit(solution)/shard_map/all_to_all | solution.py:362
  104.7 1.7 %fusion.15 = f32[4,8192]{1,0:T(4,128)} fusion(f32[1,4,64,128]{3,2,1,0:T(8,128)S(1)} %slice_bitcast_fusion, f32[4,8192]{1,0:T(4,128)} %param.20, f32[8192]{0:T(1024)S(1)} %fusion.31, f32[8192]{0:T(1024)S(1)} %copy-done.2), kind=kLoop, calls=%fused_computation.24 | loop fusion | flops 98304 | bytes 458752 | tf_op jit(solution)/shard_map/div | solution.py:370
  (48 shorter events, 14.4 us)
Async XLA Ops:
  0.6 19.6 %copy-start.7 = (f32[8192]{0:T(1024)S(1)}, f32[8192]{0:T(1024)}, u32[]{:S(2)}) copy-start(f32[8192]{0:T(1024)} %param.16) | copy-start | bytes 98308
  0.6 19.6 %copy-start.3 = (f32[4,8192]{1,0:T(4,128)S(1)}, f32[4,8192]{1,0:T(4,128)}, u32[]{:S(2)}) copy-start(f32[4,8192]{1,0:T(4,128)} %param.27) | copy-start | bytes 393220
  0.7 22.9 %copy-start.4 = (f32[4,8192]{1,0:T(4,128)S(1)}, f32[4,8192]{1,0:T(4,128)}, u32[]{:S(2)}) copy-start(f32[4,8192]{1,0:T(4,128)} %param.26) | copy-start | bytes 393220
  4.0 21.0 %all-to-all-start = ((s32[128,1,4]{2,1,0:T(1,128)}), s32[128,1,4]{2,1,0:T(1,128)S(1)}, u32[]{:S(2)}, u32[]{:S(2)}) async-start(s32[128,1,4]{2,1,0:T(1,128)} %bitcast.18), calls=%async_computation | async-start | bytes 131072 | tf_op jit(solution)/shard_map/all_to_all | solution.py:315
  15.6 34.2 %copy-start = (s32[256,128]{1,0:T(8,128)}, s32[256,128]{1,0:T(8,128)S(1)}, u32[]{:S(2)}) copy-start(s32[256,128]{1,0:T(8,128)S(1)} %add_select_fusion.2.lanes_ref) | copy-start | bytes 393220
  28.8 27.9 %all-to-all-start.1 = ((f32[128,1,2048]{2,1,0:T(1,128)}), f32[128,1,2048]{2,1,0:T(1,128)S(1)}, u32[]{:S(2)}, u32[]{:S(2)}) async-start(f32[128,1,2048]{2,1,0:T(1,128)} %bitcast.27), calls=%async_computation.1 | async-start | bytes 2097152 | tf_op jit(solution)/shard_map/all_to_all | solution.py:336
  42.9 11.2 %copy-start.1 = (s32[256,128]{1,0:T(8,128)S(1)}, s32[256,128]{1,0:T(8,128)}, u32[]{:S(2)}) copy-start(s32[256,128]{1,0:T(8,128)} %shard_map.158) | copy-start | bytes 393220
  70.5 8.2 %copy-start.6 = (bf16[72,72]{1,0:T(8,128)(2,1)S(1)}, bf16[72,72]{1,0:T(8,128)(2,1)}, u32[]{:S(2)}) copy-start(bf16[72,72]{1,0:T(8,128)(2,1)} %mix_ref.1) | copy-start | bytes 31108
  70.5 9.7 %copy-start.5 = (f32[4,64,128]{2,1,0:T(8,128)S(1)}, f32[4,64,128]{2,1,0:T(8,128)}, u32[]{:S(2)}) copy-start(f32[4,64,128]{2,1,0:T(8,128)} %get-tuple-element.15) | copy-start | bytes 393220
  70.5 29.7 %all-to-all-start.2 = ((f32[128,1,2560]{2,1,0:T(1,128)}), f32[128,1,2560]{2,1,0:T(1,128)S(1)}, u32[]{:S(2)}, u32[]{:S(2)}) async-start(f32[128,1,2560]{2,1,0:T(1,128)} %all_to_all.24), calls=%async_computation.2 | async-start | bytes 2621440 | tf_op jit(solution)/shard_map/all_to_all | solution.py:362
  103.3 1.4 %copy-start.2 = (f32[8192]{0:T(1024)S(1)}, f32[8192]{0:T(1024)}, u32[]{:S(2)}) copy-start(f32[8192]{0:T(1024)} %param.19) | copy-start | bytes 98308

commit v14 on v13

--- a/solution.py
+++ b/solution.py
@@ -185,7 +185,7 @@
     )(order, keys, last, present, values)
 
 
-def lane_sort_kernel(key_ref, sorted_ref):
+def lane_sort_kernel(key_ref, sorted_ref, present_ref, last_ref):
     values = key_ref[...]
     count = values.shape[1]
     position = lax.broadcasted_iota(jnp.int32, values.shape, 1)
@@ -204,14 +204,26 @@
             stride //= 2
         block *= 2
     sorted_ref[...] = values
+    lanes = values // count
+    below = jnp.zeros_like(position)
+    step = count // 2
+    while step >= 1:
+        probe = jnp.take_along_axis(lanes, below + (step - 1), axis=1, mode="promise_in_bounds")
+        below = jnp.where(probe <= position, below + step, below)
+        step //= 2
+    probe = jnp.take_along_axis(lanes, below, axis=1, mode="promise_in_bounds")
+    below = jnp.where(probe <= position, below + 1, below)
+    earlier = jnp.where(position >= 1, pltpu.roll(below, 1, 1), 0)
+    present_ref[...] = below - earlier
+    last_ref[...] = jnp.maximum(below - 1, 0)
 
 
 def lane_sort(keys):
     return pl.pallas_call(
         lane_sort_kernel,
-        out_shape=jax.ShapeDtypeStruct(keys.shape, keys.dtype),
+        out_shape=(jax.ShapeDtypeStruct(keys.shape, keys.dtype),) * 3,
         in_specs=[pl.BlockSpec(memory_space=pltpu.VMEM)],
-        out_specs=pl.BlockSpec(memory_space=pltpu.VMEM),
+        out_specs=(pl.BlockSpec(memory_space=pltpu.VMEM),) * 3,
     )(keys)
 
 
@@ -325,14 +337,10 @@
     )
     late_lanes, late_state, served = lax.optimization_barrier((lanes, state_by_level, served))
     base_top = top_level_mix(ocean_mixing[0], late_state)
-    ranked = lane_sort(late_lanes * width + lax.broadcasted_iota(jnp.int32, late_lanes.shape, 1))
+    ranked, present, last = lane_sort(
+        late_lanes * width + lax.broadcasted_iota(jnp.int32, late_lanes.shape, 1)
+    )
     keys, order = ranked // width, ranked % width
-    at_most = jnp.sum(
-        (late_lanes[:, None, :] <= jnp.arange(width, dtype=jnp.int32)[None, :, None]).astype(jnp.int32),
-        axis=2,
-    )
-    present = at_most - jnp.pad(at_most[:, :-1], ((0, 0), (1, 0)))
-    last = jnp.maximum(at_most - 1, 0)
     arrived = lax.all_to_all(
         served.reshape(devices, -1), ("comp", "sub"), split_axis=0, concat_axis=0, tiled=True
     )

time: 107 us -> 104 us (0.972)
  other arithmetic: 17.8 us -> 13.4 us
  waiting for transfers between devices: 3.7 us -> 7.43 us
  starting transfers between devices: 28.8 us -> 25.1 us
    reduce_sum x1 -> x0, other arithmetic: 4.38 us -> none  [per_device(): jnp.sum((late_lanes[:, None, :] <= jnp.arange(width, dtype=jnp.int32)[Non...]
    all_to_all x1, waiting for transfers between devices: 0.7 us -> 4.69 us  [per_device(): lax.all_to_all(request, ('comp', 'sub'), split_axis=0, concat_axis=0, til...]
    all_to_all x1, starting transfers between devices: 9.06 us -> 5.09 us  [per_device(): lax.all_to_all(served.reshape(devices, -1), ('comp', 'sub'), split_axis=0...]
  transfers between devices with their start and end apart: 3 -> 3, of which waited for: 3 -> 3; matrix products, arithmetic and copies ran while one was open for 18% -> 14% of each run, Pallas kernels for 25% -> 27%
where the time goes in v14:
time: 104 us; the launch traced here: 103 us
  Pallas kernels  34.5 us (33%)
  starting transfers between devices  25.1 us (24%)
  local copies, waits for them, and re-layouts  16.3 us (16%)
  other arithmetic  13.4 us (13%)
  waiting for transfers between devices  7.43 us (7%)
  matrix products  5.14 us (5%)
    pallas_call x1, Pallas kernels, ocean_update(): pl.pallas_call(ocean_kernel, grid=(cells // block,), out_shape=jax.ShapeD...  11.9 us
    all_to_all x1, starting transfers between devices, per_device(): lax.all_to_all(request, ('comp', 'sub'), split_axis=0, concat_axis=0, til...  11.5 us
    all_to_all x1, starting transfers between devices, per_device(): lax.all_to_all(send_buffer.reshape(devices, -1), ('comp', 'sub'), split_a...  8.5 us
    pallas_call x1, Pallas kernels, return_prep(): pl.pallas_call(return_prep_kernel, out_shape=(jax.ShapeDtypeStruct((field...  7.11 us
    pallas_call x1, Pallas kernels, diffuse_atmos(): pl.pallas_call(atmos_kernel, grid=(columns // block,), out_shape=jax.Shap...  5.92 us
    pallas_call x1, Pallas kernels, lane_sort(): pl.pallas_call(lane_sort_kernel, out_shape=(jax.ShapeDtypeStruct(keys.sha...  5.33 us
    all_to_all x1, starting transfers between devices, per_device(): lax.all_to_all(served.reshape(devices, -1), ('comp', 'sub'), split_axis=0...  5.09 us
    all_to_all x1, waiting for transfers between devices, per_device(): lax.all_to_all(request, ('comp', 'sub'), split_axis=0, concat_axis=0, til...  4.69 us
  transfers between devices with their start and end apart: 3, of which 3 were waited for; matrix products, arithmetic and copies ran while one was open for 14% of the time, Pallas kernels for 27%

profile of v14, /device:TPU:1, one launch (start us, length us, event | category | flops | bytes accessed | tf_op | source)
XLA Modules:
  0.0 102.7 jit_solution(773392770564265006)
XLA Ops:
  0.7 1.0 %reshape.107 = s32[256,128]{1,0:T(8,128)S(1)} reshape(s32[4,8192]{1,0:T(4,128)} %param.25) | data formatting | bytes 262144 | tf_op jit(solution)/shard_map/reshape | solution.py:319
  4.0 11.5 %all-to-all-start = ((s32[128,1,4]{2,1,0:T(1,128)}), s32[128,1,4]{2,1,0:T(1,128)S(1)}, u32[]{:S(2)}, u32[]{:S(2)}) async-start(s32[128,1,4]{2,1,0:T(1,128)} %bitcast.18), calls=%async_computation | async-start | bytes 131072 | tf_op jit(solution)/shard_map/all_to_all | solution.py:327
  16.4 1.2 %fusion.39 = (f32[1,8192]{1,0:T(1,128)S(1)}, f32[1,8192]{1,0:T(1,128)S(1)}, f32[1,8192]{1,0:T(1,128)S(1)}) fusion(f32[4,8192]{1,0:T(4,128)} %param.18), kind=kLoop, calls=%fused_computation.81 | loop fusion | flops 8192 | bytes 229376 | tf_op jit(solution)/shard_map/slice | solution.py:29
  17.6 1.1 %slice_convert_fusion = f32[4,1,8192]{2,1,0:T(1,128)S(1)} fusion(bf16[4,72,8192]{2,1,0:T(8,128)(2,1)} %x_ref), kind=kLoop, calls=%fused_computation.41 | loop fusion | flops 32768 | bytes 196608 | tf_op jit(solution)/shard_map/convert_element_type | solution.py:14
  18.8 1.4 %fusion.35 = (f32[1,8192]{1,0:T(1,128)S(1)}, f32[1,8192]{1,0:T(1,128)S(1)}, f32[1,8192]{1,0:T(1,128)S(1)}, f32[1,8192]{1,0:T(1,128)S(1)}) fusion(f32[4,1,8192]{2,1,0:T(1,128)S(1)} %slice_convert_fusion, f32[4,8192]{1,0:T(4,128)} %param.17), kind=kLoop, calls=%fused_computation.58 | loop fusion | flops 32768 | bytes 393216 | tf_op jit(solution)/shard_map/sub | solution.py:15
  20.3 4.7 %all-to-all-done = s32[128,1,4]{2,1,0:T(1,128)S(1)} async-done(((s32[128,1,4]{2,1,0:T(1,128)}), s32[128,1,4]{2,1,0:T(1,128)S(1)}, u32[]{:S(2)}, u32[]{:S(2)}) %all-to-all-start) | async-done | bytes 2080 | tf_op jit(solution)/shard_map/all_to_all | solution.py:327
  27.1 1.6 %copy.26 = f32[512,4,128]{2,1,0:T(4,128)} copy(f32[512,4,128]{2,0,1:T(8,128)S(1)} %fusion.16) | data formatting | bytes 2097152 | tf_op jit(solution)/shard_map/optimization_barrier | solution.py:338
  28.8 5.1 %all-to-all-start.1 = ((f32[128,1,2048]{2,1,0:T(1,128)}), f32[128,1,2048]{2,1,0:T(1,128)S(1)}, u32[]{:S(2)}, u32[]{:S(2)}) async-start(f32[128,1,2048]{2,1,0:T(1,128)} %bitcast.27), calls=%async_computation.1 | async-start | bytes 2097152 | tf_op jit(solution)/shard_map/all_to_all | solution.py:344
  33.8 1.2 %slice_bitcast_fusion.7.row_ref = f32[60]{0:T(128)} fusion(f32[60,60]{1,0:T(8,128)} %m_ref.1), kind=kLoop, calls=%fused_computation.78 | loop fusion | bytes 480 | tf_op jit(solution)/shard_map/squeeze | solution.py:339
  35.0 1.2 %slice.97 = f32[1,1]{1,0:T(1,128)} slice(f32[60,60]{1,0:T(8,128)} %m_ref.1), slice={[0:1], [0:1]} | slice | bytes 8 | tf_op jit(solution)/shard_map/slice | solution.py:353
  38.4 5.3 %shard_map.158 = (s32[256,128]{1,0:T(8,128)}, s32[256,128]{1,0:T(8,128)}, s32[256,128]{1,0:T(8,128)}) custom-call(s32[256,128]{1,0:T(8,128)} %iota_add_fusion.key_ref), custom_call_target="tpu_custom_call" | custom-call | tf_op jit(solution)/shard_map/pallas_call | solution.py:222
  43.7 4.3 %shard_map.157 = f32[4,8192]{1,0:T(4,128)} custom-call(f32[60]{0:T(128)} %slice_bitcast_fusion.7.row_ref, f32[60,4,8192]{2,1,0:T(4,128)} %bitcast.86), custom_call_target="tpu_custom_call" | custom-call | flops 3932160 | bytes 7995392 | tf_op jit(solution)/shard_map/pallas_call | solution.py:142
  49.7 1.6 %copy_bitcast_fusion.1 = (f32[4,64,128]{2,1,0:T(8,128)}, f32[4,64,128]{2,1,0:T(8,128)}) fusion(f32[1,4,64,128]{3,1,2,0:T(4,128)S(1)} %slice_bitcast_fusion.1, f32[1,4,64,128]{3,1,2,0:T(4,128)} %bitcast.92), kind=kLoop, calls=%fused_computation.24 | loop fusion | bytes 524288 | tf_op jit(solution)/shard_map/reshape;squeeze | solution.py:359
  51.4 1.3 %all-to-all-done.1 = f32[128,1,2048]{2,1,0:T(1,128)S(1)} async-done(((f32[128,1,2048]{2,1,0:T(1,128)}), f32[128,1,2048]{2,1,0:T(1,128)S(1)}, u32[]{:S(2)}, u32[]{:S(2)}) %all-to-all-start.1) | async-done | bytes 1048608 | tf_op jit(solution)/shard_map/all_to_all | solution.py:344
  52.6 1.5 %convolution_bitcast_fusion.win_ref = f32[4,256,128]{2,1,0:T(8,128)} fusion(f32[512,4,128]{2,1,0:T(4,128)S(1)} %bitcast.90, s32[256]{0:T(256)S(1)} %and_select_fusion.1), kind=kOutput, calls=%fused_computation.2 | convolution fusion | flops 805437440 | bytes 1573888 | tf_op jit(solution)/shard_map/qt,qfl->ftl/dot_general | solution.py:347
  54.2 7.1 %shard_map.159 = (f32[5,256,128]{2,1,0:T(8,128)}, f32[4,64,128]{2,1,0:T(8,128)}) custom-call(f32[1]{0:T(128)} %bitcast.14.m00_ref, f32[4,256,128]{2,1,0:T(8,128)} %convolution_bitcast_fusion.win_ref, s32[256,128]{1,0:T(8,128)} %copy-done, f32[256,128]{1,0:T(8,128)} %reshape.109.weight_ref, f32[256,128]{1,0:T(8,128)} %reshape.110.share_ref, ...), custom_call_target="tpu_custom_call" | custom-call | tf_op jit(solution)/shard_map/pallas_call | solution.py:273
  61.3 2.0 %fusion.8 = f32[512,5,128]{2,0,1:T(8,128)S(1)} fusion(f32[5,256,128]{2,1,0:T(8,128)} %get-tuple-element.19, s32[256]{0:T(256)S(1)} %and_select_fusion.1), kind=kOutput, calls=%fused_computation.8 | convolution fusion | flops 1006764032 | bytes 1967104 | tf_op jit(solution)/shard_map/qt,ftc->qfc/dot_general | solution.py:367
  64.1 2.4 %all_to_all.24 = f32[128,1,2560]{2,1,0:T(1,128)} reshape(f32[512,5,128]{2,1,0:T(8,128)S(1)} %copy.30) | data formatting | bytes 2621440 | tf_op jit(solution)/shard_map/all_to_all | solution.py:370
  66.4 8.5 %all-to-all-start.2 = ((f32[128,1,2560]{2,1,0:T(1,128)}), f32[128,1,2560]{2,1,0:T(1,128)S(1)}, u32[]{:S(2)}, u32[]{:S(2)}) async-start(f32[128,1,2560]{2,1,0:T(1,128)} %all_to_all.24), calls=%async_computation.2 | async-start | bytes 2621440 | tf_op jit(solution)/shard_map/all_to_all | solution.py:370
  77.2 5.9 %shard_map.160 = bf16[4,72,8192]{2,1,0:T(8,128)(2,1)} custom-call(bf16[72,72]{1,0:T(8,128)(2,1)} %mix_ref.1, f32[72,1]{1,0:T(8,128)} %slice_convert_fusion.1.low_ref, f32[4,8192]{1,0:T(4,128)} %maximum_multiply_fusion.tend_ref, bf16[4,72,8192]{2,1,0:T(8,128)(2,1)} %x_ref), custom_call_target="tpu_custom_call" | custom-call | flops 339738624 | bytes 9437184 | tf_op jit(solution)/shard_map/pallas_call | solution.py:48
  83.1 11.9 %shard_map.161 = f32[60,4,8192]{2,1,0:T(4,128)} custom-call(f32[60,60]{1,0:T(8,128)} %m_ref.1, f32[60,1]{1,0:T(8,128)} %bitcast.101, f32[60,4,8192]{2,1,0:T(4,128)} %bitcast.88, f32[4,8192]{1,0:T(4,128)} %bitcast.91, s32[1,8192]{1,0:T(1,128)} %bitcast.95), custom_call_target="tpu_custom_call" | custom-call | flops 1415577600 | bytes 15728640 | tf_op jit(solution)/shard_map/pallas_call | solution.py:113
  95.0 1.5 %all-to-all-done.2 = f32[128,1,2560]{2,1,0:T(1,128)S(1)} async-done(((f32[128,1,2560]{2,1,0:T(1,128)}), f32[128,1,2560]{2,1,0:T(1,128)S(1)}, u32[]{:S(2)}, u32[]{:S(2)}) %all-to-all-start.2) | async-done | bytes 1310752 | tf_op jit(solution)/shard_map/all_to_all | solution.py:370
  96.4 3.1 %reduce.2 = f32[128,2560]{1,0:T(8,128)S(1)} reduce(f32[128,1,2560]{2,1,0:T(1,128)S(1)} %all-to-all-done.2, f32[]{:T(128)} %constant.57), dimensions={1}, to_apply=%all_to_all.23.reduce_sub_computation | reduce | bytes 2621444 | tf_op jit(solution)/shard_map/all_to_all | solution.py:370
  101.0 1.7 %fusion.15 = f32[4,8192]{1,0:T(4,128)} fusion(f32[1,4,64,128]{3,2,1,0:T(8,128)S(1)} %slice_bitcast_fusion, f32[4,8192]{1,0:T(4,128)} %param.20, f32[8192]{0:T(1024)S(1)} %fusion.31, f32[8192]{0:T(1024)S(1)} %copy-done.1), kind=kLoop, calls=%fused_computation.22 | loop fusion | flops 98304 | bytes 458752 | tf_op jit(solution)/shard_map/div | solution.py:378
  (47 shorter events, 13.6 us)
Async XLA Ops:
  0.6 19.6 %copy-start.7 = (f32[8192]{0:T(1024)S(1)}, f32[8192]{0:T(1024)}, u32[]{:S(2)}) copy-start(f32[8192]{0:T(1024)} %param.16) | copy-start | bytes 98308
  0.6 19.6 %copy-start.3 = (f32[4,8192]{1,0:T(4,128)S(1)}, f32[4,8192]{1,0:T(4,128)}, u32[]{:S(2)}) copy-start(f32[4,8192]{1,0:T(4,128)} %param.27) | copy-start | bytes 393220
  4.0 21.0 %all-to-all-start = ((s32[128,1,4]{2,1,0:T(1,128)}), s32[128,1,4]{2,1,0:T(1,128)S(1)}, u32[]{:S(2)}, u32[]{:S(2)}) async-start(s32[128,1,4]{2,1,0:T(1,128)} %bitcast.18), calls=%async_computation | async-start | bytes 131072 | tf_op jit(solution)/shard_map/all_to_all | solution.py:327
  15.6 22.1 %copy-start = (s32[256,128]{1,0:T(8,128)}, s32[256,128]{1,0:T(8,128)S(1)}, u32[]{:S(2)}) copy-start(s32[256,128]{1,0:T(8,128)S(1)} %add_select_fusion.2.lanes_ref) | copy-start | bytes 393220
  27.1 9.9 %copy-start.4 = (f32[4,8192]{1,0:T(4,128)S(1)}, f32[4,8192]{1,0:T(4,128)}, u32[]{:S(2)}) copy-start(f32[4,8192]{1,0:T(4,128)} %param.26) | copy-start | bytes 393220
  28.8 23.9 %all-to-all-start.1 = ((f32[128,1,2048]{2,1,0:T(1,128)}), f32[128,1,2048]{2,1,0:T(1,128)S(1)}, u32[]{:S(2)}, u32[]{:S(2)}) async-start(f32[128,1,2048]{2,1,0:T(1,128)} %bitcast.27), calls=%async_computation.1 | async-start | bytes 2097152 | tf_op jit(solution)/shard_map/all_to_all | solution.py:344
  43.7 5.2 %copy-start.2 = (s32[256,128]{1,0:T(8,128)S(1)}, s32[256,128]{1,0:T(8,128)}, u32[]{:S(2)}) copy-start(s32[256,128]{1,0:T(8,128)} %get-tuple-element.16) | copy-start | bytes 393220
  66.4 8.5 %copy-start.6 = (bf16[72,72]{1,0:T(8,128)(2,1)S(1)}, bf16[72,72]{1,0:T(8,128)(2,1)}, u32[]{:S(2)}) copy-start(bf16[72,72]{1,0:T(8,128)(2,1)} %mix_ref.1) | copy-start | bytes 31108
  66.4 10.0 %copy-start.5 = (f32[4,64,128]{2,1,0:T(8,128)S(1)}, f32[4,64,128]{2,1,0:T(8,128)}, u32[]{:S(2)}) copy-start(f32[4,64,128]{2,1,0:T(8,128)} %get-tuple-element.21) | copy-start | bytes 393220
  66.4 30.0 %all-to-all-start.2 = ((f32[128,1,2560]{2,1,0:T(1,128)}), f32[128,1,2560]{2,1,0:T(1,128)S(1)}, u32[]{:S(2)}, u32[]{:S(2)}) async-start(f32[128,1,2560]{2,1,0:T(1,128)} %all_to_all.24), calls=%async_computation.2 | async-start | bytes 2621440 | tf_op jit(solution)/shard_map/all_to_all | solution.py:370
  99.5 1.4 %copy-start.1 = (f32[8192]{0:T(1024)S(1)}, f32[8192]{0:T(1024)}, u32[]{:S(2)}) copy-start(f32[8192]{0:T(1024)} %param.19) | copy-start | bytes 98308

commit v15 on v14

--- a/solution.py
+++ b/solution.py
@@ -41,7 +41,7 @@
         out_ref[member] = mixed.astype(out_ref.dtype)
 
 
-def diffuse_atmos(atmos_profiles, atmos_mixing, fluxes, block=2048):
+def diffuse_atmos(atmos_profiles, atmos_mixing, fluxes, block=4096):
     members, levels, columns = atmos_profiles.shape
     lowest = atmos_mixing[:, -1:].astype(jnp.float32)
     tendency = couple_rate * jnp.stack([fluxes[0], fluxes[1], -fluxes[2], -fluxes[3]])
@@ -108,7 +108,7 @@
         out_ref[:, field, :] = jnp.where(sea, mixed, x)
 
 
-def ocean_update(ocean_mixing, state_by_level, forcing, sea_mask, block=2048):
+def ocean_update(ocean_mixing, state_by_level, forcing, sea_mask, block=4096):
     levels, fields, cells = state_by_level.shape
     return pl.pallas_call(
         ocean_kernel,

time: 104 us -> 103 us (level)
    pallas_call x1, Pallas kernels: 11.9 us -> 13.4 us  [ocean_update(): pl.pallas_call(ocean_kernel, grid=(cells // block,), out_shape=jax.ShapeD...]
    pallas_call x1, Pallas kernels: 5.92 us -> 4.77 us  [diffuse_atmos(): pl.pallas_call(atmos_kernel, grid=(columns // block,), out_shape=jax.Shap...]
where the time goes in v15:
time: 103 us
  Pallas kernels  34.9 us (34%)
  starting transfers between devices  25.1 us (24%)
  local copies, waits for them, and re-layouts  16.3 us (16%)
  other arithmetic  13.4 us (13%)
  waiting for transfers between devices  7.04 us (7%)
  matrix products  5.14 us (5%)
    pallas_call x1, Pallas kernels, ocean_update(): pl.pallas_call(ocean_kernel, grid=(cells // block,), out_shape=jax.ShapeD...  13.4 us
    all_to_all x1, starting transfers between devices, per_device(): lax.all_to_all(request, ('comp', 'sub'), split_axis=0, concat_axis=0, til...  11.5 us
    all_to_all x1, starting transfers between devices, per_device(): lax.all_to_all(send_buffer.reshape(devices, -1), ('comp', 'sub'), split_a...  8.5 us
    pallas_call x1, Pallas kernels, return_prep(): pl.pallas_call(return_prep_kernel, out_shape=(jax.ShapeDtypeStruct((field...  7.11 us
    pallas_call x1, Pallas kernels, lane_sort(): pl.pallas_call(lane_sort_kernel, out_shape=(jax.ShapeDtypeStruct(keys.sha...  5.33 us
    all_to_all x1, starting transfers between devices, per_device(): lax.all_to_all(served.reshape(devices, -1), ('comp', 'sub'), split_axis=0...  5.09 us
    pallas_call x1, Pallas kernels, diffuse_atmos(): pl.pallas_call(atmos_kernel, grid=(columns // block,), out_shape=jax.Shap...  4.77 us
    all_to_all x1, waiting for transfers between devices, per_device(): lax.all_to_all(request, ('comp', 'sub'), split_axis=0, concat_axis=0, til...  4.69 us
  transfers between devices with their start and end apart: 3, of which 3 were waited for; matrix products, arithmetic and copies ran while one was open for 14% of the time, Pallas kernels for 27%

profile of v15, /device:TPU:1, one launch (start us, length us, event | category | flops | bytes accessed | tf_op | source)
XLA Modules:
  0.0 102.7 jit_solution(2186118249699533633)
XLA Ops:
  0.7 1.0 %reshape.107 = s32[256,128]{1,0:T(8,128)S(1)} reshape(s32[4,8192]{1,0:T(4,128)} %param.25) | data formatting | bytes 262144 | tf_op jit(solution)/shard_map/reshape | solution.py:319
  4.0 11.5 %all-to-all-start = ((s32[128,1,4]{2,1,0:T(1,128)}), s32[128,1,4]{2,1,0:T(1,128)S(1)}, u32[]{:S(2)}, u32[]{:S(2)}) async-start(s32[128,1,4]{2,1,0:T(1,128)} %bitcast.18), calls=%async_computation | async-start | bytes 131072 | tf_op jit(solution)/shard_map/all_to_all | solution.py:327
  16.4 1.2 %fusion.39 = (f32[1,8192]{1,0:T(1,128)S(1)}, f32[1,8192]{1,0:T(1,128)S(1)}, f32[1,8192]{1,0:T(1,128)S(1)}) fusion(f32[4,8192]{1,0:T(4,128)} %param.18), kind=kLoop, calls=%fused_computation.81 | loop fusion | flops 8192 | bytes 229376 | tf_op jit(solution)/shard_map/slice | solution.py:29
  17.6 1.1 %slice_convert_fusion = f32[4,1,8192]{2,1,0:T(1,128)S(1)} fusion(bf16[4,72,8192]{2,1,0:T(8,128)(2,1)} %x_ref), kind=kLoop, calls=%fused_computation.41 | loop fusion | flops 32768 | bytes 196608 | tf_op jit(solution)/shard_map/convert_element_type | solution.py:14
  18.8 1.4 %fusion.35 = (f32[1,8192]{1,0:T(1,128)S(1)}, f32[1,8192]{1,0:T(1,128)S(1)}, f32[1,8192]{1,0:T(1,128)S(1)}, f32[1,8192]{1,0:T(1,128)S(1)}) fusion(f32[4,1,8192]{2,1,0:T(1,128)S(1)} %slice_convert_fusion, f32[4,8192]{1,0:T(4,128)} %param.17), kind=kLoop, calls=%fused_computation.58 | loop fusion | flops 32768 | bytes 393216 | tf_op jit(solution)/shard_map/sub | solution.py:15
  20.3 4.7 %all-to-all-done = s32[128,1,4]{2,1,0:T(1,128)S(1)} async-done(((s32[128,1,4]{2,1,0:T(1,128)}), s32[128,1,4]{2,1,0:T(1,128)S(1)}, u32[]{:S(2)}, u32[]{:S(2)}) %all-to-all-start) | async-done | bytes 2080 | tf_op jit(solution)/shard_map/all_to_all | solution.py:327
  27.1 1.6 %copy.26 = f32[512,4,128]{2,1,0:T(4,128)} copy(f32[512,4,128]{2,0,1:T(8,128)S(1)} %fusion.16) | data formatting | bytes 2097152 | tf_op jit(solution)/shard_map/optimization_barrier | solution.py:338
  28.8 5.1 %all-to-all-start.1 = ((f32[128,1,2048]{2,1,0:T(1,128)}), f32[128,1,2048]{2,1,0:T(1,128)S(1)}, u32[]{:S(2)}, u32[]{:S(2)}) async-start(f32[128,1,2048]{2,1,0:T(1,128)} %bitcast.27), calls=%async_computation.1 | async-start | bytes 2097152 | tf_op jit(solution)/shard_map/all_to_all | solution.py:344
  33.8 1.2 %slice_bitcast_fusion.7.row_ref = f32[60]{0:T(128)} fusion(f32[60,60]{1,0:T(8,128)} %m_ref.1), kind=kLoop, calls=%fused_computation.78 | loop fusion | bytes 480 | tf_op jit(solution)/shard_map/squeeze | solution.py:339
  35.0 1.2 %slice.97 = f32[1,1]{1,0:T(1,128)} slice(f32[60,60]{1,0:T(8,128)} %m_ref.1), slice={[0:1], [0:1]} | slice | bytes 8 | tf_op jit(solution)/shard_map/slice | solution.py:353
  38.4 5.3 %shard_map.158 = (s32[256,128]{1,0:T(8,128)}, s32[256,128]{1,0:T(8,128)}, s32[256,128]{1,0:T(8,128)}) custom-call(s32[256,128]{1,0:T(8,128)} %iota_add_fusion.key_ref), custom_call_target="tpu_custom_call" | custom-call | tf_op jit(solution)/shard_map/pallas_call | solution.py:222
  43.7 4.3 %shard_map.157 = f32[4,8192]{1,0:T(4,128)} custom-call(f32[60]{0:T(128)} %slice_bitcast_fusion.7.row_ref, f32[60,4,8192]{2,1,0:T(4,128)} %bitcast.86), custom_call_target="tpu_custom_call" | custom-call | flops 3932160 | bytes 7995392 | tf_op jit(solution)/shard_map/pallas_call | solution.py:142
  49.7 1.6 %copy_bitcast_fusion.1 = (f32[4,64,128]{2,1,0:T(8,128)}, f32[4,64,128]{2,1,0:T(8,128)}) fusion(f32[1,4,64,128]{3,1,2,0:T(4,128)S(1)} %slice_bitcast_fusion.1, f32[1,4,64,128]{3,1,2,0:T(4,128)} %bitcast.92), kind=kLoop, calls=%fused_computation.24 | loop fusion | bytes 524288 | tf_op jit(solution)/shard_map/reshape;squeeze | solution.py:359
  51.4 1.3 %all-to-all-done.1 = f32[128,1,2048]{2,1,0:T(1,128)S(1)} async-done(((f32[128,1,2048]{2,1,0:T(1,128)}), f32[128,1,2048]{2,1,0:T(1,128)S(1)}, u32[]{:S(2)}, u32[]{:S(2)}) %all-to-all-start.1) | async-done | bytes 1048608 | tf_op jit(solution)/shard_map/all_to_all | solution.py:344
  52.6 1.5 %convolution_bitcast_fusion.win_ref = f32[4,256,128]{2,1,0:T(8,128)} fusion(f32[512,4,128]{2,1,0:T(4,128)S(1)} %bitcast.90, s32[256]{0:T(256)S(1)} %and_select_fusion.1), kind=kOutput, calls=%fused_computation.2 | convolution fusion | flops 805437440 | bytes 1573888 | tf_op jit(solution)/shard_map/qt,qfl->ftl/dot_general | solution.py:347
  54.2 7.1 %shard_map.159 = (f32[5,256,128]{2,1,0:T(8,128)}, f32[4,64,128]{2,1,0:T(8,128)}) custom-call(f32[1]{0:T(128)} %bitcast.14.m00_ref, f32[4,256,128]{2,1,0:T(8,128)} %convolution_bitcast_fusion.win_ref, s32[256,128]{1,0:T(8,128)} %copy-done, f32[256,128]{1,0:T(8,128)} %reshape.109.weight_ref, f32[256,128]{1,0:T(8,128)} %reshape.110.share_ref, ...), custom_call_target="tpu_custom_call" | custom-call | tf_op jit(solution)/shard_map/pallas_call | solution.py:273
  61.3 2.0 %fusion.8 = f32[512,5,128]{2,0,1:T(8,128)S(1)} fusion(f32[5,256,128]{2,1,0:T(8,128)} %get-tuple-element.19, s32[256]{0:T(256)S(1)} %and_select_fusion.1), kind=kOutput, calls=%fused_computation.8 | convolution fusion | flops 1006764032 | bytes 1967104 | tf_op jit(solution)/shard_map/qt,ftc->qfc/dot_general | solution.py:367
  64.1 2.4 %all_to_all.24 = f32[128,1,2560]{2,1,0:T(1,128)} reshape(f32[512,5,128]{2,1,0:T(8,128)S(1)} %copy.30) | data formatting | bytes 2621440 | tf_op jit(solution)/shard_map/all_to_all | solution.py:370
  66.4 8.5 %all-to-all-start.2 = ((f32[128,1,2560]{2,1,0:T(1,128)}), f32[128,1,2560]{2,1,0:T(1,128)S(1)}, u32[]{:S(2)}, u32[]{:S(2)}) async-start(f32[128,1,2560]{2,1,0:T(1,128)} %all_to_all.24), calls=%async_computation.2 | async-start | bytes 2621440 | tf_op jit(solution)/shard_map/all_to_all | solution.py:370
  77.2 4.8 %shard_map.160 = bf16[4,72,8192]{2,1,0:T(8,128)(2,1)} custom-call(bf16[72,72]{1,0:T(8,128)(2,1)} %mix_ref.1, f32[72,1]{1,0:T(8,128)} %slice_convert_fusion.1.low_ref, f32[4,8192]{1,0:T(4,128)} %maximum_multiply_fusion.tend_ref, bf16[4,72,8192]{2,1,0:T(8,128)(2,1)} %x_ref), custom_call_target="tpu_custom_call" | custom-call | flops 339738624 | bytes 9437184 | tf_op jit(solution)/shard_map/pallas_call | solution.py:48
  82.0 13.4 %shard_map.161 = f32[60,4,8192]{2,1,0:T(4,128)} custom-call(f32[60,60]{1,0:T(8,128)} %m_ref.1, f32[60,1]{1,0:T(8,128)} %bitcast.101, f32[60,4,8192]{2,1,0:T(4,128)} %bitcast.88, f32[4,8192]{1,0:T(4,128)} %bitcast.91, s32[1,8192]{1,0:T(1,128)} %bitcast.95), custom_call_target="tpu_custom_call" | custom-call | flops 1415577600 | bytes 15728640 | tf_op jit(solution)/shard_map/pallas_call | solution.py:113
  95.3 1.1 %all-to-all-done.2 = f32[128,1,2560]{2,1,0:T(1,128)S(1)} async-done(((f32[128,1,2560]{2,1,0:T(1,128)}), f32[128,1,2560]{2,1,0:T(1,128)S(1)}, u32[]{:S(2)}, u32[]{:S(2)}) %all-to-all-start.2) | async-done | bytes 1310752 | tf_op jit(solution)/shard_map/all_to_all | solution.py:370
  96.4 3.1 %reduce.2 = f32[128,2560]{1,0:T(8,128)S(1)} reduce(f32[128,1,2560]{2,1,0:T(1,128)S(1)} %all-to-all-done.2, f32[]{:T(128)} %constant.57), dimensions={1}, to_apply=%all_to_all.23.reduce_sub_computation | reduce | bytes 2621444 | tf_op jit(solution)/shard_map/all_to_all | solution.py:370
  101.0 1.7 %fusion.15 = f32[4,8192]{1,0:T(4,128)} fusion(f32[1,4,64,128]{3,2,1,0:T(8,128)S(1)} %slice_bitcast_fusion, f32[4,8192]{1,0:T(4,128)} %param.20, f32[8192]{0:T(1024)S(1)} %fusion.31, f32[8192]{0:T(1024)S(1)} %copy-done.1), kind=kLoop, calls=%fused_computation.22 | loop fusion | flops 98304 | bytes 458752 | tf_op jit(solution)/shard_map/div | solution.py:378
  (47 shorter events, 13.6 us)
Async XLA Ops:
  0.6 19.6 %copy-start.7 = (f32[8192]{0:T(1024)S(1)}, f32[8192]{0:T(1024)}, u32[]{:S(2)}) copy-start(f32[8192]{0:T(1024)} %param.16) | copy-start | bytes 98308
  0.6 19.6 %copy-start.3 = (f32[4,8192]{1,0:T(4,128)S(1)}, f32[4,8192]{1,0:T(4,128)}, u32[]{:S(2)}) copy-start(f32[4,8192]{1,0:T(4,128)} %param.27) | copy-start | bytes 393220
  4.0 21.0 %all-to-all-start = ((s32[128,1,4]{2,1,0:T(1,128)}), s32[128,1,4]{2,1,0:T(1,128)S(1)}, u32[]{:S(2)}, u32[]{:S(2)}) async-start(s32[128,1,4]{2,1,0:T(1,128)} %bitcast.18), calls=%async_computation | async-start | bytes 131072 | tf_op jit(solution)/shard_map/all_to_all | solution.py:327
  15.6 22.1 %copy-start = (s32[256,128]{1,0:T(8,128)}, s32[256,128]{1,0:T(8,128)S(1)}, u32[]{:S(2)}) copy-start(s32[256,128]{1,0:T(8,128)S(1)} %add_select_fusion.2.lanes_ref) | copy-start | bytes 393220
  27.1 9.9 %copy-start.4 = (f32[4,8192]{1,0:T(4,128)S(1)}, f32[4,8192]{1,0:T(4,128)}, u32[]{:S(2)}) copy-start(f32[4,8192]{1,0:T(4,128)} %param.26) | copy-start | bytes 393220
  28.8 23.9 %all-to-all-start.1 = ((f32[128,1,2048]{2,1,0:T(1,128)}), f32[128,1,2048]{2,1,0:T(1,128)S(1)}, u32[]{:S(2)}, u32[]{:S(2)}) async-start(f32[128,1,2048]{2,1,0:T(1,128)} %bitcast.27), calls=%async_computation.1 | async-start | bytes 2097152 | tf_op jit(solution)/shard_map/all_to_all | solution.py:344
  43.7 5.2 %copy-start.2 = (s32[256,128]{1,0:T(8,128)S(1)}, s32[256,128]{1,0:T(8,128)}, u32[]{:S(2)}) copy-start(s32[256,128]{1,0:T(8,128)} %get-tuple-element.16) | copy-start | bytes 393220
  66.4 8.5 %copy-start.6 = (bf16[72,72]{1,0:T(8,128)(2,1)S(1)}, bf16[72,72]{1,0:T(8,128)(2,1)}, u32[]{:S(2)}) copy-start(bf16[72,72]{1,0:T(8,128)(2,1)} %mix_ref.1) | copy-start | bytes 31108
  66.4 10.0 %copy-start.5 = (f32[4,64,128]{2,1,0:T(8,128)S(1)}, f32[4,64,128]{2,1,0:T(8,128)}, u32[]{:S(2)}) copy-start(f32[4,64,128]{2,1,0:T(8,128)} %get-tuple-element.21) | copy-start | bytes 393220
  66.4 30.0 %all-to-all-start.2 = ((f32[128,1,2560]{2,1,0:T(1,128)}), f32[128,1,2560]{2,1,0:T(1,128)S(1)}, u32[]{:S(2)}, u32[]{:S(2)}) async-start(f32[128,1,2560]{2,1,0:T(1,128)} %all_to_all.24), calls=%async_computation.2 | async-start | bytes 2621440 | tf_op jit(solution)/shard_map/all_to_all | solution.py:370
  99.5 1.4 %copy-start.1 = (f32[8192]{0:T(1024)S(1)}, f32[8192]{0:T(1024)}, u32[]{:S(2)}) copy-start(f32[8192]{0:T(1024)} %param.19) | copy-start | bytes 98308

commit v16 on v14

--- a/solution.py
+++ b/solution.py
@@ -342,7 +342,7 @@
     )
     keys, order = ranked // width, ranked % width
     arrived = lax.all_to_all(
-        served.reshape(devices, -1), ("comp", "sub"), split_axis=0, concat_axis=0, tiled=True
+        served.reshape(devices, -1, width), ("comp", "sub"), split_axis=0, concat_axis=0, tiled=True
     )
     win_local = jnp.einsum(
         "qt,qfl->ftl", placement, arrived.reshape(slot_tiles, 4, width), precision=highest
@@ -368,7 +368,7 @@
     late_profiles, send_buffer = lax.optimization_barrier((atmos_profiles, send_buffer))
     atmos_updated = diffuse_atmos(late_profiles, atmos_mixing, fluxes)
     returned = lax.all_to_all(
-        send_buffer.reshape(devices, -1), ("comp", "sub"), split_axis=0, concat_axis=0, tiled=True
+        send_buffer.reshape(devices, -1, width), ("comp", "sub"), split_axis=0, concat_axis=0, tiled=True
     )
     summed = jnp.einsum(
         "qw,qfc->fwc", window_hot, returned.reshape(slot_tiles, 5, width), precision=highest

time: 104 us -> 104 us (level)
  other arithmetic: 13.4 us -> 9.36 us
  waiting for transfers between devices: 7.43 us -> 9.9 us
  matrix products: 5.14 us -> 6.73 us
    all_to_all x1 -> x0, other arithmetic: 3.11 us -> none  [per_device(): lax.all_to_all(send_buffer.reshape(devices, -1), ('comp', 'sub'), split_a...]
    all_to_all x2, waiting for transfers between devices: 2.74 us -> 5.2 us  [the longest x1 4.07 us: per_device(): lax.all_to_all(send_buffer.reshape(devices, -1, width), ('comp', 'sub'),...]
    all_to_all x1 -> x0, local copies, waits for them, and re-layouts: 2.38 us -> none  [per_device(): lax.all_to_all(send_buffer.reshape(devices, -1), ('comp', 'sub'), split_a...]
    dot_general x1, matrix products: 0.69 us -> 2.27 us  [per_device(): jnp.einsum('qw,qfc->fwc', window_hot, returned.reshape(slot_tiles, 5, wid...]
    reshape x0 -> x1, local copies, waits for them, and re-layouts: none -> 1.35 us  [per_device(): send_buffer.reshape(devices, -1, width)]
  transfers between devices with their start and end apart: 3 -> 3, of which waited for: 3 -> 3; matrix products, arithmetic and copies ran while one was open for 14% -> 15% of each run, Pallas kernels for 27% -> 27%
where the time goes in v16:
time: 104 us; the launch traced here: 103 us
  Pallas kernels  34.6 us (33%)
  starting transfers between devices  25.2 us (24%)
  local copies, waits for them, and re-layouts  16.3 us (16%)
  waiting for transfers between devices  9.9 us (10%)
  other arithmetic  9.36 us (9%)
  matrix products  6.73 us (6%)
    pallas_call x1, Pallas kernels, ocean_update(): pl.pallas_call(ocean_kernel, grid=(cells // block,), out_shape=jax.ShapeD...  11.8 us
    all_to_all x1, starting transfers between devices, per_device(): lax.all_to_all(request, ('comp', 'sub'), split_axis=0, concat_axis=0, til...  11.5 us
    all_to_all x1, starting transfers between devices, per_device(): lax.all_to_all(send_buffer.reshape(devices, -1, width), ('comp', 'sub'),...  8.64 us
    pallas_call x1, Pallas kernels, return_prep(): pl.pallas_call(return_prep_kernel, out_shape=(jax.ShapeDtypeStruct((field...  7.21 us
    pallas_call x1, Pallas kernels, diffuse_atmos(): pl.pallas_call(atmos_kernel, grid=(columns // block,), out_shape=jax.Shap...  5.93 us
    pallas_call x1, Pallas kernels, lane_sort(): pl.pallas_call(lane_sort_kernel, out_shape=(jax.ShapeDtypeStruct(keys.sha...  5.32 us
    all_to_all x1, starting transfers between devices, per_device(): lax.all_to_all(served.reshape(devices, -1, width), ('comp', 'sub'), split...  5.09 us
    all_to_all x1, waiting for transfers between devices, per_device(): lax.all_to_all(request, ('comp', 'sub'), split_axis=0, concat_axis=0, til...  4.69 us
  transfers between devices with their start and end apart: 3, of which 3 were waited for; matrix products, arithmetic and copies ran while one was open for 15% of the time, Pallas kernels for 27%

profile of v16, /device:TPU:1, one launch (start us, length us, event | category | flops | bytes accessed | tf_op | source)
XLA Modules:
  0.0 102.9 jit_solution(4292830779663198855)
XLA Ops:
  0.7 1.0 %reshape.103 = s32[256,128]{1,0:T(8,128)S(1)} reshape(s32[4,8192]{1,0:T(4,128)} %param.25) | data formatting | bytes 262144 | tf_op jit(solution)/shard_map/reshape | solution.py:319
  4.0 11.5 %all-to-all-start = ((s32[128,1,4]{2,1,0:T(1,128)}), s32[128,1,4]{2,1,0:T(1,128)S(1)}, u32[]{:S(2)}, u32[]{:S(2)}) async-start(s32[128,1,4]{2,1,0:T(1,128)} %bitcast.18), calls=%async_computation | async-start | bytes 131072 | tf_op jit(solution)/shard_map/all_to_all | solution.py:327
  16.4 1.2 %fusion.39 = (f32[1,8192]{1,0:T(1,128)S(1)}, f32[1,8192]{1,0:T(1,128)S(1)}, f32[1,8192]{1,0:T(1,128)S(1)}) fusion(f32[4,8192]{1,0:T(4,128)} %param.18), kind=kLoop, calls=%fused_computation.81 | loop fusion | flops 8192 | bytes 229376 | tf_op jit(solution)/shard_map/slice | solution.py:29
  17.6 1.1 %slice_convert_fusion = f32[4,1,8192]{2,1,0:T(1,128)S(1)} fusion(bf16[4,72,8192]{2,1,0:T(8,128)(2,1)} %x_ref), kind=kLoop, calls=%fused_computation.41 | loop fusion | flops 32768 | bytes 196608 | tf_op jit(solution)/shard_map/convert_element_type | solution.py:14
  18.8 1.4 %fusion.35 = (f32[1,8192]{1,0:T(1,128)S(1)}, f32[1,8192]{1,0:T(1,128)S(1)}, f32[1,8192]{1,0:T(1,128)S(1)}, f32[1,8192]{1,0:T(1,128)S(1)}) fusion(f32[4,1,8192]{2,1,0:T(1,128)S(1)} %slice_convert_fusion, f32[4,8192]{1,0:T(4,128)} %param.17), kind=kLoop, calls=%fused_computation.58 | loop fusion | flops 32768 | bytes 393216 | tf_op jit(solution)/shard_map/sub | solution.py:15
  20.3 4.7 %all-to-all-done = s32[128,1,4]{2,1,0:T(1,128)S(1)} async-done(((s32[128,1,4]{2,1,0:T(1,128)}), s32[128,1,4]{2,1,0:T(1,128)S(1)}, u32[]{:S(2)}, u32[]{:S(2)}) %all-to-all-start) | async-done | bytes 2080 | tf_op jit(solution)/shard_map/all_to_all | solution.py:327
  27.1 1.6 %copy.26 = f32[512,4,128]{2,1,0:T(4,128)} copy(f32[512,4,128]{2,0,1:T(8,128)S(1)} %fusion.16) | data formatting | bytes 2097152 | tf_op jit(solution)/shard_map/optimization_barrier | solution.py:338
  28.8 5.1 %all-to-all-start.1 = ((f32[128,16,128]{2,1,0:T(8,128)}), f32[128,16,128]{2,1,0:T(8,128)S(1)}, u32[]{:S(2)}, u32[]{:S(2)}) async-start(f32[128,16,128]{2,1,0:T(8,128)} %bitcast.27), calls=%async_computation.1 | async-start | bytes 2097152 | tf_op jit(solution)/shard_map/all_to_all | solution.py:344
  33.8 1.3 %slice_bitcast_fusion.7.row_ref = f32[60]{0:T(128)} fusion(f32[60,60]{1,0:T(8,128)} %m_ref.1), kind=kLoop, calls=%fused_computation.78 | loop fusion | bytes 480 | tf_op jit(solution)/shard_map/squeeze | solution.py:339
  35.1 1.3 %slice.97 = f32[1,1]{1,0:T(1,128)} slice(f32[60,60]{1,0:T(8,128)} %m_ref.1), slice={[0:1], [0:1]} | slice | bytes 8 | tf_op jit(solution)/shard_map/slice | solution.py:353
  38.5 5.3 %shard_map.158 = (s32[256,128]{1,0:T(8,128)}, s32[256,128]{1,0:T(8,128)}, s32[256,128]{1,0:T(8,128)}) custom-call(s32[256,128]{1,0:T(8,128)} %iota_add_fusion.key_ref), custom_call_target="tpu_custom_call" | custom-call | tf_op jit(solution)/shard_map/pallas_call | solution.py:222
  43.8 4.3 %shard_map.157 = f32[4,8192]{1,0:T(4,128)} custom-call(f32[60]{0:T(128)} %slice_bitcast_fusion.7.row_ref, f32[60,4,8192]{2,1,0:T(4,128)} %bitcast.86), custom_call_target="tpu_custom_call" | custom-call | flops 3932160 | bytes 7995392 | tf_op jit(solution)/shard_map/pallas_call | solution.py:142
  49.9 1.6 %copy_bitcast_fusion.1 = (f32[4,64,128]{2,1,0:T(8,128)}, f32[4,64,128]{2,1,0:T(8,128)}) fusion(f32[1,4,64,128]{3,1,2,0:T(4,128)S(1)} %slice_bitcast_fusion.1, f32[1,4,64,128]{3,1,2,0:T(4,128)} %bitcast.92), kind=kLoop, calls=%fused_computation.24 | loop fusion | bytes 524288 | tf_op jit(solution)/shard_map/reshape;squeeze | solution.py:359
  51.5 1.1 %all-to-all-done.1 = f32[128,16,128]{2,1,0:T(8,128)S(1)} async-done(((f32[128,16,128]{2,1,0:T(8,128)}), f32[128,16,128]{2,1,0:T(8,128)S(1)}, u32[]{:S(2)}, u32[]{:S(2)}) %all-to-all-start.1) | async-done | bytes 1048608 | tf_op jit(solution)/shard_map/all_to_all | solution.py:344
  52.6 1.5 %convolution_bitcast_fusion.win_ref = f32[4,256,128]{2,1,0:T(8,128)} fusion(f32[512,4,128]{2,1,0:T(4,128)S(1)} %bitcast.90, s32[256]{0:T(256)S(1)} %and_select_fusion.1), kind=kOutput, calls=%fused_computation.2 | convolution fusion | flops 805437440 | bytes 1573888 | tf_op jit(solution)/shard_map/qt,qfl->ftl/dot_general | solution.py:347
  54.2 7.2 %shard_map.159 = (f32[5,256,128]{2,1,0:T(8,128)}, f32[4,64,128]{2,1,0:T(8,128)}) custom-call(f32[1]{0:T(128)} %bitcast.14.m00_ref, f32[4,256,128]{2,1,0:T(8,128)} %convolution_bitcast_fusion.win_ref, s32[256,128]{1,0:T(8,128)} %copy-done, f32[256,128]{1,0:T(8,128)} %reshape.106.weight_ref, f32[256,128]{1,0:T(8,128)} %reshape.107.share_ref, ...), custom_call_target="tpu_custom_call" | custom-call | tf_op jit(solution)/shard_map/pallas_call | solution.py:273
  61.4 2.0 %fusion.8 = f32[512,5,128]{2,0,1:T(8,128)S(1)} fusion(f32[5,256,128]{2,1,0:T(8,128)} %get-tuple-element.19, s32[256]{0:T(256)S(1)} %and_select_fusion.1), kind=kOutput, calls=%fused_computation.8 | convolution fusion | flops 1006764032 | bytes 1967104 | tf_op jit(solution)/shard_map/qt,ftc->qfc/dot_general | solution.py:367
  64.2 1.4 %reshape.112 = f32[128,20,128]{2,1,0:T(8,128)} reshape(f32[512,5,128]{2,1,0:T(8,128)S(1)} %copy.29) | data formatting | bytes 2621440 | tf_op jit(solution)/shard_map/reshape | solution.py:371
  65.5 8.6 %all-to-all-start.2 = ((f32[128,20,128]{2,1,0:T(8,128)}), f32[128,20,128]{2,1,0:T(8,128)S(1)}, u32[]{:S(2)}, u32[]{:S(2)}) async-start(f32[128,20,128]{2,1,0:T(8,128)} %reshape.112), calls=%async_computation.2 | async-start | bytes 3145728 | tf_op jit(solution)/shard_map/all_to_all | solution.py:370
  76.4 5.9 %shard_map.160 = bf16[4,72,8192]{2,1,0:T(8,128)(2,1)} custom-call(bf16[72,72]{1,0:T(8,128)(2,1)} %mix_ref.1, f32[72,1]{1,0:T(8,128)} %slice_convert_fusion.1.low_ref, f32[4,8192]{1,0:T(4,128)} %maximum_multiply_fusion.tend_ref, bf16[4,72,8192]{2,1,0:T(8,128)(2,1)} %x_ref), custom_call_target="tpu_custom_call" | custom-call | flops 339738624 | bytes 9437184 | tf_op jit(solution)/shard_map/pallas_call | solution.py:48
  82.3 11.8 %shard_map.161 = f32[60,4,8192]{2,1,0:T(4,128)} custom-call(f32[60,60]{1,0:T(8,128)} %m_ref.1, f32[60,1]{1,0:T(8,128)} %bitcast.101, f32[60,4,8192]{2,1,0:T(4,128)} %bitcast.88, f32[4,8192]{1,0:T(4,128)} %bitcast.91, s32[1,8192]{1,0:T(1,128)} %bitcast.95), custom_call_target="tpu_custom_call" | custom-call | flops 1415577600 | bytes 15728640 | tf_op jit(solution)/shard_map/pallas_call | solution.py:113
  94.2 4.1 %all-to-all-done.2 = f32[128,20,128]{2,1,0:T(8,128)S(1)} async-done(((f32[128,20,128]{2,1,0:T(8,128)}), f32[128,20,128]{2,1,0:T(8,128)S(1)}, u32[]{:S(2)}, u32[]{:S(2)}) %all-to-all-start.2) | async-done | bytes 1310752 | tf_op jit(solution)/shard_map/all_to_all | solution.py:370
  98.3 1.5 %reshape.113 = f32[512,5,128]{2,1,0:T(8,128)} reshape(f32[128,20,128]{2,1,0:T(8,128)S(1)} %all-to-all-done.2) | data formatting | bytes 2621440 | tf_op jit(solution)/shard_map/reshape | solution.py:374
  99.8 2.3 %fusion.2 = f32[5,64,128]{2,1,0:T(8,128)S(1)} fusion(f32[512,5,128]{2,1,0:T(8,128)} %reshape.113, s32[512]{0:T(512)S(1)} %eq.34), kind=kOutput, calls=%fused_computation.3 | convolution fusion | flops 251691008 | bytes 1476608 | tf_op jit(solution)/shard_map/qw,qfc->fwc/dot_general | solution.py:373
  (48 shorter events, 13.0 us)
Async XLA Ops:
  0.6 19.6 %copy-start.8 = (f32[8192]{0:T(1024)S(1)}, f32[8192]{0:T(1024)}, u32[]{:S(2)}) copy-start(f32[8192]{0:T(1024)} %param.16) | copy-start | bytes 98308
  0.6 19.6 %copy-start.4 = (f32[4,8192]{1,0:T(4,128)S(1)}, f32[4,8192]{1,0:T(4,128)}, u32[]{:S(2)}) copy-start(f32[4,8192]{1,0:T(4,128)} %param.27) | copy-start | bytes 393220
  4.0 21.0 %all-to-all-start = ((s32[128,1,4]{2,1,0:T(1,128)}), s32[128,1,4]{2,1,0:T(1,128)S(1)}, u32[]{:S(2)}, u32[]{:S(2)}) async-start(s32[128,1,4]{2,1,0:T(1,128)} %bitcast.18), calls=%async_computation | async-start | bytes 131072 | tf_op jit(solution)/shard_map/all_to_all | solution.py:327
  15.6 22.3 %copy-start = (s32[256,128]{1,0:T(8,128)}, s32[256,128]{1,0:T(8,128)S(1)}, u32[]{:S(2)}) copy-start(s32[256,128]{1,0:T(8,128)S(1)} %add_select_fusion.2.lanes_ref) | copy-start | bytes 393220
  27.1 10.0 %copy-start.5 = (f32[4,8192]{1,0:T(4,128)S(1)}, f32[4,8192]{1,0:T(4,128)}, u32[]{:S(2)}) copy-start(f32[4,8192]{1,0:T(4,128)} %param.26) | copy-start | bytes 393220
  28.8 23.9 %all-to-all-start.1 = ((f32[128,16,128]{2,1,0:T(8,128)}), f32[128,16,128]{2,1,0:T(8,128)S(1)}, u32[]{:S(2)}, u32[]{:S(2)}) async-start(f32[128,16,128]{2,1,0:T(8,128)} %bitcast.27), calls=%async_computation.1 | async-start | bytes 2097152 | tf_op jit(solution)/shard_map/all_to_all | solution.py:344
  43.8 5.2 %copy-start.3 = (s32[256,128]{1,0:T(8,128)S(1)}, s32[256,128]{1,0:T(8,128)}, u32[]{:S(2)}) copy-start(s32[256,128]{1,0:T(8,128)} %get-tuple-element.16) | copy-start | bytes 393220
  65.5 8.7 %copy-start.7 = (bf16[72,72]{1,0:T(8,128)(2,1)S(1)}, bf16[72,72]{1,0:T(8,128)(2,1)}, u32[]{:S(2)}) copy-start(bf16[72,72]{1,0:T(8,128)(2,1)} %mix_ref.1) | copy-start | bytes 31108
  65.5 10.1 %copy-start.6 = (f32[4,64,128]{2,1,0:T(8,128)S(1)}, f32[4,64,128]{2,1,0:T(8,128)}, u32[]{:S(2)}) copy-start(f32[4,64,128]{2,1,0:T(8,128)} %get-tuple-element.21) | copy-start | bytes 393220
  65.5 32.7 %all-to-all-start.2 = ((f32[128,20,128]{2,1,0:T(8,128)}), f32[128,20,128]{2,1,0:T(8,128)S(1)}, u32[]{:S(2)}, u32[]{:S(2)}) async-start(f32[128,20,128]{2,1,0:T(8,128)} %reshape.112), calls=%async_computation.2 | async-start | bytes 3145728 | tf_op jit(solution)/shard_map/all_to_all | solution.py:370
  94.2 7.9 %copy-start.1 = (f32[8192]{0:T(1024)S(1)}, f32[8192]{0:T(1024)}, u32[]{:S(2)}) copy-start(f32[8192]{0:T(1024)} %param.19) | copy-start | bytes 98308
  94.2 7.9 %copy-start.2 = (f32[4,8192]{1,0:T(4,128)S(1)}, f32[4,8192]{1,0:T(4,128)}, u32[]{:S(2)}) copy-start(f32[4,8192]{1,0:T(4,128)} %param.20) | copy-start | bytes 393220

commit v17 on v14

--- a/solution.py
+++ b/solution.py
@@ -326,6 +326,11 @@
     request = (request + 0.5).astype(jnp.int32).reshape(devices, slot_tiles // devices)
     asked = lax.all_to_all(request, ("comp", "sub"), split_axis=0, concat_axis=0, tiled=True)
     asked = asked.reshape(slot_tiles)
+    ranked, present, last = lane_sort(
+        lanes * width + lax.broadcasted_iota(jnp.int32, lanes.shape, 1)
+    )
+    ranked, present, last, asked = lax.optimization_barrier((ranked, present, last, asked))
+    keys, order = ranked // width, ranked % width
     window_hot = (asked[:, None] == jnp.arange(windows, dtype=jnp.int32)[None, :]).astype(
         jnp.float32
     )
@@ -337,10 +342,6 @@
     )
     late_lanes, late_state, served = lax.optimization_barrier((lanes, state_by_level, served))
     base_top = top_level_mix(ocean_mixing[0], late_state)
-    ranked, present, last = lane_sort(
-        late_lanes * width + lax.broadcasted_iota(jnp.int32, late_lanes.shape, 1)
-    )
-    keys, order = ranked // width, ranked % width
     arrived = lax.all_to_all(
         served.reshape(devices, -1), ("comp", "sub"), split_axis=0, concat_axis=0, tiled=True
     )

time: 104 us -> 104 us (level)
  other arithmetic: 13.4 us -> 11.4 us
  waiting for transfers between devices: 7.43 us -> 9.4 us
    all_to_all x1, waiting for transfers between devices: 1.27 us -> 7.11 us  [per_device(): lax.all_to_all(served.reshape(devices, -1), ('comp', 'sub'), split_axis=0...]
    all_to_all x1, waiting for transfers between devices: 4.69 us -> 0.74 us  [per_device(): lax.all_to_all(request, ('comp', 'sub'), split_axis=0, concat_axis=0, til...]
    all_to_all x1, starting transfers between devices: 5.09 us -> 9.03 us  [per_device(): lax.all_to_all(served.reshape(devices, -1), ('comp', 'sub'), split_axis=0...]
    all_to_all x1, starting transfers between devices: 8.5 us -> 4.89 us  [per_device(): lax.all_to_all(send_buffer.reshape(devices, -1), ('comp', 'sub'), split_a...]
    sub x1, other arithmetic: 1.41 us -> 0.15 us  [surface_fluxes(): east_gap = bottom[2] - surface_before[2]]
  transfers between devices with their start and end apart: 3 -> 3, of which waited for: 3 -> 3; matrix products, arithmetic and copies ran while one was open for 14% -> 13% of each run, Pallas kernels for 27% -> 27%
where the time goes in v17:
time: 104 us; the launch traced here: 103 us
  Pallas kernels  34.6 us (33%)
  starting transfers between devices  25.4 us (24%)
  local copies, waits for them, and re-layouts  16.4 us (16%)
  other arithmetic  11.4 us (11%)
  waiting for transfers between devices  9.4 us (9%)
  matrix products  5.15 us (5%)
    pallas_call x1, Pallas kernels, ocean_update(): pl.pallas_call(ocean_kernel, grid=(cells // block,), out_shape=jax.ShapeD...  11.9 us
    all_to_all x1, starting transfers between devices, per_device(): lax.all_to_all(request, ('comp', 'sub'), split_axis=0, concat_axis=0, til...  11.5 us
    all_to_all x1, starting transfers between devices, per_device(): lax.all_to_all(served.reshape(devices, -1), ('comp', 'sub'), split_axis=0...  9.03 us
    pallas_call x1, Pallas kernels, return_prep(): pl.pallas_call(return_prep_kernel, out_shape=(jax.ShapeDtypeStruct((field...  7.17 us
    all_to_all x1, waiting for transfers between devices, per_device(): lax.all_to_all(served.reshape(devices, -1), ('comp', 'sub'), split_axis=0...  7.11 us
    pallas_call x1, Pallas kernels, diffuse_atmos(): pl.pallas_call(atmos_kernel, grid=(columns // block,), out_shape=jax.Shap...  5.94 us
    pallas_call x1, Pallas kernels, lane_sort(): pl.pallas_call(lane_sort_kernel, out_shape=(jax.ShapeDtypeStruct(keys.sha...  5.33 us
    all_to_all x1, starting transfers between devices, per_device(): lax.all_to_all(send_buffer.reshape(devices, -1), ('comp', 'sub'), split_a...  4.89 us
  transfers between devices with their start and end apart: 3, of which 3 were waited for; matrix products, arithmetic and copies ran while one was open for 13% of the time, Pallas kernels for 27%

profile of v17, /device:TPU:1, one launch (start us, length us, event | category | flops | bytes accessed | tf_op | source)
XLA Modules:
  0.0 103.2 jit_solution(9314752898134526954)
XLA Ops:
  0.7 1.0 %reshape.110 = s32[256,128]{1,0:T(8,128)S(1)} reshape(s32[4,8192]{1,0:T(4,128)} %param.25) | data formatting | bytes 262144 | tf_op jit(solution)/shard_map/reshape | solution.py:319
  1.8 1.0 reshape.109
  4.0 11.5 %all-to-all-start = ((s32[128,1,4]{2,1,0:T(1,128)}), s32[128,1,4]{2,1,0:T(1,128)S(1)}, u32[]{:S(2)}, u32[]{:S(2)}) async-start(s32[128,1,4]{2,1,0:T(1,128)} %bitcast.18), calls=%async_computation | async-start | bytes 131072 | tf_op jit(solution)/shard_map/all_to_all | solution.py:327
  16.3 1.2 %fusion.39 = (f32[1,8192]{1,0:T(1,128)S(1)}, f32[1,8192]{1,0:T(1,128)S(1)}, f32[1,8192]{1,0:T(1,128)S(1)}) fusion(f32[4,8192]{1,0:T(4,128)} %param.18), kind=kLoop, calls=%fused_computation.81 | loop fusion | flops 8192 | bytes 229376 | tf_op jit(solution)/shard_map/slice | solution.py:29
  17.5 1.1 %slice_convert_fusion = f32[4,1,8192]{2,1,0:T(1,128)S(1)} fusion(bf16[4,72,8192]{2,1,0:T(8,128)(2,1)} %x_ref), kind=kLoop, calls=%fused_computation.41 | loop fusion | flops 32768 | bytes 196608 | tf_op jit(solution)/shard_map/convert_element_type | solution.py:14
  19.0 5.3 %shard_map.157 = (s32[256,128]{1,0:T(8,128)}, s32[256,128]{1,0:T(8,128)}, s32[256,128]{1,0:T(8,128)}) custom-call(s32[256,128]{1,0:T(8,128)} %get-tuple-element.41.key_ref), custom_call_target="tpu_custom_call" | custom-call | tf_op jit(solution)/shard_map/pallas_call | solution.py:222
  27.1 1.6 %copy.26 = f32[512,4,128]{2,1,0:T(4,128)} copy(f32[512,4,128]{2,0,1:T(8,128)S(1)} %fusion.16) | data formatting | bytes 2097152 | tf_op jit(solution)/shard_map/optimization_barrier | solution.py:343
  28.8 9.0 %all-to-all-start.1 = ((f32[128,1,2048]{2,1,0:T(1,128)}), f32[128,1,2048]{2,1,0:T(1,128)S(1)}, u32[]{:S(2)}, u32[]{:S(2)}) async-start(f32[128,1,2048]{2,1,0:T(1,128)} %bitcast.27), calls=%async_computation.1 | async-start | bytes 2097152 | tf_op jit(solution)/shard_map/all_to_all | solution.py:345
  37.9 1.2 %slice.97 = f32[1,1]{1,0:T(1,128)} slice(f32[60,60]{1,0:T(8,128)} %m_ref.1), slice={[0:1], [0:1]} | slice | bytes 8 | tf_op jit(solution)/shard_map/slice | solution.py:354
  40.6 1.2 %slice_bitcast_fusion.7.row_ref = f32[60]{0:T(128)} fusion(f32[60,60]{1,0:T(8,128)} %m_ref.1), kind=kLoop, calls=%fused_computation.78 | loop fusion | bytes 480 | tf_op jit(solution)/shard_map/squeeze | solution.py:344
  41.8 4.3 %shard_map.158 = f32[4,8192]{1,0:T(4,128)} custom-call(f32[60]{0:T(128)} %slice_bitcast_fusion.7.row_ref, f32[60,4,8192]{2,1,0:T(4,128)} %bitcast.86), custom_call_target="tpu_custom_call" | custom-call | flops 3932160 | bytes 7995392 | tf_op jit(solution)/shard_map/pallas_call | solution.py:142
  46.1 0.9 slice_bitcast_fusion.1
  47.9 1.6 %copy_bitcast_fusion.1 = (f32[4,64,128]{2,1,0:T(8,128)}, f32[4,64,128]{2,1,0:T(8,128)}) fusion(f32[1,4,64,128]{3,1,2,0:T(4,128)S(1)} %slice_bitcast_fusion.1, f32[1,4,64,128]{3,1,2,0:T(4,128)} %bitcast.92), kind=kLoop, calls=%fused_computation.24 | loop fusion | bytes 524288 | tf_op jit(solution)/shard_map/reshape;squeeze | solution.py:360
  49.5 7.1 %all-to-all-done.1 = f32[128,1,2048]{2,1,0:T(1,128)S(1)} async-done(((f32[128,1,2048]{2,1,0:T(1,128)}), f32[128,1,2048]{2,1,0:T(1,128)S(1)}, u32[]{:S(2)}, u32[]{:S(2)}) %all-to-all-start.1) | async-done | bytes 1048608 | tf_op jit(solution)/shard_map/all_to_all | solution.py:345
  56.6 1.5 %convolution_bitcast_fusion.win_ref = f32[4,256,128]{2,1,0:T(8,128)} fusion(f32[512,4,128]{2,1,0:T(4,128)S(1)} %bitcast.90, s32[256]{0:T(256)S(1)} %and_select_fusion.1), kind=kOutput, calls=%fused_computation.2 | convolution fusion | flops 805437440 | bytes 1573888 | tf_op jit(solution)/shard_map/qt,qfl->ftl/dot_general | solution.py:348
  58.1 7.2 %shard_map.159 = (f32[5,256,128]{2,1,0:T(8,128)}, f32[4,64,128]{2,1,0:T(8,128)}) custom-call(f32[1]{0:T(128)} %bitcast.14.m00_ref, f32[4,256,128]{2,1,0:T(8,128)} %convolution_bitcast_fusion.win_ref, s32[256,128]{1,0:T(8,128)} %get-tuple-element.22.lanes_ref, f32[256,128]{1,0:T(8,128)} %reshape.113.weight_ref, f32[256,128]{1,0:T(8,128)} %reshape.114.share_ref, ...), custom_call_target="tpu_custom_call" | custom-call | tf_op jit(solution)/shard_map/pallas_call | solution.py:273
  65.3 2.0 %fusion.8 = f32[512,5,128]{2,0,1:T(8,128)S(1)} fusion(f32[5,256,128]{2,1,0:T(8,128)} %get-tuple-element.27, s32[256]{0:T(256)S(1)} %and_select_fusion.1), kind=kOutput, calls=%fused_computation.8 | convolution fusion | flops 1006764032 | bytes 1967104 | tf_op jit(solution)/shard_map/qt,ftc->qfc/dot_general | solution.py:368
  68.1 2.4 %all_to_all.24 = f32[128,1,2560]{2,1,0:T(1,128)} reshape(f32[512,5,128]{2,1,0:T(8,128)S(1)} %copy.30) | data formatting | bytes 2621440 | tf_op jit(solution)/shard_map/all_to_all | solution.py:371
  70.5 4.9 %all-to-all-start.2 = ((f32[128,1,2560]{2,1,0:T(1,128)}), f32[128,1,2560]{2,1,0:T(1,128)S(1)}, u32[]{:S(2)}, u32[]{:S(2)}) async-start(f32[128,1,2560]{2,1,0:T(1,128)} %all_to_all.24), calls=%async_computation.2 | async-start | bytes 2621440 | tf_op jit(solution)/shard_map/all_to_all | solution.py:371
  77.6 5.9 %shard_map.160 = bf16[4,72,8192]{2,1,0:T(8,128)(2,1)} custom-call(bf16[72,72]{1,0:T(8,128)(2,1)} %mix_ref.1, f32[72,1]{1,0:T(8,128)} %slice_convert_fusion.1.low_ref, f32[4,8192]{1,0:T(4,128)} %maximum_multiply_fusion.tend_ref, bf16[4,72,8192]{2,1,0:T(8,128)(2,1)} %x_ref), custom_call_target="tpu_custom_call" | custom-call | flops 339738624 | bytes 9437184 | tf_op jit(solution)/shard_map/pallas_call | solution.py:48
  83.5 11.9 %shard_map.161 = f32[60,4,8192]{2,1,0:T(4,128)} custom-call(f32[60,60]{1,0:T(8,128)} %m_ref.1, f32[60,1]{1,0:T(8,128)} %bitcast.101, f32[60,4,8192]{2,1,0:T(4,128)} %bitcast.88, f32[4,8192]{1,0:T(4,128)} %bitcast.91, s32[1,8192]{1,0:T(1,128)} %bitcast.95), custom_call_target="tpu_custom_call" | custom-call | flops 1415577600 | bytes 15728640 | tf_op jit(solution)/shard_map/pallas_call | solution.py:113
  95.4 1.6 %all-to-all-done.2 = f32[128,1,2560]{2,1,0:T(1,128)S(1)} async-done(((f32[128,1,2560]{2,1,0:T(1,128)}), f32[128,1,2560]{2,1,0:T(1,128)S(1)}, u32[]{:S(2)}, u32[]{:S(2)}) %all-to-all-start.2) | async-done | bytes 1310752 | tf_op jit(solution)/shard_map/all_to_all | solution.py:371
  97.0 3.1 %reduce.2 = f32[128,2560]{1,0:T(8,128)S(1)} reduce(f32[128,1,2560]{2,1,0:T(1,128)S(1)} %all-to-all-done.2, f32[]{:T(128)} %constant.57), dimensions={1}, to_apply=%all_to_all.23.reduce_sub_computation | reduce | bytes 2621444 | tf_op jit(solution)/shard_map/all_to_all | solution.py:371
  101.5 1.7 %fusion.15 = f32[4,8192]{1,0:T(4,128)} fusion(f32[1,4,64,128]{3,2,1,0:T(8,128)S(1)} %slice_bitcast_fusion, f32[4,8192]{1,0:T(4,128)} %param.20, f32[8192]{0:T(1024)S(1)} %fusion.31, f32[8192]{0:T(1024)S(1)} %copy-done.1), kind=kLoop, calls=%fused_computation.22 | loop fusion | flops 98304 | bytes 458752 | tf_op jit(solution)/shard_map/div | solution.py:379
  (48 shorter events, 11.9 us)
Async XLA Ops:
  0.6 18.1 %copy-start.2 = (f32[4,8192]{1,0:T(4,128)S(1)}, f32[4,8192]{1,0:T(4,128)}, u32[]{:S(2)}) copy-start(f32[4,8192]{1,0:T(4,128)} %param.17) | copy-start | bytes 393220
  0.6 18.2 %copy-start.8 = (f32[8192]{0:T(1024)S(1)}, f32[8192]{0:T(1024)}, u32[]{:S(2)}) copy-start(f32[8192]{0:T(1024)} %param.16) | copy-start | bytes 98308
  0.7 18.3 %copy-start = (s32[8192]{0:T(1024)S(1)}, s32[8192]{0:T(1024)}, u32[]{:S(2)}) copy-start(s32[8192]{0:T(1024)} %param.23) | copy-start | bytes 98308
  4.0 21.0 %all-to-all-start = ((s32[128,1,4]{2,1,0:T(1,128)}), s32[128,1,4]{2,1,0:T(1,128)S(1)}, u32[]{:S(2)}, u32[]{:S(2)}) async-start(s32[128,1,4]{2,1,0:T(1,128)} %bitcast.18), calls=%async_computation | async-start | bytes 131072 | tf_op jit(solution)/shard_map/all_to_all | solution.py:327
  27.1 10.7 %copy-start.4 = (f32[4,8192]{1,0:T(4,128)S(1)}, f32[4,8192]{1,0:T(4,128)}, u32[]{:S(2)}) copy-start(f32[4,8192]{1,0:T(4,128)} %param.27) | copy-start | bytes 393220
  27.1 12.7 %copy-start.5 = (f32[4,8192]{1,0:T(4,128)S(1)}, f32[4,8192]{1,0:T(4,128)}, u32[]{:S(2)}) copy-start(f32[4,8192]{1,0:T(4,128)} %param.26) | copy-start | bytes 393220
  28.8 27.8 %all-to-all-start.1 = ((f32[128,1,2048]{2,1,0:T(1,128)}), f32[128,1,2048]{2,1,0:T(1,128)S(1)}, u32[]{:S(2)}, u32[]{:S(2)}) async-start(f32[128,1,2048]{2,1,0:T(1,128)} %bitcast.27), calls=%async_computation.1 | async-start | bytes 2097152 | tf_op jit(solution)/shard_map/all_to_all | solution.py:345
  41.8 5.2 %copy-start.3 = (s32[256,128]{1,0:T(8,128)S(1)}, s32[256,128]{1,0:T(8,128)}, u32[]{:S(2)}) copy-start(s32[256,128]{1,0:T(8,128)} %get-tuple-element.24) | copy-start | bytes 393220
  70.5 4.9 %copy-start.7 = (bf16[72,72]{1,0:T(8,128)(2,1)S(1)}, bf16[72,72]{1,0:T(8,128)(2,1)}, u32[]{:S(2)}) copy-start(bf16[72,72]{1,0:T(8,128)(2,1)} %mix_ref.1) | copy-start | bytes 31108
  70.5 6.4 %copy-start.6 = (f32[4,64,128]{2,1,0:T(8,128)S(1)}, f32[4,64,128]{2,1,0:T(8,128)}, u32[]{:S(2)}) copy-start(f32[4,64,128]{2,1,0:T(8,128)} %get-tuple-element.29) | copy-start | bytes 393220
  70.5 26.5 %all-to-all-start.2 = ((f32[128,1,2560]{2,1,0:T(1,128)}), f32[128,1,2560]{2,1,0:T(1,128)S(1)}, u32[]{:S(2)}, u32[]{:S(2)}) async-start(f32[128,1,2560]{2,1,0:T(1,128)} %all_to_all.24), calls=%async_computation.2 | async-start | bytes 2621440 | tf_op jit(solution)/shard_map/all_to_all | solution.py:371
  100.1 1.4 %copy-start.1 = (f32[8192]{0:T(1024)S(1)}, f32[8192]{0:T(1024)}, u32[]{:S(2)}) copy-start(f32[8192]{0:T(1024)} %param.19) | copy-start | bytes 98308

commit v18 on v14

--- a/solution.py
+++ b/solution.py
@@ -41,7 +41,7 @@
         out_ref[member] = mixed.astype(out_ref.dtype)
 
 
-def diffuse_atmos(atmos_profiles, atmos_mixing, fluxes, block=2048):
+def diffuse_atmos(atmos_profiles, atmos_mixing, fluxes, block=1024):
     members, levels, columns = atmos_profiles.shape
     lowest = atmos_mixing[:, -1:].astype(jnp.float32)
     tendency = couple_rate * jnp.stack([fluxes[0], fluxes[1], -fluxes[2], -fluxes[3]])

time: 104 us -> 104 us (level)
  Pallas kernels: 34.5 us -> 36.5 us
  waiting for transfers between devices: 7.43 us -> 5.96 us
    pallas_call x1, Pallas kernels: 5.92 us -> 7.89 us  [diffuse_atmos(): pl.pallas_call(atmos_kernel, grid=(columns // block,), out_shape=jax.Shap...]
    all_to_all x1, waiting for transfers between devices: 1.47 us -> 0.01 us  [per_device(): lax.all_to_all(send_buffer.reshape(devices, -1), ('comp', 'sub'), split_a...]
  transfers between devices with their start and end apart: 3 -> 3, of which waited for: 3 -> 2; matrix products, arithmetic and copies ran while one was open for 14% -> 14% of each run, Pallas kernels for 27% -> 28%
where the time goes in v18:
time: 104 us; the launch traced here: 103 us
  Pallas kernels  36.5 us (35%)
  starting transfers between devices  25.1 us (24%)
  local copies, waits for them, and re-layouts  16.3 us (16%)
  other arithmetic  13.4 us (13%)
  waiting for transfers between devices  5.96 us (6%)
  matrix products  5.14 us (5%)
    pallas_call x1, Pallas kernels, ocean_update(): pl.pallas_call(ocean_kernel, grid=(cells // block,), out_shape=jax.ShapeD...  11.9 us
    all_to_all x1, starting transfers between devices, per_device(): lax.all_to_all(request, ('comp', 'sub'), split_axis=0, concat_axis=0, til...  11.5 us
    all_to_all x1, starting transfers between devices, per_device(): lax.all_to_all(send_buffer.reshape(devices, -1), ('comp', 'sub'), split_a...  8.5 us
    pallas_call x1, Pallas kernels, diffuse_atmos(): pl.pallas_call(atmos_kernel, grid=(columns // block,), out_shape=jax.Shap...  7.89 us
    pallas_call x1, Pallas kernels, return_prep(): pl.pallas_call(return_prep_kernel, out_shape=(jax.ShapeDtypeStruct((field...  7.11 us
    pallas_call x1, Pallas kernels, lane_sort(): pl.pallas_call(lane_sort_kernel, out_shape=(jax.ShapeDtypeStruct(keys.sha...  5.33 us
    all_to_all x1, starting transfers between devices, per_device(): lax.all_to_all(served.reshape(devices, -1), ('comp', 'sub'), split_axis=0...  5.09 us
    all_to_all x1, waiting for transfers between devices, per_device(): lax.all_to_all(request, ('comp', 'sub'), split_axis=0, concat_axis=0, til...  4.69 us
  transfers between devices with their start and end apart: 3, of which 2 were waited for; matrix products, arithmetic and copies ran while one was open for 14% of the time, Pallas kernels for 28%

profile of v18, /device:TPU:1, one launch (start us, length us, event | category | flops | bytes accessed | tf_op | source)
XLA Modules:
  0.0 103.2 jit_solution(12815541133434739380)
XLA Ops:
  0.7 1.0 %reshape.107 = s32[256,128]{1,0:T(8,128)S(1)} reshape(s32[4,8192]{1,0:T(4,128)} %param.25) | data formatting | bytes 262144 | tf_op jit(solution)/shard_map/reshape | solution.py:319
  1.8 1.0 reshape.106
  4.0 11.5 %all-to-all-start = ((s32[128,1,4]{2,1,0:T(1,128)}), s32[128,1,4]{2,1,0:T(1,128)S(1)}, u32[]{:S(2)}, u32[]{:S(2)}) async-start(s32[128,1,4]{2,1,0:T(1,128)} %bitcast.18), calls=%async_computation | async-start | bytes 131072 | tf_op jit(solution)/shard_map/all_to_all | solution.py:327
  16.4 1.2 %fusion.39 = (f32[1,8192]{1,0:T(1,128)S(1)}, f32[1,8192]{1,0:T(1,128)S(1)}, f32[1,8192]{1,0:T(1,128)S(1)}) fusion(f32[4,8192]{1,0:T(4,128)} %param.18), kind=kLoop, calls=%fused_computation.81 | loop fusion | flops 8192 | bytes 229376 | tf_op jit(solution)/shard_map/slice | solution.py:29
  17.6 1.1 %slice_convert_fusion = f32[4,1,8192]{2,1,0:T(1,128)S(1)} fusion(bf16[4,72,8192]{2,1,0:T(8,128)(2,1)} %x_ref), kind=kLoop, calls=%fused_computation.41 | loop fusion | flops 32768 | bytes 196608 | tf_op jit(solution)/shard_map/convert_element_type | solution.py:14
  18.8 1.4 %fusion.35 = (f32[1,8192]{1,0:T(1,128)S(1)}, f32[1,8192]{1,0:T(1,128)S(1)}, f32[1,8192]{1,0:T(1,128)S(1)}, f32[1,8192]{1,0:T(1,128)S(1)}) fusion(f32[4,1,8192]{2,1,0:T(1,128)S(1)} %slice_convert_fusion, f32[4,8192]{1,0:T(4,128)} %param.17), kind=kLoop, calls=%fused_computation.58 | loop fusion | flops 32768 | bytes 393216 | tf_op jit(solution)/shard_map/sub | solution.py:15
  20.3 4.7 %all-to-all-done = s32[128,1,4]{2,1,0:T(1,128)S(1)} async-done(((s32[128,1,4]{2,1,0:T(1,128)}), s32[128,1,4]{2,1,0:T(1,128)S(1)}, u32[]{:S(2)}, u32[]{:S(2)}) %all-to-all-start) | async-done | bytes 2080 | tf_op jit(solution)/shard_map/all_to_all | solution.py:327
  27.1 1.6 %copy.26 = f32[512,4,128]{2,1,0:T(4,128)} copy(f32[512,4,128]{2,0,1:T(8,128)S(1)} %fusion.16) | data formatting | bytes 2097152 | tf_op jit(solution)/shard_map/optimization_barrier | solution.py:338
  28.8 5.1 %all-to-all-start.1 = ((f32[128,1,2048]{2,1,0:T(1,128)}), f32[128,1,2048]{2,1,0:T(1,128)S(1)}, u32[]{:S(2)}, u32[]{:S(2)}) async-start(f32[128,1,2048]{2,1,0:T(1,128)} %bitcast.27), calls=%async_computation.1 | async-start | bytes 2097152 | tf_op jit(solution)/shard_map/all_to_all | solution.py:344
  33.8 1.2 %slice_bitcast_fusion.7.row_ref = f32[60]{0:T(128)} fusion(f32[60,60]{1,0:T(8,128)} %m_ref.1), kind=kLoop, calls=%fused_computation.78 | loop fusion | bytes 480 | tf_op jit(solution)/shard_map/squeeze | solution.py:339
  35.0 1.2 %slice.97 = f32[1,1]{1,0:T(1,128)} slice(f32[60,60]{1,0:T(8,128)} %m_ref.1), slice={[0:1], [0:1]} | slice | bytes 8 | tf_op jit(solution)/shard_map/slice | solution.py:353
  38.4 5.3 %shard_map.158 = (s32[256,128]{1,0:T(8,128)}, s32[256,128]{1,0:T(8,128)}, s32[256,128]{1,0:T(8,128)}) custom-call(s32[256,128]{1,0:T(8,128)} %iota_add_fusion.key_ref), custom_call_target="tpu_custom_call" | custom-call | tf_op jit(solution)/shard_map/pallas_call | solution.py:222
  43.7 4.3 %shard_map.157 = f32[4,8192]{1,0:T(4,128)} custom-call(f32[60]{0:T(128)} %slice_bitcast_fusion.7.row_ref, f32[60,4,8192]{2,1,0:T(4,128)} %bitcast.86), custom_call_target="tpu_custom_call" | custom-call | flops 3932160 | bytes 7995392 | tf_op jit(solution)/shard_map/pallas_call | solution.py:142
  49.7 1.6 %copy_bitcast_fusion.1 = (f32[4,64,128]{2,1,0:T(8,128)}, f32[4,64,128]{2,1,0:T(8,128)}) fusion(f32[1,4,64,128]{3,1,2,0:T(4,128)S(1)} %slice_bitcast_fusion.1, f32[1,4,64,128]{3,1,2,0:T(4,128)} %bitcast.92), kind=kLoop, calls=%fused_computation.24 | loop fusion | bytes 524288 | tf_op jit(solution)/shard_map/reshape;squeeze | solution.py:359
  51.4 1.3 %all-to-all-done.1 = f32[128,1,2048]{2,1,0:T(1,128)S(1)} async-done(((f32[128,1,2048]{2,1,0:T(1,128)}), f32[128,1,2048]{2,1,0:T(1,128)S(1)}, u32[]{:S(2)}, u32[]{:S(2)}) %all-to-all-start.1) | async-done | bytes 1048608 | tf_op jit(solution)/shard_map/all_to_all | solution.py:344
  52.6 1.5 %convolution_bitcast_fusion.win_ref = f32[4,256,128]{2,1,0:T(8,128)} fusion(f32[512,4,128]{2,1,0:T(4,128)S(1)} %bitcast.90, s32[256]{0:T(256)S(1)} %and_select_fusion.1), kind=kOutput, calls=%fused_computation.2 | convolution fusion | flops 805437440 | bytes 1573888 | tf_op jit(solution)/shard_map/qt,qfl->ftl/dot_general | solution.py:347
  54.2 7.1 %shard_map.159 = (f32[5,256,128]{2,1,0:T(8,128)}, f32[4,64,128]{2,1,0:T(8,128)}) custom-call(f32[1]{0:T(128)} %bitcast.14.m00_ref, f32[4,256,128]{2,1,0:T(8,128)} %convolution_bitcast_fusion.win_ref, s32[256,128]{1,0:T(8,128)} %copy-done, f32[256,128]{1,0:T(8,128)} %reshape.109.weight_ref, f32[256,128]{1,0:T(8,128)} %reshape.110.share_ref, ...), custom_call_target="tpu_custom_call" | custom-call | tf_op jit(solution)/shard_map/pallas_call | solution.py:273
  61.3 2.0 %fusion.8 = f32[512,5,128]{2,0,1:T(8,128)S(1)} fusion(f32[5,256,128]{2,1,0:T(8,128)} %get-tuple-element.19, s32[256]{0:T(256)S(1)} %and_select_fusion.1), kind=kOutput, calls=%fused_computation.8 | convolution fusion | flops 1006764032 | bytes 1967104 | tf_op jit(solution)/shard_map/qt,ftc->qfc/dot_general | solution.py:367
  64.1 2.4 %all_to_all.24 = f32[128,1,2560]{2,1,0:T(1,128)} reshape(f32[512,5,128]{2,1,0:T(8,128)S(1)} %copy.30) | data formatting | bytes 2621440 | tf_op jit(solution)/shard_map/all_to_all | solution.py:370
  66.4 8.5 %all-to-all-start.2 = ((f32[128,1,2560]{2,1,0:T(1,128)}), f32[128,1,2560]{2,1,0:T(1,128)S(1)}, u32[]{:S(2)}, u32[]{:S(2)}) async-start(f32[128,1,2560]{2,1,0:T(1,128)} %all_to_all.24), calls=%async_computation.2 | async-start | bytes 2621440 | tf_op jit(solution)/shard_map/all_to_all | solution.py:370
  77.2 7.9 %shard_map.160 = bf16[4,72,8192]{2,1,0:T(8,128)(2,1)} custom-call(bf16[72,72]{1,0:T(8,128)(2,1)} %mix_ref.1, f32[72,1]{1,0:T(8,128)} %slice_convert_fusion.1.low_ref, f32[4,8192]{1,0:T(4,128)} %maximum_multiply_fusion.tend_ref, bf16[4,72,8192]{2,1,0:T(8,128)(2,1)} %x_ref), custom_call_target="tpu_custom_call" | custom-call | flops 339738624 | bytes 9437184 | tf_op jit(solution)/shard_map/pallas_call | solution.py:48
  85.1 11.9 %shard_map.161 = f32[60,4,8192]{2,1,0:T(4,128)} custom-call(f32[60,60]{1,0:T(8,128)} %m_ref.1, f32[60,1]{1,0:T(8,128)} %bitcast.101, f32[60,4,8192]{2,1,0:T(4,128)} %bitcast.88, f32[4,8192]{1,0:T(4,128)} %bitcast.91, s32[1,8192]{1,0:T(1,128)} %bitcast.95), custom_call_target="tpu_custom_call" | custom-call | flops 1415577600 | bytes 15728640 | tf_op jit(solution)/shard_map/pallas_call | solution.py:113
  96.9 3.1 %reduce.2 = f32[128,2560]{1,0:T(8,128)S(1)} reduce(f32[128,1,2560]{2,1,0:T(1,128)S(1)} %all-to-all-done.2, f32[]{:T(128)} %constant.57), dimensions={1}, to_apply=%all_to_all.23.reduce_sub_computation | reduce | bytes 2621444 | tf_op jit(solution)/shard_map/all_to_all | solution.py:370
  101.5 1.7 %fusion.15 = f32[4,8192]{1,0:T(4,128)} fusion(f32[1,4,64,128]{3,2,1,0:T(8,128)S(1)} %slice_bitcast_fusion, f32[4,8192]{1,0:T(4,128)} %param.20, f32[8192]{0:T(1024)S(1)} %fusion.31, f32[8192]{0:T(1024)S(1)} %copy-done.1), kind=kLoop, calls=%fused_computation.22 | loop fusion | flops 98304 | bytes 458752 | tf_op jit(solution)/shard_map/div | solution.py:378
  (47 shorter events, 12.6 us)
Async XLA Ops:
  0.6 19.6 %copy-start.7 = (f32[8192]{0:T(1024)S(1)}, f32[8192]{0:T(1024)}, u32[]{:S(2)}) copy-start(f32[8192]{0:T(1024)} %param.16) | copy-start | bytes 98308
  0.6 19.6 %copy-start.3 = (f32[4,8192]{1,0:T(4,128)S(1)}, f32[4,8192]{1,0:T(4,128)}, u32[]{:S(2)}) copy-start(f32[4,8192]{1,0:T(4,128)} %param.27) | copy-start | bytes 393220
  4.0 21.0 %all-to-all-start = ((s32[128,1,4]{2,1,0:T(1,128)}), s32[128,1,4]{2,1,0:T(1,128)S(1)}, u32[]{:S(2)}, u32[]{:S(2)}) async-start(s32[128,1,4]{2,1,0:T(1,128)} %bitcast.18), calls=%async_computation | async-start | bytes 131072 | tf_op jit(solution)/shard_map/all_to_all | solution.py:327
  15.6 22.1 %copy-start = (s32[256,128]{1,0:T(8,128)}, s32[256,128]{1,0:T(8,128)S(1)}, u32[]{:S(2)}) copy-start(s32[256,128]{1,0:T(8,128)S(1)} %add_select_fusion.2.lanes_ref) | copy-start | bytes 393220
  27.1 9.9 %copy-start.4 = (f32[4,8192]{1,0:T(4,128)S(1)}, f32[4,8192]{1,0:T(4,128)}, u32[]{:S(2)}) copy-start(f32[4,8192]{1,0:T(4,128)} %param.26) | copy-start | bytes 393220
  28.8 23.9 %all-to-all-start.1 = ((f32[128,1,2048]{2,1,0:T(1,128)}), f32[128,1,2048]{2,1,0:T(1,128)S(1)}, u32[]{:S(2)}, u32[]{:S(2)}) async-start(f32[128,1,2048]{2,1,0:T(1,128)} %bitcast.27), calls=%async_computation.1 | async-start | bytes 2097152 | tf_op jit(solution)/shard_map/all_to_all | solution.py:344
  43.7 5.2 %copy-start.2 = (s32[256,128]{1,0:T(8,128)S(1)}, s32[256,128]{1,0:T(8,128)}, u32[]{:S(2)}) copy-start(s32[256,128]{1,0:T(8,128)} %get-tuple-element.16) | copy-start | bytes 393220
  66.4 8.5 %copy-start.6 = (bf16[72,72]{1,0:T(8,128)(2,1)S(1)}, bf16[72,72]{1,0:T(8,128)(2,1)}, u32[]{:S(2)}) copy-start(bf16[72,72]{1,0:T(8,128)(2,1)} %mix_ref.1) | copy-start | bytes 31108
  66.4 10.0 %copy-start.5 = (f32[4,64,128]{2,1,0:T(8,128)S(1)}, f32[4,64,128]{2,1,0:T(8,128)}, u32[]{:S(2)}) copy-start(f32[4,64,128]{2,1,0:T(8,128)} %get-tuple-element.21) | copy-start | bytes 393220
  66.4 30.5 %all-to-all-start.2 = ((f32[128,1,2560]{2,1,0:T(1,128)}), f32[128,1,2560]{2,1,0:T(1,128)S(1)}, u32[]{:S(2)}, u32[]{:S(2)}) async-start(f32[128,1,2560]{2,1,0:T(1,128)} %all_to_all.24), calls=%async_computation.2 | async-start | bytes 2621440 | tf_op jit(solution)/shard_map/all_to_all | solution.py:370
  100.1 1.4 %copy-start.1 = (f32[8192]{0:T(1024)S(1)}, f32[8192]{0:T(1024)}, u32[]{:S(2)}) copy-start(f32[8192]{0:T(1024)} %param.19) | copy-start | bytes 98308
